TPU v7x, 32 devices: a whole 2x2x4 slice. The times are simulated.
32 devices in a mesh: dp: 4 (over y, x), sp: 8 (over z, core).
Axes of the slice: x: 2, y: 2, z: 4, core: 2. Of those that a mesh axis runs over, the one named last changes fastest.
Arguments:
- tokens: bfloat16 [32768, 1024], P(('dp', 'sp')), may hold values from -6 to 6
- doc_ids: int32 [4, 8192], P('dp'), may hold values from 0 to 15, never falling along the last dimension, each value on 1 to 4096 neighbouring positions
- gain_attn: bfloat16 [1024], P('sp'), may hold values from 0.5 to 1.5
- w_query: bfloat16 [1024, 256], P('sp'), may hold values from -0.1875 to 0.1875
- w_key: bfloat16 [1024, 256], P('sp'), may hold values from -0.1875 to 0.1875
- w_value: bfloat16 [1024, 1024], P('sp'), may hold values from -0.1875 to 0.1875
- w_out: bfloat16 [1024, 1024], P(None, 'sp'), may hold values from -2 to 2
- gain_mlp: bfloat16 [1024], P('sp'), may hold values from 0.5 to 1.5
- w_gate: bfloat16 [1024, 2752], P('sp'), may hold values from -0.1875 to 0.1875
- w_up: bfloat16 [1024, 2752], P('sp'), may hold values from -0.1875 to 0.1875
- w_down: bfloat16 [2752, 1024], P(None, 'sp'), may hold values from -0.109375 to 0.109375
- cotangent: bfloat16 [32768, 1024], P(('dp', 'sp')), may hold values from -6 to 6
Outputs:
- output: bfloat16 [32768, 1024], P(('dp', 'sp'))
- grad_input: float32 [32768, 1024], P(('dp', 'sp'))
- grad_gain_attn: float32 [1024], P('sp')
- grad_query: float32 [1024, 256], P('sp')
- grad_key: float32 [1024, 256], P('sp')
- grad_value: float32 [1024, 1024], P('sp')
- grad_out: float32 [1024, 1024], P(None, 'sp')
- grad_gain_mlp: float32 [1024], P('sp')
- grad_gate: float32 [1024, 2752], P('sp')
- grad_up: float32 [1024, 2752], P('sp')
- grad_down: float32 [2752, 1024], P(None, 'sp')
Inputs may be any that keep to these rules, and one draw needn't show every extreme that they name: `doc_ids`: within each group document numbers never fall along the tokens, every number 0 to 15 is used, each document has 1 to 4096 tokens and one has exactly 4096.
All inputs are finite; a program needn't handle non-finite values.
Results may differ from a plain program's by a relative error of at most 0.019.
Values may be sent and summed in bfloat16 or wider, within the bound.
A program may use at most 192 MiB of HBM per device.

v0:
```python
import math

import jax
import jax.numpy as jnp
from jax import lax
from jax.sharding import PartitionSpec as P

FEAT = 16
HEAD_V = 64
BLOCK = 512


EPSILON = 1e-05
CAREFUL = lax.Precision.HIGH


def rms_scale(values, weights):
    return values * lax.rsqrt(jnp.mean(values * values, axis=-1, keepdims=True) + EPSILON) * weights


def taylor(vectors):
    feature_dim = vectors.shape[-1]
    scale_one = 1.0 / math.sqrt(math.sqrt(feature_dim))
    scale_two = 1.0 / (math.sqrt(2.0) * math.sqrt(feature_dim))
    products = (vectors[..., :, None] * vectors[..., None, :]).reshape(
        vectors.shape[:-1] + (feature_dim * feature_dim,)
    )
    return jnp.concatenate(
        [
            jnp.ones(vectors.shape[:-1] + (1,), vectors.dtype),
            vectors * scale_one,
            products * scale_two,
        ],
        axis=-1,
    )


def attend_block(carried, blocks):
    kv_state, key_total, last_doc = carried
    query_blk, key_blk, value_blk, doc_blk = blocks
    feature_dim = query_blk.shape[-1]
    length_blk = doc_blk.shape[0]
    scores = jnp.einsum("hif,hjf->hij", query_blk, key_blk, precision=CAREFUL)
    position = lax.iota(jnp.int32, length_blk)
    allowed = (position[:, None] >= position[None, :]) & (doc_blk[:, None] == doc_blk[None, :])
    weights = jnp.where(
        allowed[None],
        1.0 + scores / math.sqrt(feature_dim) + scores * scores / (2.0 * feature_dim),
        0.0,
    )
    query_map = taylor(query_blk)
    key_map = taylor(key_blk)
    sees_prior = (doc_blk == last_doc).astype(query_blk.dtype)
    numerator = jnp.einsum("hij,hjv->hiv", weights, value_blk, precision=CAREFUL) + sees_prior[
        None, :, None
    ] * jnp.einsum("hif,hfv->hiv", query_map, kv_state, precision=CAREFUL)
    denominator = jnp.sum(weights, axis=-1) + sees_prior[None, :] * jnp.einsum(
        "hif,hf->hi", query_map, key_total, precision=CAREFUL
    )
    attended = numerator / denominator[..., None]
    tail_doc = doc_blk[length_blk - 1]
    keep_old = (tail_doc == last_doc).astype(query_blk.dtype)
    in_tail = (doc_blk == tail_doc).astype(query_blk.dtype)
    key_tail = key_map * in_tail[None, :, None]
    kv_state = keep_old * kv_state + jnp.einsum(
        "hjf,hjv->hfv", key_tail, value_blk, precision=CAREFUL
    )
    key_total = keep_old * key_total + jnp.sum(key_tail, axis=1)
    return ((kv_state, key_total, tail_doc), attended)


def attend(queries, keys_in, values_in, doc_row):
    head_count, feature_dim, length = queries.shape
    value_dim = values_in.shape[1]
    block_count = length // BLOCK
    mapped_dim = 1 + feature_dim + feature_dim * feature_dim

    def blocked(tensor):
        inner_dim = tensor.shape[1]
        return tensor.reshape(head_count, inner_dim, block_count, BLOCK).transpose(2, 0, 3, 1)

    initial = (
        jnp.zeros((head_count, mapped_dim, value_dim), queries.dtype),
        jnp.zeros((head_count, mapped_dim), queries.dtype),
        jnp.array(-1, jnp.int32),
    )
    _, outputs = lax.scan(
        jax.checkpoint(attend_block),
        initial,
        (
            blocked(queries),
            blocked(keys_in),
            blocked(values_in),
            doc_row.reshape(block_count, BLOCK),
        ),
    )
    return outputs.transpose(1, 3, 0, 2).reshape(head_count, value_dim, length)


def joined(query_w, key_w, value_w):
    model_dim = query_w.shape[0]
    head_count = query_w.shape[1] // FEAT
    stacked = jnp.concatenate(
        [
            query_w.reshape(model_dim, head_count, FEAT),
            key_w.reshape(model_dim, head_count, FEAT),
            value_w.reshape(model_dim, head_count, HEAD_V),
        ],
        axis=2,
    )
    return stacked.reshape(model_dim, head_count * (2 * FEAT + HEAD_V))


def body(
    tokens,
    doc_ids,
    gain_attn,
    w_query,
    w_key,
    w_value,
    w_out,
    gain_mlp,
    w_gate,
    w_up,
    w_down,
    cotangent,
):
    head_count = w_query.shape[1] // FEAT
    shard_sp = lax.axis_size("sp")
    heads_here = head_count // shard_sp
    per_head = 2 * FEAT + HEAD_V
    tok_local = tokens.shape[0]
    contract_first = (((0,), (0,)), ((), ()))
    attn_full = (
        lax.all_gather(gain_attn, "sp", axis=0, tiled=True),
        lax.all_gather(w_query, "sp", axis=0, tiled=True),
        lax.all_gather(w_key, "sp", axis=0, tiled=True),
        lax.all_gather(w_value, "sp", axis=0, tiled=True),
        lax.all_gather(w_out, "sp", axis=1, tiled=True),
    )
    mlp_full = (
        lax.all_gather(gain_mlp, "sp", axis=0, tiled=True),
        lax.all_gather(w_gate, "sp", axis=0, tiled=True),
        lax.all_gather(w_up, "sp", axis=0, tiled=True),
        lax.all_gather(w_down, "sp", axis=1, tiled=True),
    )
    resid = tokens.astype(jnp.float32)
    gain_one = attn_full[0].astype(jnp.float32)
    w_joint = joined(attn_full[1], attn_full[2], attn_full[3])
    model_dim = w_joint.shape[0]
    normed_one = rms_scale(resid, gain_one).astype(jnp.bfloat16)
    projected = lax.dot_general(
        w_joint, normed_one, (((0,), (1,)), ((), ())), preferred_element_type=jnp.float32
    ).astype(jnp.bfloat16)
    by_head = lax.all_to_all(
        projected.reshape(head_count, per_head, tok_local),
        "sp",
        split_axis=0,
        concat_axis=2,
        tiled=True,
    )
    head_rows = by_head.astype(jnp.float32)
    doc_row = doc_ids[0]

    def local_attention(queries, keys_in, values_in):
        return attend(queries, keys_in, values_in, doc_row)

    attended, attention_back = jax.vjp(
        local_attention,
        head_rows[:, :FEAT],
        head_rows[:, FEAT : 2 * FEAT],
        head_rows[:, 2 * FEAT :],
    )
    attended_rows = attended.astype(jnp.bfloat16).reshape(heads_here * HEAD_V, attended.shape[2])
    token_heads = lax.all_to_all(attended_rows, "sp", split_axis=1, concat_axis=0, tiled=True)
    branch = lax.dot_general(
        token_heads, attn_full[4], contract_first, preferred_element_type=jnp.float32
    )
    hidden = resid + branch
    gain_two = mlp_full[0].astype(jnp.float32)
    normed_two = rms_scale(hidden, gain_two).astype(jnp.bfloat16)
    gate = jnp.dot(normed_two, mlp_full[1], preferred_element_type=jnp.float32)
    up_proj = jnp.dot(normed_two, mlp_full[2], preferred_element_type=jnp.float32)
    sigmoid_gate = jax.nn.sigmoid(gate)
    mixed = (gate * sigmoid_gate * up_proj).astype(jnp.bfloat16)
    output = (hidden + jnp.dot(mixed, mlp_full[3], preferred_element_type=jnp.float32)).astype(
        jnp.bfloat16
    )
    fetched = (
        lax.all_gather(gain_attn, "sp", axis=0, tiled=True),
        lax.all_gather(w_query, "sp", axis=0, tiled=True),
        lax.all_gather(w_key, "sp", axis=0, tiled=True),
        lax.all_gather(w_value, "sp", axis=0, tiled=True),
        lax.all_gather(w_out, "sp", axis=1, tiled=True),
        lax.all_gather(gain_mlp, "sp", axis=0, tiled=True),
        lax.all_gather(w_gate, "sp", axis=0, tiled=True),
        lax.all_gather(w_up, "sp", axis=0, tiled=True),
        lax.all_gather(w_down, "sp", axis=1, tiled=True),
    )
    out_back = fetched[4]
    gate_back = fetched[6]
    up_back = fetched[7]
    down_back = fetched[8]
    joint_back = joined(fetched[1], fetched[2], fetched[3])
    grad_top = cotangent.astype(jnp.float32)
    grad_down = lax.dot_general(
        mixed, cotangent, contract_first, preferred_element_type=jnp.float32
    )
    grad_mixed = lax.dot_general(
        cotangent, down_back, (((1,), (1,)), ((), ())), preferred_element_type=jnp.float32
    )
    grad_gate_in = (
        grad_mixed * up_proj * sigmoid_gate * (1.0 + gate * (1.0 - sigmoid_gate))
    ).astype(jnp.bfloat16)
    grad_up_in = (grad_mixed * gate * sigmoid_gate).astype(jnp.bfloat16)
    grad_gate = lax.dot_general(
        normed_two, grad_gate_in, contract_first, preferred_element_type=jnp.float32
    )
    grad_up = lax.dot_general(
        normed_two, grad_up_in, contract_first, preferred_element_type=jnp.float32
    )
    grad_normed_two = lax.dot_general(
        grad_gate_in, gate_back, (((1,), (1,)), ((), ())), preferred_element_type=jnp.float32
    ) + lax.dot_general(
        grad_up_in, up_back, (((1,), (1,)), ((), ())), preferred_element_type=jnp.float32
    )
    _, norm_two_back = jax.vjp(rms_scale, hidden, gain_two)
    grad_hidden_part, grad_gain_two = norm_two_back(grad_normed_two)
    grad_hidden = grad_top + grad_hidden_part
    grad_branch = grad_hidden.astype(jnp.bfloat16)
    grad_out = jnp.dot(token_heads, grad_branch, preferred_element_type=jnp.float32)
    grad_attended = lax.dot_general(
        out_back, grad_branch, (((1,), (1,)), ((), ())), preferred_element_type=jnp.float32
    ).astype(jnp.bfloat16)
    grad_heads = lax.all_to_all(grad_attended, "sp", split_axis=0, concat_axis=1, tiled=True)
    grad_q, grad_k, grad_v = attention_back(
        grad_heads.astype(jnp.float32).reshape(heads_here, HEAD_V, grad_heads.shape[1])
    )
    grad_stack = jnp.concatenate([grad_q, grad_k, grad_v], axis=1).astype(jnp.bfloat16)
    grad_proj = lax.all_to_all(grad_stack, "sp", split_axis=2, concat_axis=0, tiled=True).reshape(
        head_count * per_head, tok_local
    )
    grad_joint = lax.dot_general(
        normed_one, grad_proj, (((0,), (1,)), ((), ())), preferred_element_type=jnp.float32
    ).reshape(model_dim, head_count, per_head)
    grad_query = grad_joint[:, :, :FEAT].reshape(model_dim, head_count * FEAT)
    grad_key = grad_joint[:, :, FEAT : 2 * FEAT].reshape(model_dim, head_count * FEAT)
    grad_value = grad_joint[:, :, 2 * FEAT :].reshape(model_dim, head_count * HEAD_V)
    grad_normed_one = lax.dot_general(
        grad_proj, joint_back, (((0,), (1,)), ((), ())), preferred_element_type=jnp.float32
    )
    _, norm_one_back = jax.vjp(rms_scale, resid, gain_one)
    grad_input_part, grad_gain_one = norm_one_back(grad_normed_one)
    grad_input = grad_hidden + grad_input_part
    shards = (
        lax.psum_scatter(
            grad_gain_one.astype(jnp.bfloat16), "sp", scatter_dimension=0, tiled=True
        ).astype(jnp.float32),
        lax.psum_scatter(
            grad_query.astype(jnp.bfloat16), "sp", scatter_dimension=0, tiled=True
        ).astype(jnp.float32),
        lax.psum_scatter(
            grad_key.astype(jnp.bfloat16), "sp", scatter_dimension=0, tiled=True
        ).astype(jnp.float32),
        lax.psum_scatter(
            grad_value.astype(jnp.bfloat16), "sp", scatter_dimension=0, tiled=True
        ).astype(jnp.float32),
        lax.psum_scatter(
            grad_out.astype(jnp.bfloat16), "sp", scatter_dimension=1, tiled=True
        ).astype(jnp.float32),
        lax.psum_scatter(
            grad_gain_two.astype(jnp.bfloat16), "sp", scatter_dimension=0, tiled=True
        ).astype(jnp.float32),
        lax.psum_scatter(
            grad_gate.astype(jnp.bfloat16), "sp", scatter_dimension=0, tiled=True
        ).astype(jnp.float32),
        lax.psum_scatter(
            grad_up.astype(jnp.bfloat16), "sp", scatter_dimension=0, tiled=True
        ).astype(jnp.float32),
        lax.psum_scatter(
            grad_down.astype(jnp.bfloat16), "sp", scatter_dimension=1, tiled=True
        ).astype(jnp.float32),
    )
    summed = (
        lax.psum(shards[0].astype(jnp.bfloat16), "dp").astype(jnp.float32),
        lax.psum(shards[1].astype(jnp.bfloat16), "dp").astype(jnp.float32),
        lax.psum(shards[2].astype(jnp.bfloat16), "dp").astype(jnp.float32),
        lax.psum(shards[3].astype(jnp.bfloat16), "dp").astype(jnp.float32),
        lax.psum(shards[4].astype(jnp.bfloat16), "dp").astype(jnp.float32),
        lax.psum(shards[5].astype(jnp.bfloat16), "dp").astype(jnp.float32),
        lax.psum(shards[6].astype(jnp.bfloat16), "dp").astype(jnp.float32),
        lax.psum(shards[7].astype(jnp.bfloat16), "dp").astype(jnp.float32),
        lax.psum(shards[8].astype(jnp.bfloat16), "dp").astype(jnp.float32),
    )
    return (
        output,
        grad_input,
        summed[0],
        summed[1],
        summed[2],
        summed[3],
        summed[4],
        summed[5],
        summed[6],
        summed[7],
        summed[8],
    )


def solution(mesh):
    placed = (
        P(("dp", "sp"), None),
        P("dp", None),
        P("sp"),
        P("sp", None),
        P("sp", None),
        P("sp", None),
        P(None, "sp"),
        P("sp"),
        P("sp", None),
        P("sp", None),
        P(None, "sp"),
        P(("dp", "sp"), None),
    )
    return jax.shard_map(
        body,
        mesh=mesh,
        in_specs=placed,
        out_specs=(
            P(("dp", "sp"), None),
            P(("dp", "sp"), None),
            P("sp"),
            P("sp", None),
            P("sp", None),
            P("sp", None),
            P(None, "sp"),
            P("sp"),
            P("sp", None),
            P("sp", None),
            P(None, "sp"),
        ),
        check_vma=False,
    )
```

profile of v0, /device:TPU:0, one launch (start us, length us, event | category | flops | bytes accessed | tf_op | source)
XLA Modules:
  0.0 1510.6 jit_solution(1957601974484054943)
XLA Ops:
  14.1 13.4 all-gather
  28.8 16.1 %all_gather.34 = bf16[1024,256]{0,1:T(8,128)(2,1)S(1)} all-gather(bf16[128,256]{0,1:T(8,128)(2,1)S(1)} %copy.123), channel_id=1, replica_groups=mesh['dp'=4,'sp'=8] {'sp'}, dimensions={0}, use_global_device_ids=true | all-gather | bytes 589824 | tf_op jit(solution)/shard_map/all_gather | solution.py:136
  45.0 13.9 all_gather.35
  73.0 115.9 %all-to-all-done = bf16[16,96,1024]{2,1,0:T(8,128)(2,1)} async-done(((bf16[16,96,1024]{2,1,0:T(8,128)(2,1)}), bf16[16,96,1024]{2,1,0:T(8,128)(2,1)}, u32[]{:S(2)}, u32[]{:S(2)}) %all-to-all-start) | async-done | bytes 3145760 | tf_op jit(solution)/shard_map/all_to_all | solution.py:155
  207.8 278.0 %while.47 = (s32[]{:T(128)}, f32[2,273,64]{1,2,0:T(8,128)S(1)}, f32[2,273]{1,0:T(2,128)S(1)}, s32[]{:T(128)}, bf16[16,2,512,64]{2,3,1,0:T(8,128)(2,1)}, /*index=...) while((s32[]{:T(128)}, f32[2,273,64]{1,2,0:T(8,128)S(1)}, ...), condition=%wide.region_4.5_spmd.clone, body=%wide.region_1.4_spmd.clone.sunk | while | flops 477021408 | bytes 14363353 | solution.py:87
  503.8 41.4 %all-gather.1 = bf16[8,1,128]{2,1,0:T(2,128)(2,1)S(1)} all-gather(bf16[1,1,128]{2,1,0:T(2,128)(2,1)S(1)} %bitcast.362), channel_id=1, replica_groups=mesh['dp'=4,'sp'=8] {'sp'}, dimensions={0}, use_global_device_ids=true | all-gather | bytes 2304 | tf_op jit(solution)/shard_map/all_gather | solution.py:142
  561.5 11.3 fusion.89
  572.8 11.3 fusion.88
  584.1 20.1 %multiply_convert_fusion = (bf16[1024,2752]{0,1:T(8,128)(2,1)}, bf16[1024,2752]{0,1:T(8,128)(2,1)}, bf16[1024,2752]{0,1:T(8,128)(2,1)}) fusion(f32[1024,2752]{0,1:T(8,128)} %fusion.88, f32[1024,2752]{0,1:T(8,128)} %fusion.89, bf16[1024,1024]{1,0:T(8,128)(2,1)S(1)} %copy-done.9, bf16[2752,1024]{1,0:T(8,128)(2,1)} %all-gather.16.cloned.1.call-done), kind=kOutput, calls=%fused_computation.130 | convolution fusion | flops 5816451072 | bytes 47185920 | tf_op jit(solution)/shard_map/dot_general | solution.py:209
  604.2 11.5 fusion.87
  615.7 10.2 multiply_reduce_fusion.4
  638.3 10.8 convolution_convert_fusion
  659.1 10.5 convolution_convert_fusion.2
  695.6 10.3 convolution_convert_fusion.1
  714.3 64.4 %all-to-all-done.2 = bf16[8,128,1024]{2,1,0:T(8,128)(2,1)S(1)} async-done(((bf16[8,128,1024]{2,1,0:T(8,128)(2,1)}), bf16[8,128,1024]{2,1,0:T(8,128)(2,1)S(1)}, u32[]{:S(2)}, u32[]{:S(2)}) %all-to-all-start.2) | async-done | bytes 2097184 | tf_op jit(solution)/shard_map/all_to_all | solution.py:235
  790.2 394.0 %while.48 = (s32[]{:T(128)}, f32[2,273,64]{1,2,0:T(8,128)S(1)}, f32[2,273]{1,0:T(2,128)S(1)}, bf16[16,2,512,16]{2,3,1,0:T(8,128)(2,1)S(1)}, bf16[16,2,512,16]{2,...) while((s32[]{:T(128)}, f32[2,273,64]{1,2,0:T(8,128)S(1)}, ...), condition=%wide.region_14.15_spmd.clone, body=%wide.region_7.14_spmd.clone.sunk | while | flops 1318872064 | bytes 42693776 | solution.py:87
  1193.3 98.5 %all_to_all.53 = bf16[2,96,8192]{1,0,2:T(2,128)(2,1)} all-to-all(bf16[2,96,8192]{1,0,2:T(2,128)(2,1)} %copy.144), channel_id=1, replica_groups=mesh['dp'=4,'sp'=8] {'sp'}, dimensions={2} | all-to-all | bytes 6291456 | tf_op jit(solution)/shard_map/all_to_all | solution.py:240
  1291.8 11.0 copy.174
  1330.3 11.2 reduce-scatter.16.cloned.1.call-done
  1341.5 32.1 %reduce-scatter.18.cloned.1.call-done = bf16[128,256]{1,0:T(8,128)(2,1)} async-done(((bf16[1024,256]{1,0:T(8,128)(2,1)}), bf16[128,256]{1,0:T(8,128)(2,1)}) %reduce-scatter.18.cloned.1.call-update) | async-done | bytes 65552 | tf_op jit(solution)/shard_map/reduce_scatter | solution.py:262
  1373.6 36.8 %reduce-scatter.20.cloned.1.call-done = bf16[128,1024]{1,0:T(8,128)(2,1)} async-done(((bf16[1024,1024]{1,0:T(8,128)(2,1)}), bf16[128,1024]{1,0:T(8,128)(2,1)}) %reduce-scatter.20.cloned.1.call-update) | async-done | bytes 262160 | tf_op jit(solution)/shard_map/reduce_scatter | solution.py:265
  1410.5 11.5 add_convert_fusion
  1434.9 14.8 all-reduce.2
  1472.9 23.2 %all-reduce.7.cloned.1.call-done = (bf16[128,256]{1,0:T(8,128)(2,1)}, bf16[128,256]{1,0:T(8,128)(2,1)}, bf16[128,1024]{1,0:T(8,128)(2,1)}, bf16[1024,128]{1,0:T(...) async-done(((bf16[128,256]{1,0:T(8,128)(2,1)}, bf16[128,256]{1,0:T(8,128)(2,1)}, bf16[128,1024]{1,0:T(8,128)(2,1)}, ...) | async-done | bytes 2768912 | tf_op jit(solution)/shard_map/psum | solution.py:286
  (1297 shorter events, 846.9 us)
Async XLA Ops:
  7.2 51.7 %all-gather.8.cloned.1.call-start = ((), (), s32[]{:S(2)}) async-start(), calls=%async_computation.11 | async-start | bytes 2359296 | tf_op jit(solution)/shard_map/all_gather | solution.py:138
  9.0 540.6 %all-gather.10.cloned.1.call-start = ((), (), s32[]{:S(2)}) async-start(), calls=%async_computation.12 | async-start | bytes 2359296 | tf_op jit(solution)/shard_map/all_gather | solution.py:139
  9.8 550.5 %all-gather.14.cloned.1.call-start = ((), (), s32[]{:S(2)}) async-start(), calls=%async_computation.14 | async-start | bytes 6340608 | tf_op jit(solution)/shard_map/all_gather | solution.py:144
  10.5 562.3 %all-gather.12.cloned.1.call-start = ((), (), s32[]{:S(2)}) async-start(), calls=%async_computation.13 | async-start | bytes 6340608 | tf_op jit(solution)/shard_map/all_gather | solution.py:143
  11.1 16.4 %copy-start.22 = (bf16[128,256]{1,0:T(8,128)(2,1)S(1)}, bf16[128,256]{1,0:T(8,128)(2,1)}, u32[]{:S(2)}) copy-start(bf16[128,256]{1,0:T(8,128)(2,1)} %param.19) | copy-start | bytes 196612
  11.1 16.5 %copy-start.23 = (bf16[128,256]{1,0:T(8,128)(2,1)S(1)}, bf16[128,256]{1,0:T(8,128)(2,1)}, u32[]{:S(2)}) copy-start(bf16[128,256]{1,0:T(8,128)(2,1)} %param.20) | copy-start | bytes 196612
  14.0 538.9 %copy-start = (bf16[1024,1024]{0,1:T(8,128)(2,1)}, bf16[1024,1024]{0,1:T(8,128)(2,1)S(1)}, u32[]{:S(2)}) copy-start(bf16[1024,1024]{0,1:T(8,128)(2,1)S(1)} %copy.122) | copy-start | bytes 6291460
  27.5 33.4 %copy-start.27 = (f32[8,1,128]{2,1,0:T(1,128)}, f32[8,1,128]{2,1,0:T(1,128)S(1)}, u32[]{:S(2)}) copy-start(f32[8,1,128]{2,1,0:T(1,128)S(1)} %convert_element_type.246) | copy-start | bytes 12292
  28.8 32.0 %copy-start.29 = (f32[1024]{0:T(1024)}, f32[1024]{0:T(1024)S(1)}, u32[]{:S(2)}) copy-start(f32[1024]{0:T(1024)S(1)} %fusion.80) | copy-start | bytes 12292
  65.9 123.0 %all-to-all-start = ((bf16[16,96,1024]{2,1,0:T(8,128)(2,1)}), bf16[16,96,1024]{2,1,0:T(8,128)(2,1)}, u32[]{:S(2)}, u32[]{:S(2)}) async-start(bf16[16,96,1024]{2,1,0:T(8,128)(2,1)} %bitcast.333), calls=%async_computation | async-start | bytes 6291456 | tf_op jit(solution)/shard_map/all_to_all | solution.py:155
  70.5 513.7 %all-gather.16.cloned.1.call-start = ((), (), s32[]{:S(2)}) async-start(), calls=%async_computation.15 | async-start | bytes 6340608 | tf_op jit(solution)/shard_map/all_gather | solution.py:145
  498.2 54.7 %all-to-all-start.1 = ((bf16[128,8,1024]{2,0,1:T(8,128)(2,1)}), bf16[128,8,1024]{2,0,1:T(8,128)(2,1)}, u32[]{:S(2)}, u32[]{:S(2)}) async-start(bf16[128,8,1024]{2,0,1:T(8,128)(2,1)} %copy.131), calls=%async_computation.1 | async-start | bytes 4194304 | tf_op jit(solution)/shard_map/all_to_all | solution.py:175
  503.8 818.0 %reduce-scatter.22.cloned.1.call-start = ((), (), s32[]{:S(2)}) async-start(), calls=%async_computation.19 | async-start | bytes 2359296
  604.2 11.5 copy-start.3
  604.2 11.5 copy-start.39
  638.3 685.3 %reduce-scatter.28.cloned.1.call-start = ((), (), s32[]{:S(2)}) async-start(), calls=%async_computation.22 | async-start | bytes 6488064
  657.5 668.3 %reduce-scatter.24.cloned.1.call-start = ((), (), s32[]{:S(2)}) async-start(), calls=%async_computation.20 | async-start | bytes 6488064
  685.3 93.3 %all-to-all-start.2 = ((bf16[8,128,1024]{2,1,0:T(8,128)(2,1)}), bf16[8,128,1024]{2,1,0:T(8,128)(2,1)S(1)}, u32[]{:S(2)}, u32[]{:S(2)}) async-start(bf16[8,128,1024]{2,1,0:T(8,128)(2,1)} %bitcast.339), calls=%async_computation.2 | async-start | bytes 4194304 | tf_op jit(solution)/shard_map/all_to_all | solution.py:235
  695.5 632.6 %reduce-scatter.26.cloned.1.call-start = ((), (), s32[]{:S(2)}) async-start(), calls=%async_computation.21 | async-start | bytes 6488064
  714.2 627.3 %reduce-scatter.16.cloned.1.call-start = ((), (), s32[]{:S(2)}) async-start(), calls=%async_computation.16 | async-start | bytes 589824 | tf_op jit(solution)/shard_map/reduce_scatter | solution.py:259
  1311.6 62.0 %reduce-scatter.18.cloned.1.call-start = ((), (), s32[]{:S(2)}) async-start(), calls=%async_computation.17 | async-start | bytes 589824 | tf_op jit(solution)/shard_map/reduce_scatter | solution.py:262
  1312.7 97.7 %reduce-scatter.20.cloned.1.call-start = ((), (), s32[]{:S(2)}) async-start(), calls=%async_computation.18 | async-start | bytes 2359296 | tf_op jit(solution)/shard_map/reduce_scatter | solution.py:265
  1319.9 176.2 %all-reduce.7.cloned.1.call-start = ((), (), s32[]{:S(2)}) async-start(), calls=%async_computation.23 | async-start | bytes 5537792 | tf_op jit(solution)/shard_map/psum | solution.py:286
  1425.9 34.8 %copy-start.25 = (f32[1024]{0:T(1024)S(1)}, f32[1024]{0:T(1024)}, u32[]{:S(2)}) copy-start(f32[1024]{0:T(1024)} %copy-done.24) | copy-start | bytes 12292
  (137 other events, 365.9 us)
Sparse Core Ops, SparseCore 0:
  10.2 37.7 all-gather.7
  49.5 39.1 all-gather.9
  90.3 103.3 all-gather.13
  195.2 58.0 all-gather.11
  254.8 57.9 all-gather.15
  638.4 42.0 reduce-scatter.21
  682.7 100.5 reduce-scatter.27
  785.6 70.4 reduce-scatter.23
  858.4 63.2 reduce-scatter.25
  1311.8 29.6 reduce-scatter.15
  1344.4 29.1 reduce-scatter.17
  1376.3 34.0 reduce-scatter.19
  1415.0 81.0 all-reduce.6
where the time goes:
time: 1530 us; the launch traced here: 1510 us
  matrix products  473 us (31%)
  waiting for transfers between devices  289 us (19%)
  local copies, waits for them, and re-layouts  286 us (19%)
  blocking collectives  208 us (14%)
  other arithmetic  170 us (11%)
  loops' own time  48 us (3%)
  starting transfers between devices  20.9 us (1%)
  between operations  15.3 us (1%)
    dot_general x64, matrix products, attend_block(): jnp.einsum('hij,hjv->hiv', weights, value_blk, precision=CAREFUL)  118 us
    all_to_all x1, waiting for transfers between devices, body(): lax.all_to_all(projected.reshape(head_count, per_head, tok_local), 'sp',...  116 us
    all_to_all x1, blocking collectives, body(): lax.all_to_all(grad_stack, 'sp', split_axis=2, concat_axis=0, tiled=True)  98.5 us
    unnamed x91, local copies, waits for them, and re-layouts  80.6 us
    dot_general x64, matrix products, attend_block(): scores = jnp.einsum('hif,hjf->hij', query_blk, key_blk, precision=CAREFUL)  75.8 us
    all_to_all x1, waiting for transfers between devices, body(): lax.all_to_all(grad_attended, 'sp', split_axis=0, concat_axis=1, tiled=True)  64.4 us
    squeeze x64, local copies, waits for them, and re-layouts, attend(): lax.scan(jax.checkpoint(attend_block), initial, (blocked(queries), blocke...  56.3 us
    dynamic_slice x48, local copies, waits for them, and re-layouts, attend(): lax.scan(jax.checkpoint(attend_block), initial, (blocked(queries), blocke...  50.9 us
  transfers between devices with their start and end apart: 16, of which 7 were waited for; matrix products, arithmetic and copies ran while one was open for 56% of the time, Pallas kernels for 0%

commit v1 on v0

v1 whole, which is shorter than its diff:
```python
import functools
import math

import jax
import jax.numpy as jnp
import numpy as np
from jax import lax
from jax.experimental import pallas as pl
from jax.experimental.pallas import tpu as pltpu
from jax.sharding import PartitionSpec as P

FEAT = 16
HEAD_V = 64
EPSILON = 1e-05
BF16 = jnp.bfloat16
F32 = jnp.float32
BLK = 256
PAD_F = 256
ROWS_S = 80
NN = (((1,), (0,)), ((), ()))
NT = (((1,), (1,)), ((), ()))
TN = (((0,), (0,)), ((), ()))


def mm(a, b, dims=NN):
    return lax.dot_general(a, b, dims, preferred_element_type=F32)


def feature_table():
    rows = []
    for a in range(FEAT):
        for b in range(a, FEAT):
            rows.append((a, b, 0.0, 0.0, 1.0 if a == b else 2.0))
    for a in range(FEAT):
        rows.append((a, -1, 0.0, 1.0, 8.0))
    rows.append((-1, -1, 1.0, 1.0, 32.0))
    while len(rows) < PAD_F:
        rows.append((-1, -1, 0.0, 0.0, 0.0))
    table = np.zeros((8, PAD_F), np.float32)
    table[:5] = np.array(rows, np.float32).T
    return jnp.asarray(table)


def selectors(table, head, lanes):
    row = lax.broadcasted_iota(jnp.int32, (lanes, PAD_F), 0).astype(F32)
    base = (head * FEAT).astype(F32)
    first = jnp.where((row == table[0:1] + base) & (table[0:1] >= 0), 1.0, 0.0).astype(BF16)
    second = jnp.where((row == table[1:2] + base) & (table[1:2] >= 0), 1.0, 0.0).astype(BF16)
    return first, second


def head_lanes(values, head, scale=1):
    lane = lax.broadcasted_iota(jnp.int32, values.shape, 1)
    return jnp.where(lane // FEAT == head, values * scale, jnp.zeros_like(values))


def factors(values, sel, table):
    one = mm(values, sel[0]) + table[2:3]
    two = mm(values, sel[1]) + table[3:4]
    return one, two


def with_ones(v_pair):
    return jnp.concatenate([v_pair, jnp.ones_like(v_pair)], axis=1)


def states_kernel(k_ref, v_ref, tail_ref, table_ref, out_ref):
    lanes = k_ref.shape[1]
    table = table_ref[...]
    tail = tail_ref[...]

    def pair(p, carry):
        columns = pl.ds(pl.multiple_of(p * 128, 128), 128)
        v_t = v_ref[:, columns].astype(F32).T * tail
        ones = jnp.broadcast_to(tail, (16, tail.shape[1]))
        for side in range(2):
            head = p * 2 + side
            sel = selectors(table, head, lanes)
            one, two = factors(k_ref[...], sel, table)
            phi = (one * two).astype(BF16)
            lhs = jnp.concatenate([v_t[side * 64 : side * 64 + 64], ones], axis=0)
            out_ref[head] = mm(lhs.astype(BF16), phi).astype(BF16)
        return carry

    lax.fori_loop(0, v_ref.shape[1] // 128, pair, 0)


def placed(state, side, z_rows):
    zero = jnp.zeros((64, PAD_F), state.dtype)
    values = [state[0:64], zero] if side == 0 else [zero, state[0:64]]
    return jnp.concatenate(values + [z_rows], axis=0)


def forward_kernel(
    q_ref, k_ref, v_ref, state_ref, doc_col_ref, doc_row_ref, prior_ref, table_ref,
    att_ref, inv_ref, mask_ref,
):
    tok, lanes = q_ref.shape
    table = table_ref[...]
    row = lax.broadcasted_iota(jnp.int32, (tok, tok), 0)
    col = lax.broadcasted_iota(jnp.int32, (tok, tok), 1)
    mask_ref[...] = jnp.where(
        (row >= col) & (doc_col_ref[...] == doc_row_ref[...]), 1.0, 0.0
    )
    lane = lax.broadcasted_iota(jnp.int32, (BLK, 128), 1)

    def pair(p, carry):
        columns = pl.ds(pl.multiple_of(p * 128, 128), 128)
        v_hat = with_ones(v_ref[:, columns])
        results = []
        for side in range(2):
            head = p * 2 + side
            sel = selectors(table, head, lanes)
            state = state_ref[head]
            z_rows = jnp.broadcast_to(state[64:65].astype(F32), (128, PAD_F)).astype(BF16)
            rows_n = placed(state, side, z_rows)
            one, two = factors(q_ref[...], sel, table)
            phi = (one * two).astype(BF16)
            inter = mm(phi, rows_n, NT) * prior_ref[...]
            q_head = head_lanes(q_ref[...], head)
            parts = []
            for i in range(tok // BLK):
                rows = slice(i * BLK, (i + 1) * BLK)
                keys = slice(0, (i + 1) * BLK)
                t = mm(q_head[rows], k_ref[keys, :], NT) + 4.0
                w = ((t * t + 16.0) * mask_ref[rows, keys]).astype(BF16)
                total = mm(w, v_hat[keys]) + inter[rows]
                inv = 1.0 / total[:, 128:]
                parts.append((total[:, :128] * inv, inv))
            results.append(parts)
        for i in range(tok // BLK):
            rows = slice(i * BLK, (i + 1) * BLK)
            att_ref[rows, columns] = jnp.where(
                lane < 64, results[0][i][0], results[1][i][0]
            ).astype(BF16)
            inv_ref[rows, columns] = jnp.where(lane < 64, results[0][i][1], results[1][i][1])
        return carry

    lax.fori_loop(0, v_ref.shape[1] // 128, pair, 0)


def ghat_kernel(q_ref, g_ref, att_ref, inv_ref, head_row_ref, table_ref, ghat_ref, out_ref):
    tok, lanes = q_ref.shape
    table = table_ref[...]
    r = lax.broadcasted_iota(jnp.int32, (128, 128), 0)
    c = lax.broadcasted_iota(jnp.int32, (128, 128), 1)
    same = jnp.where(r // 64 == c // 64, 1.0, 0.0).astype(BF16)
    lane = lax.broadcasted_iota(jnp.int32, (tok, 128), 1) % 64
    head_row = head_row_ref[...]

    def pair(p, carry):
        columns = pl.ds(pl.multiple_of(p * 128, 128), 128)
        scaled = g_ref[:, columns].astype(F32) * inv_ref[:, columns]
        product = scaled * att_ref[:, columns].astype(F32)
        high = product.astype(BF16)
        low = (product - high.astype(F32)).astype(BF16)
        dots = -(mm(high, same) + mm(low, same))
        dots_high = dots.astype(BF16)
        dots_low = (dots - dots_high.astype(F32)).astype(BF16)
        extra = jnp.where(lane == 0, dots_high, jnp.where(lane == 1, dots_low, jnp.zeros_like(dots_low)))
        ghat = jnp.concatenate([scaled.astype(BF16), extra], axis=1)
        ghat_ref[p] = ghat
        ghat_t = ghat.astype(F32).T * head_row
        for side in range(2):
            head = p * 2 + side
            sel = selectors(table, head, lanes)
            one, two = factors(q_ref[...], sel, table)
            phi = (one * two).astype(BF16)
            lhs = jnp.concatenate(
                [ghat_t[side * 64 : side * 64 + 64], ghat_t[128 + side * 64 : 128 + side * 64 + 16]], axis=0
            )
            state = mm(lhs.astype(BF16), phi)
            z_row = jnp.sum(state[64:80], axis=0, keepdims=True)
            out_ref[head] = jnp.concatenate(
                [state[0:64], jnp.broadcast_to(z_row, (16, PAD_F))], axis=0
            ).astype(BF16)
        return carry

    lax.fori_loop(0, g_ref.shape[1] // 128, pair, 0)


def backward_kernel(
    q_ref, k_ref, v_ref, ghat_ref, prior_state_ref, later_state_ref, doc_col_ref, doc_row_ref,
    prior_ref, later_ref, table_ref, gq_ref, gk_ref, gv_ref, mask_ref, gq_acc, gk_acc,
):
    tok, lanes = q_ref.shape
    table = table_ref[...]
    row = lax.broadcasted_iota(jnp.int32, (tok, tok), 0)
    col = lax.broadcasted_iota(jnp.int32, (tok, tok), 1)
    mask_ref[...] = jnp.where(
        (row <= col) & (doc_col_ref[...] == doc_row_ref[...]), 1.0, 0.0
    )
    gq_acc[...] = jnp.zeros_like(gq_acc)
    gk_acc[...] = jnp.zeros_like(gk_acc)
    lane = lax.broadcasted_iota(jnp.int32, (tok, 256), 1)
    first_row = lax.broadcasted_iota(jnp.int32, (128, PAD_F), 0)

    def pair(p, carry):
        columns = pl.ds(pl.multiple_of(p * 128, 128), 128)
        v_hat = with_ones(v_ref[:, columns])
        gv = [jnp.zeros((BLK, 128), F32) for _ in range(tok // BLK)]
        gv_inter = None
        for side in range(2):
            head = p * 2 + side
            sel = selectors(table, head, lanes)
            ghat = jnp.where((lane % 128) // 64 == side, ghat_ref[p], jnp.zeros((tok, 256), BF16))
            q_head = head_lanes(q_ref[...], head)
            q_twice = q_head + q_head
            k_twice = head_lanes(k_ref[...], head, 2)

            later = later_state_ref[head]
            z_one = jnp.where(first_row == 0, later[64:65], jnp.zeros((128, PAD_F), BF16))
            rows_n = placed(later, side, z_one)
            k_one, k_two = factors(k_ref[...], sel, table)
            phi_k = (k_one * k_two).astype(BF16)
            gvi = mm(phi_k, rows_n[0:128], NT)
            gv_inter = gvi if gv_inter is None else gv_inter + gvi
            d_phi = mm(v_hat, rows_n) * later_ref[...]
            gk_acc[...] += mm((d_phi * k_two).astype(BF16), sel[0], NT) + mm(
                (d_phi * k_one).astype(BF16), sel[1], NT
            )

            prior = prior_state_ref[head]
            z_two = jnp.where(first_row // 2 == side * 32, prior[64:65], jnp.zeros((128, PAD_F), BF16))
            rows_p = placed(prior, side, z_two)
            q_one, q_two = factors(q_ref[...], sel, table)
            d_phi = mm(ghat, rows_p) * prior_ref[...]
            gq_acc[...] += mm((d_phi * q_two).astype(BF16), sel[0], NT) + mm(
                (d_phi * q_one).astype(BF16), sel[1], NT
            )

            for j in range(tok // BLK):
                rows = slice(j * BLK, (j + 1) * BLK)
                onward = slice(j * BLK, tok)
                t = mm(k_ref[rows, :], q_head[onward], NT) + 4.0
                g_w = mm(v_hat[rows], ghat[onward], NT)
                mask = mask_ref[rows, onward]
                masked_t = t * mask
                w = (masked_t * t + 16.0 * mask).astype(BF16)
                g_s = (g_w * masked_t).astype(BF16)
                gv[j] = gv[j] + mm(w, ghat[onward, 0:128])
                gk_acc[rows, :] += mm(g_s, q_twice[onward])
                gq_acc[onward, :] += mm(g_s, k_twice[rows], TN)
        for j in range(tok // BLK):
            rows = slice(j * BLK, (j + 1) * BLK)
            gv_ref[rows, columns] = (gv[j] + gv_inter[rows] * later_ref[rows, :]).astype(BF16)
        return carry

    lax.fori_loop(0, v_ref.shape[1] // 128, pair, 0)
    gq_ref[...] = gq_acc[...].astype(BF16)
    gk_ref[...] = gk_acc[...].astype(BF16)


def call(kernel, out_shape, *args, scratch=(), name=None):
    vmem = pl.BlockSpec(memory_space=pltpu.VMEM)
    return pl.pallas_call(
        kernel,
        out_shape=out_shape,
        in_specs=[vmem] * len(args),
        out_specs=jax.tree.map(lambda _: vmem, out_shape),
        scratch_shapes=list(scratch),
        compiler_params=pltpu.CompilerParams(vmem_limit_bytes=60 << 20),
        name=name,
    )(*args)


def ffn_kernel(
    width, x_ref, att_ref, out_t_ref, gain_ref, cot_ref, wg_ref, wu_ref, wd_ref,
    output_ref, gh_ref, ggain_ref, dg_ref, du_ref, dd_ref,
    hid, n2, n2_t, cot_t, acc_o, acc_n,
):
    step = pl.program_id(0)

    @pl.when(step == 0)
    def _():
        hidden = x_ref[...].astype(F32) + mm(att_ref[...], out_t_ref[...], NT)
        hid[...] = hidden
        scale = lax.rsqrt(jnp.mean(hidden * hidden, axis=1, keepdims=True) + EPSILON)
        normed = (hidden * scale * gain_ref[...]).astype(BF16)
        n2[...] = normed
        n2_t[...] = normed.T
        cot_t[...] = cot_ref[...].T
        acc_o[...] = jnp.zeros_like(acc_o)
        acc_n[...] = jnp.zeros_like(acc_n)

    chunk = wg_ref.shape[1]
    lane = lax.broadcasted_iota(jnp.int32, wg_ref.shape, 1) + step * chunk
    valid = lane < width
    zero = jnp.zeros(wg_ref.shape, BF16)
    wg = jnp.where(valid, wg_ref[...], zero)
    wu = jnp.where(valid, wu_ref[...], zero)
    wd = jnp.where(valid, wd_ref[...], zero)
    gate = mm(n2[...], wg)
    up = mm(n2[...], wu)
    g_mixed = mm(cot_ref[...], wd)
    sig = 1.0 / (1.0 + jnp.exp(-gate))
    act = gate * sig
    mixed = (act * up).astype(BF16)
    g_gate = (g_mixed * up * sig * (1.0 + gate * (1.0 - sig))).astype(BF16)
    g_up = (g_mixed * act).astype(BF16)
    dd_ref[...] = mm(cot_t[...], mixed).astype(BF16)
    dg_ref[...] = mm(n2_t[...], g_gate).astype(BF16)
    du_ref[...] = mm(n2_t[...], g_up).astype(BF16)
    acc_o[...] += mm(mixed, wd, NT)
    acc_n[...] += mm(g_gate, wg, NT) + mm(g_up, wu, NT)

    @pl.when(step == pl.num_programs(0) - 1)
    def _():
        hidden = hid[...]
        output_ref[...] = (hidden + acc_o[...]).astype(BF16)
        scale = lax.rsqrt(jnp.mean(hidden * hidden, axis=1, keepdims=True) + EPSILON)
        e = acc_n[...]
        ggain_ref[...] = jnp.sum(e * hidden * scale, axis=0, keepdims=True)
        eg = e * gain_ref[...]
        inner = jnp.mean(eg * hidden, axis=1, keepdims=True)
        gh_ref[...] = (
            cot_ref[...].astype(F32) + scale * eg - hidden * (scale * scale * scale * inner)
        )


def ffn(x, att, out_t, gain, cot, wg, wu, wd):
    tok, dim = x.shape
    width = wg.shape[1]
    chunk = 256
    whole = lambda shape: pl.BlockSpec(shape, lambda i: (0, 0))
    lanes = pl.BlockSpec((dim, chunk), lambda i: (0, i))
    grad = jax.ShapeDtypeStruct((dim, width), BF16)
    return pl.pallas_call(
        functools.partial(ffn_kernel, width),
        grid=(pl.cdiv(width, chunk),),
        out_shape=(
            jax.ShapeDtypeStruct((tok, dim), BF16),
            jax.ShapeDtypeStruct((tok, dim), F32),
            jax.ShapeDtypeStruct((1, dim), F32),
            grad, grad, grad,
        ),
        in_specs=[
            whole((tok, dim)), whole((tok, dim)), whole((dim, dim)), whole((1, dim)), whole((tok, dim)),
            lanes, lanes, lanes,
        ],
        out_specs=(whole((tok, dim)), whole((tok, dim)), whole((1, dim)), lanes, lanes, lanes),
        scratch_shapes=[
            pltpu.VMEM((tok, dim), F32),
            pltpu.VMEM((tok, dim), BF16),
            pltpu.VMEM((dim, tok), BF16),
            pltpu.VMEM((dim, tok), BF16),
            pltpu.VMEM((tok, dim), F32),
            pltpu.VMEM((tok, dim), F32),
        ],
        compiler_params=pltpu.CompilerParams(vmem_limit_bytes=60 << 20),
        name="ffn",
    )(x, att, out_t, gain, cot, wg, wu, wd)


def rms_scale(values, weights):
    return values * lax.rsqrt(jnp.mean(values * values, axis=-1, keepdims=True) + EPSILON) * weights


def rms_back(u, gain, e):
    scale = lax.rsqrt(jnp.mean(u * u, axis=-1, keepdims=True) + EPSILON)
    grad_gain = jnp.sum(e * u * scale, axis=0)
    eg = e * gain
    inner = jnp.mean(eg * u, axis=-1, keepdims=True)
    return scale * eg - u * (scale * scale * scale * inner), grad_gain


def body(
    tokens, doc_ids, gain_attn, w_query, w_key, w_value, w_out, gain_mlp, w_gate, w_up, w_down, cotangent
):
    n_sp = lax.axis_size("sp")
    me = lax.axis_index("sp")
    tok = tokens.shape[0]
    heads = w_query.shape[1] // FEAT
    table = feature_table()
    gather = lambda a: lax.all_gather(a, "sp", axis=0, tiled=True)
    gain_one = gather(gain_attn).astype(F32)
    gain_two = gather(gain_mlp).astype(F32)
    w_joint = gather(jnp.concatenate([w_query, w_key, w_value], axis=1))
    out_t = gather(w_out.T)
    wg = gather(w_gate)
    wu = gather(w_up)
    wd = gather(w_down.T)

    doc_all = doc_ids[0]
    doc = lax.dynamic_slice(doc_all, (me * tok,), (tok,))
    ends = doc_all.reshape(n_sp, tok)
    firsts, lasts = ends[:, 0], ends[:, tok - 1]
    my_first, my_last = doc[0], doc[tok - 1]
    prev_last = jnp.where(me > 0, lasts[jnp.maximum(me - 1, 0)], -1)
    next_first = jnp.where(me < n_sp - 1, firsts[jnp.minimum(me + 1, n_sp - 1)], -1)
    order = jnp.arange(n_sp)
    from_prior = ((order < me) & (lasts == prev_last)).astype(F32)
    from_later = ((order > me) & (firsts == next_first)).astype(F32)
    tail_row = (doc == my_last).astype(F32)[None, :]
    head_row = (doc == my_first).astype(F32)[None, :]
    prior_col = (doc == prev_last).astype(F32)[:, None]
    later_col = (doc == next_first).astype(F32)[:, None]
    doc_col, doc_row = doc[:, None], doc[None, :]

    resid = tokens.astype(F32)
    normed_one = rms_scale(resid, gain_one).astype(BF16)
    projected = mm(normed_one, w_joint).astype(BF16)
    lanes = heads * FEAT
    q, k, v = projected[:, :lanes], projected[:, lanes : 2 * lanes], projected[:, 2 * lanes :]
    state_shape = jax.ShapeDtypeStruct((heads, ROWS_S, PAD_F), BF16)
    own_state = call(states_kernel, state_shape, k, v, tail_row, table, name="states")

    def combine(state, weights):
        every = lax.all_gather(state, "sp", axis=0, tiled=False).astype(F32)
        return (jnp.einsum("n,nhrf->hrf", weights, every) * table[4]).astype(BF16)

    prior_state = combine(own_state, from_prior)
    att, inv = call(
        forward_kernel,
        (jax.ShapeDtypeStruct(v.shape, BF16), jax.ShapeDtypeStruct(v.shape, F32)),
        q, k, v, prior_state, doc_col, doc_row, prior_col, table,
        scratch=[pltpu.VMEM((tok, tok), F32)],
        name="attend",
    )
    output, g_hidden, grad_gain_two, dg, du, dd = ffn(
        tokens, att, out_t, gain_two[None, :], cotangent, wg, wu, wd
    )
    g_branch = g_hidden.astype(BF16)
    grad_out = mm(g_branch, att, TN)
    g_att = mm(g_branch, out_t).astype(BF16)
    ghat, own_later = call(
        ghat_kernel,
        (jax.ShapeDtypeStruct((heads // 2, tok, 256), BF16), state_shape),
        q, g_att, att, inv, head_row, table,
        name="ghat",
    )
    later_state = combine(own_later, from_later)
    gq, gk, gv = call(
        backward_kernel,
        (
            jax.ShapeDtypeStruct(q.shape, BF16),
            jax.ShapeDtypeStruct(q.shape, BF16),
            jax.ShapeDtypeStruct(v.shape, BF16),
        ),
        q, k, v, ghat, prior_state, later_state, doc_col, doc_row, prior_col, later_col, table,
        scratch=[pltpu.VMEM((tok, tok), F32), pltpu.VMEM(q.shape, F32), pltpu.VMEM(q.shape, F32)],
        name="attend_back",
    )
    g_proj = jnp.concatenate([gq, gk, gv], axis=1)
    grad_joint = mm(normed_one, g_proj, TN)
    g_norm1 = mm(g_proj, w_joint, NT)
    g_in, grad_gain_one = rms_back(resid, gain_one, g_norm1)
    grad_input = g_hidden + g_in

    def reduced(grad):
        part = lax.psum_scatter(grad.astype(BF16), "sp", scatter_dimension=0, tiled=True)
        return lax.psum(part, "dp").astype(F32)

    s_joint = reduced(grad_joint)
    return (
        output,
        grad_input,
        reduced(grad_gain_one),
        s_joint[:, :lanes],
        s_joint[:, lanes : 2 * lanes],
        s_joint[:, 2 * lanes :],
        reduced(grad_out).T,
        reduced(grad_gain_two[0]),
        reduced(dg),
        reduced(du),
        reduced(dd).T,
    )


def solution(mesh):
    placed_in = (
        P(("dp", "sp"), None), P("dp", None), P("sp"), P("sp", None), P("sp", None), P("sp", None),
        P(None, "sp"), P("sp"), P("sp", None), P("sp", None), P(None, "sp"), P(("dp", "sp"), None),
    )
    return jax.shard_map(
        body,
        mesh=mesh,
        in_specs=placed_in,
        out_specs=(
            P(("dp", "sp"), None), P(("dp", "sp"), None), P("sp"), P("sp", None), P("sp", None),
            P("sp", None), P(None, "sp"), P("sp"), P("sp", None), P("sp", None), P(None, "sp"),
        ),
        check_vma=False,
    )
```

time: 1530 us -> 869 us (0.57)
  matrix products: 473 us -> 43 us
  local copies, waits for them, and re-layouts: 286 us -> 25.2 us
  waiting for transfers between devices: 289 us -> 521 us
  Pallas kernels: 0 us -> 191 us
  blocking collectives: 208 us -> 48.5 us
  other arithmetic: 170 us -> 19 us
  loops' own time: 48 us -> 0 us
  starting transfers between devices: 20.9 us -> 0.53 us
    dot_general x303 -> x7, matrix products: 473 us -> 43 us  [the longest x5 31.1 us: mm(): return lax.dot_general(a, b, dims, preferred_element_type=F32)]
    all_gather x5 -> x7, waiting for transfers between devices: 0.03 us -> 282 us  [the longest x5 201 us: body(): gather = lambda a: lax.all_gather(a, 'sp', axis=0, tiled=True)]
    pallas_call x0 -> x5, Pallas kernels: none -> 191 us  [the longest x4 120 us: call(): pl.pallas_call(kernel, out_shape=out_shape, in_specs=[vmem] * len(args),...]
    all_to_all x3 -> x0, waiting for transfers between devices: 184 us -> none  [the longest x1 116 us: body(): lax.all_to_all(projected.reshape(head_count, per_head, tok_local), 'sp',...]
    reduce_scatter x3 -> x5, waiting for transfers between devices: 80.1 us -> 194 us  [reduced(): lax.psum_scatter(grad.astype(BF16), 'sp', scatter_dimension=0, tiled=True)]
    all_to_all x1 -> x0, blocking collectives: 98.5 us -> none  [body(): lax.all_to_all(grad_stack, 'sp', split_axis=2, concat_axis=0, tiled=True)]
    unnamed x91 -> x56, local copies, waits for them, and re-layouts: 80.6 us -> 16.1 us
    all_gather x4 -> x2, blocking collectives: 84.9 us -> 23.6 us  [body(): gather = lambda a: lax.all_gather(a, 'sp', axis=0, tiled=True)]
  transfers between devices with their start and end apart: 16 -> 13, of which waited for: 7 -> 11; matrix products, arithmetic and copies ran while one was open for 56% -> 7% of each run, Pallas kernels for 0% -> 11%
where the time goes in v1:
time: 869 us; the launch traced here: 865 us
  waiting for transfers between devices  521 us (60%)
  Pallas kernels  191 us (22%)
  blocking collectives  48.5 us (6%)
  matrix products  43 us (5%)
  local copies, waits for them, and re-layouts  25.2 us (3%)
  other arithmetic  19 us (2%)
  between operations  16.3 us (2%)
    all_gather x5, waiting for transfers between devices, body(): gather = lambda a: lax.all_gather(a, 'sp', axis=0, tiled=True)  201 us
    reduce_scatter x5, waiting for transfers between devices, reduced(): lax.psum_scatter(grad.astype(BF16), 'sp', scatter_dimension=0, tiled=True)  194 us
    pallas_call x4, Pallas kernels, call(): pl.pallas_call(kernel, out_shape=out_shape, in_specs=[vmem] * len(args),...  120 us
    all_gather x2, waiting for transfers between devices, combine(): every = lax.all_gather(state, 'sp', axis=0, tiled=False).astype(F32)  81.3 us
    pallas_call x1, Pallas kernels, ffn(): pl.pallas_call(functools.partial(ffn_kernel, width), grid=(pl.cdiv(width,...  71.2 us
    psum x1, waiting for transfers between devices, reduced(): return lax.psum(part, 'dp').astype(F32)  42.9 us
    dot_general x5, matrix products, mm(): return lax.dot_general(a, b, dims, preferred_element_type=F32)  31.1 us
    all_gather x2, blocking collectives, body(): gather = lambda a: lax.all_gather(a, 'sp', axis=0, tiled=True)  23.6 us
  transfers between devices with their start and end apart: 13, of which 11 were waited for; matrix products, arithmetic and copies ran while one was open for 7% of the time, Pallas kernels for 11%

profile of v1, /device:TPU:0, one launch (start us, length us, event | category | flops | bytes accessed | tf_op | source)
XLA Modules:
  0.0 864.6 jit_solution(15566456177185346269)
XLA Ops:
  9.2 13.5 %all-gather.2 = bf16[8,1,128]{2,1,0:T(2,128)(2,1)S(1)} all-gather(bf16[1,1,128]{2,1,0:T(2,128)(2,1)} %bitcast.63), channel_id=1, replica_groups=mesh['dp'=4,'sp'=8] {'sp'}, dimensions={0}, use_global_device_ids=true | all-gather | bytes 2304 | tf_op jit(solution)/shard_map/all_gather | solution.py:375
  29.3 22.0 %all-gather.12.cloned.1.call-done = bf16[1024,1536]{1,0:T(8,128)(2,1)} async-done(((bf16[128,1536]{1,0:T(8,128)(2,1)}), bf16[1024,1536]{1,0:T(8,128)(2,1)}) %all-gather.12.cloned.1.call-update) | async-done | bytes 3145744 | tf_op jit(solution)/shard_map/all_gather | solution.py:375
  59.8 10.8 %states.1 = bf16[16,80,256]{2,1,0:T(8,128)(2,1)} custom-call(bf16[1024,256]{1,0:T(8,128)(2,1)} %get-tuple-element.94.k_ref, bf16[1024,1024]{1,0:T(8,128)(2,1)} %slice.49.v_ref, f32[1,1024]{1,0:T(1,128)} %compare_convert_fusion.3.tail_ref, f32[8,256]{1,0:T(8,128)} %constant.33.clone.table_ref), custom_call_target="tpu_custom_call" | custom-call | tf_op jit(solution)/shard_map/states/pallas_call | solution.py:256
  79.5 10.0 %all-gather.3 = bf16[8,1,128]{2,1,0:T(2,128)(2,1)S(1)} all-gather(bf16[1,1,128]{2,1,0:T(2,128)(2,1)S(1)} %bitcast.64), channel_id=1, replica_groups=mesh['dp'=4,'sp'=8] {'sp'}, dimensions={0}, use_global_device_ids=true | all-gather | bytes 2304 | tf_op jit(solution)/shard_map/all_gather | solution.py:375
  91.2 34.5 %all-gather.22.cloned.1.call-done = bf16[128,80,256]{2,1,0:T(8,128)(2,1)} async-done(((bf16[16,80,256]{2,1,0:T(8,128)(2,1)}), bf16[128,80,256]{2,1,0:T(8,128)(2,1)}) %all-gather.22.cloned.1.call-update) | async-done | bytes 5242896 | tf_op jit(solution)/shard_map/all_gather | solution.py:409
  125.6 5.9 fusion.2
  132.6 28.2 %attend.1 = (bf16[1024,1024]{1,0:T(8,128)(2,1)}, f32[1024,1024]{1,0:T(8,128)}) custom-call(bf16[1024,256]{1,0:T(8,128)(2,1)} %get-tuple-element.95.q_ref, bf16[1024,256]{1,0:T(8,128)(2,1)} %get-tuple-element.94.k_ref, bf16[1024,1024]{1,0:T(8,128)(2,1)} %slice.49.v_ref, bf16[16,80,256]{2,1,0:T(8,128)(2,1)} %fusion.13.state_ref.prior_state_ref, ...), custom_call_target="tpu_custom_call" | custom-call | tf_op jit(solution)/shard_map/attend/pallas_call | solution.py:256
  160.8 56.4 %all-gather.16.cloned.1.call-done.wg_ref = bf16[1024,2752]{1,0:T(8,128)(2,1)} async-done(((bf16[128,2752]{1,0:T(8,128)(2,1)}), bf16[1024,2752]{1,0:T(8,128)(2,1)}) %all-gather.16.cloned.1.call-update) | async-done | bytes 5636112 | tf_op jit(solution)/shard_map/all_gather | solution.py:375
  217.2 61.2 %all-gather.18.cloned.1.call-done.wu_ref = bf16[1024,2752]{1,0:T(8,128)(2,1)} async-done(((bf16[128,2752]{1,0:T(8,128)(2,1)}), bf16[1024,2752]{1,0:T(8,128)(2,1)}) %all-gather.18.cloned.1.call-update) | async-done | bytes 5636112 | tf_op jit(solution)/shard_map/all_gather | solution.py:375
  278.4 61.2 %all-gather.20.cloned.1.call-done.wd_ref = bf16[1024,2752]{1,0:T(8,128)(2,1)} async-done(((bf16[128,2752]{1,0:T(8,128)(2,1)}), bf16[1024,2752]{1,0:T(8,128)(2,1)}) %all-gather.20.cloned.1.call-update) | async-done | bytes 5636112 | tf_op jit(solution)/shard_map/all_gather | solution.py:375
  339.6 71.2 %ffn.1 = (bf16[1024,1024]{1,0:T(8,128)(2,1)}, f32[1024,1024]{1,0:T(8,128)}, f32[1,1024]{1,0:T(1,128)}, bf16[1024,2752]{1,0:T(8,128)(2,1)}, bf16[1024,2752]{1,0:T(8,128)(2,1)}, /*index=5*/bf16[1024,2752]{1,0:T(8,128)(2,1)}) custom-call(bf16[1024,1024]{1,0:T(8,128)(2,1)} %x_ref.1, bf16[1024,1024]{1,0:T(8,128)(2,1)} %get-tuple-element.24.att_ref, ...), custom_call_target="tpu_custom_call" | custom-call | tf_op jit(solution)/shard_map/ffn/pallas_call | solution.py:328
  416.6 16.3 %ghat.1 = (bf16[8,1024,256]{2,1,0:T(8,128)(2,1)}, bf16[16,80,256]{2,1,0:T(8,128)(2,1)}) custom-call(bf16[1024,256]{1,0:T(8,128)(2,1)} %get-tuple-element.95.q_ref, bf16[1024,1024]{1,0:T(8,128)(2,1)} %convolution_convert_fusion.3.g_ref, bf16[1024,1024]{1,0:T(8,128)(2,1)} %get-tuple-element.24.att_ref, f32[1024,1024]{1,0:T(8,128)} %get-tuple-element.27.inv_ref, ...), custom_call_target="tpu_custom_call" | custom-call | tf_op jit(solution)/shard_map/ghat/pallas_call | solution.py:256
  441.0 46.8 %all-gather.24.cloned.1.call-done = bf16[128,80,256]{2,1,0:T(8,128)(2,1)} async-done(((bf16[16,80,256]{2,1,0:T(8,128)(2,1)}), bf16[128,80,256]{2,1,0:T(8,128)(2,1)}) %all-gather.24.cloned.1.call-update) | async-done | bytes 5242896 | tf_op jit(solution)/shard_map/all_gather | solution.py:409
  487.8 5.9 fusion
  494.7 64.9 %attend_back.1 = (bf16[1024,256]{1,0:T(8,128)(2,1)}, bf16[1024,256]{1,0:T(8,128)(2,1)}, bf16[1024,1024]{1,0:T(8,128)(2,1)}) custom-call(bf16[1024,256]{1,0:T(8,128)(2,1)} %get-tuple-element.95.q_ref, bf16[1024,256]{1,0:T(8,128)(2,1)} %get-tuple-element.94.k_ref, bf16[1024,1024]{1,0:T(8,128)(2,1)} %slice.49.v_ref, ...), custom_call_target="tpu_custom_call" | custom-call | tf_op jit(solution)/shard_map/attend_back/pallas_call | solution.py:256
  569.1 21.3 %reduce-scatter.14.cloned.1.call-done = bf16[128,2752]{1,0:T(8,128)(2,1)} async-done(((bf16[1024,2752]{1,0:T(8,128)(2,1)}), bf16[128,2752]{1,0:T(8,128)(2,1)}) %reduce-scatter.14.cloned.1.call-update) | async-done | bytes 704528 | tf_op jit(solution)/shard_map/reduce_scatter | solution.py:451
  590.4 65.4 %reduce-scatter.10.cloned.1.call-done = bf16[128,2752]{1,0:T(8,128)(2,1)} async-done(((bf16[1024,2752]{1,0:T(8,128)(2,1)}), bf16[128,2752]{1,0:T(8,128)(2,1)}) %reduce-scatter.10.cloned.1.call-update) | async-done | bytes 704528 | tf_op jit(solution)/shard_map/reduce_scatter | solution.py:451
  655.8 65.6 %reduce-scatter.12.cloned.1.call-done = bf16[128,2752]{1,0:T(8,128)(2,1)} async-done(((bf16[1024,2752]{1,0:T(8,128)(2,1)}), bf16[128,2752]{1,0:T(8,128)(2,1)}) %reduce-scatter.12.cloned.1.call-update) | async-done | bytes 704528 | tf_op jit(solution)/shard_map/reduce_scatter | solution.py:451
  721.4 41.5 %reduce-scatter.6.cloned.1.call-done = bf16[128,1536]{1,0:T(8,128)(2,1)} async-done(((bf16[1024,1536]{1,0:T(8,128)(2,1)}), bf16[128,1536]{1,0:T(8,128)(2,1)}) %reduce-scatter.6.cloned.1.call-update) | async-done | bytes 393232 | tf_op jit(solution)/shard_map/reduce_scatter | solution.py:451
  764.2 8.6 fusion.11
  772.8 15.0 %all-reduce.2 = (bf16[1024]{0:T(1024)(128)(2,1)S(1)}, bf16[1024]{0:T(1024)(128)(2,1)S(1)}) all-reduce(bf16[1024]{0:T(1024)(128)(2,1)S(1)} %get-tuple-element.81, bf16[1024]{0:T(1024)(128)(2,1)S(1)} %convert_reduce_fusion), channel_id=4, replica_groups=mesh['dp'=4,'sp'=8] {'sp'}, use_global_device_ids=true, to_apply=%region_3.4.clone | all-reduce | flops 2048 | bytes 8192
  787.9 9.9 %all-reduce.3 = (bf16[128]{0:T(256)(128)(2,1)S(1)}, bf16[128]{0:T(256)(128)(2,1)S(1)}) all-reduce(bf16[128]{0:T(256)(128)(2,1)S(1)} %dynamic-slice.4, bf16[128]{0:T(256)(128)(2,1)S(1)} %dynamic-slice.6), channel_id=1, replica_groups=mesh['dp'=4,'sp'=8] {'dp'}, use_global_device_ids=true, to_apply=%region_4.5 | all-reduce | flops 256 | bytes 1024 | tf_op jit(solution)/shard_map/psum | solution.py:452
  798.9 6.4 fusion.9
  805.3 42.9 %all-reduce.7.cloned.1.call-done = (bf16[128,1536]{1,0:T(8,128)(2,1)}, bf16[1024,128]{0,1:T(8,128)(2,1)}, bf16[128,2752]{1,0:T(8,128)(2,1)}, bf16[128,2752]{1,0:T(8,128)(2,1)}, bf16[2752,128]{0,1:T(8,128)(2,1)}) async-done(((bf16[128,1536]{1,0:T(8,128)(2,1)}, bf16[1024,128]{0,1:T(8,128)(2,1)}, bf16[128,2752]{1,0:T(8,128)(2,1)}, bf16[128,2752]{1,0:T(8,128)(2,1)}, bf16[2752,128]{0,1:T(8,128)(2,1)}), ...) | async-done | bytes 2768912 | tf_op jit(solution)/shard_map/psum | solution.py:452
  (114 shorter events, 62.8 us)
Async XLA Ops:
  7.2 44.1 %copy-start = (bf16[1024,1024]{1,0:T(8,128)(2,1)S(1)}, bf16[1024,1024]{1,0:T(8,128)(2,1)}, u32[]{:S(2)}) copy-start(bf16[1024,1024]{1,0:T(8,128)(2,1)} %x_ref.1) | copy-start | bytes 6291460
  7.2 44.1 %all-gather.12.cloned.1.call-start = ((), (), s32[]{:S(2)}) async-start(), calls=%async_computation.5 | async-start | bytes 3538944 | tf_op jit(solution)/shard_map/all_gather | solution.py:375
  9.1 116.5 %all-gather.22.cloned.1.call-start = ((), (), s32[]{:S(2)}) async-start(), calls=%async_computation.15 | async-start | bytes 5898240 | tf_op jit(solution)/shard_map/all_gather | solution.py:409
  25.9 50.8 %copy-start.13 = (s32[1,1024]{1,0:T(1,128)}, s32[1,1024]{1,0:T(1,128)S(1)}, u32[]{:S(2)}) copy-start(s32[1,1024]{1,0:T(1,128)S(1)} %get-tuple-element.93.doc_row_ref) | copy-start | bytes 12292
  58.1 12.6 %copy-start.12 = (bf16[1024,128]{1,0:T(8,128)(2,1)S(1)}, bf16[1024,128]{1,0:T(8,128)(2,1)}, u32[]{:S(2)}) copy-start(bf16[1024,128]{1,0:T(8,128)(2,1)} %param.19) | copy-start | bytes 786436
  59.8 11.8 %copy-start.8 = (bf16[128,2752]{0,1:T(8,128)(2,1)S(1)}, bf16[128,2752]{0,1:T(8,128)(2,1)}, u32[]{:S(2)}) copy-start(bf16[128,2752]{0,1:T(8,128)(2,1)} %param.21) | copy-start | bytes 2113540
  59.8 13.0 %copy-start.9 = (bf16[128,2752]{0,1:T(8,128)(2,1)S(1)}, bf16[128,2752]{0,1:T(8,128)(2,1)}, u32[]{:S(2)}) copy-start(bf16[128,2752]{0,1:T(8,128)(2,1)} %param.22) | copy-start | bytes 2113540
  70.6 90.2 %all-gather.14.cloned.1.call-start = ((), (), s32[]{:S(2)}) async-start(), calls=%async_computation.6 | async-start | bytes 2359296 | tf_op jit(solution)/shard_map/all_gather | solution.py:375
  71.5 145.7 %all-gather.16.cloned.1.call-start = ((), (), s32[]{:S(2)}) async-start(), calls=%async_computation.7 | async-start | bytes 6488064 | tf_op jit(solution)/shard_map/all_gather | solution.py:375
  72.7 205.6 %all-gather.18.cloned.1.call-start = ((), (), s32[]{:S(2)}) async-start(), calls=%async_computation.8 | async-start | bytes 6488064 | tf_op jit(solution)/shard_map/all_gather | solution.py:375
  74.0 265.6 %all-gather.20.cloned.1.call-start = ((), (), s32[]{:S(2)}) async-start(), calls=%async_computation.9 | async-start | bytes 6488064 | tf_op jit(solution)/shard_map/all_gather | solution.py:375
  75.2 412.6 %all-gather.24.cloned.1.call-start = ((), (), s32[]{:S(2)}) async-start(), calls=%async_computation.16 | async-start | bytes 5898240 | tf_op jit(solution)/shard_map/all_gather | solution.py:409
  76.9 54.7 %copy-start.3 = (s32[1024,1]{1,0:T(8,128)}, s32[1024,1]{1,0:T(8,128)S(1)}, u32[]{:S(2)}) copy-start(s32[1024,1]{1,0:T(8,128)S(1)} %copy.65.doc_col_ref) | copy-start | bytes 12292
  339.6 71.2 %copy-start.5 = (bf16[1024,1024]{1,0:T(8,128)(2,1)S(1)}, bf16[1024,1024]{1,0:T(8,128)(2,1)}, u32[]{:S(2)}) copy-start(bf16[1024,1024]{1,0:T(8,128)(2,1)} %all-gather.14.cloned.1.call-done.out_t_ref) | copy-start | bytes 6291460
  416.6 16.4 %copy-start.2 = (bf16[1024,1024]{1,0:T(8,128)(2,1)S(1)}, bf16[1024,1024]{1,0:T(8,128)(2,1)}, u32[]{:S(2)}) copy-start(bf16[1024,1024]{1,0:T(8,128)(2,1)} %get-tuple-element.24.att_ref) | copy-start | bytes 6291460
  432.9 136.2 %reduce-scatter.8.cloned.1.call-start = ((), (), s32[]{:S(2)}) async-start(), calls=%async_computation.11 | async-start | bytes 2359296 | tf_op jit(solution)/shard_map/reduce_scatter | solution.py:451
  438.9 151.5 %reduce-scatter.14.cloned.1.call-start = ((), (), s32[]{:S(2)}) async-start(), calls=%async_computation.14 | async-start | bytes 6488064 | tf_op jit(solution)/shard_map/reduce_scatter | solution.py:451
  439.6 216.2 %reduce-scatter.10.cloned.1.call-start = ((), (), s32[]{:S(2)}) async-start(), calls=%async_computation.12 | async-start | bytes 6488064 | tf_op jit(solution)/shard_map/reduce_scatter | solution.py:451
  440.2 281.2 %reduce-scatter.12.cloned.1.call-start = ((), (), s32[]{:S(2)}) async-start(), calls=%async_computation.13 | async-start | bytes 6488064 | tf_op jit(solution)/shard_map/reduce_scatter | solution.py:451
  441.0 321.9 %reduce-scatter.6.cloned.1.call-start = ((), (), s32[]{:S(2)}) async-start(), calls=%async_computation.10 | async-start | bytes 3538944 | tf_op jit(solution)/shard_map/reduce_scatter | solution.py:451
  569.0 193.9 %copy-start.19 = (u32[32]{0:T(128)S(1)}, u32[32]{0:T(128)}, u32[]{:S(2)}) copy-start(u32[32]{0:T(128)} %constant.39) | copy-start | bytes 388
  569.0 195.2 %copy-start.17 = (f32[1,1024]{1,0:T(1,128)S(1)}, f32[1,1024]{1,0:T(1,128)}, u32[]{:S(2)}) copy-start(f32[1,1024]{1,0:T(1,128)} %get-tuple-element.33) | copy-start | bytes 12292
  569.0 279.2 %all-reduce.7.cloned.1.call-start = ((), (), s32[]{:S(2)}) async-start(), calls=%async_computation.17 | async-start | bytes 5636096 | tf_op jit(solution)/shard_map/psum | solution.py:452
  848.2 7.4 copy-start.6
  (9 other events, 40.2 us)
Sparse Core Ops, SparseCore 0:
  10.2 40.9 all-gather.11
  70.7 54.8 all-gather.21
  127.2 27.8 all-gather.13
  157.2 59.9 all-gather.15
  219.2 59.0 all-gather.17
  280.4 59.0 all-gather.19
  433.1 54.7 all-gather.23
  490.1 34.5 reduce-scatter.7
  527.0 63.3 reduce-scatter.13
  592.6 63.2 reduce-scatter.9
  658.1 63.2 reduce-scatter.11
  724.1 38.7 reduce-scatter.5
  766.5 81.6 all-reduce.6

commit v2 on v1

--- a/solution.py
+++ b/solution.py
@@ -64,12 +64,210 @@
     return jnp.concatenate([v_pair, jnp.ones_like(v_pair)], axis=1)
 
 
-def states_kernel(k_ref, v_ref, tail_ref, table_ref, out_ref):
-    lanes = k_ref.shape[1]
+class Copies:
+    def __init__(self, send_sem, recv_sem):
+        self.send_sem, self.recv_sem, self.made = send_sem, recv_sem, {}
+
+    def add(self, name, src, dst, device):
+        self.made[name] = (src, dst, len(self.made), device)
+
+    def get(self, name):
+        src, dst, index, device = self.made[name]
+        return pltpu.make_async_remote_copy(
+            src_ref=src,
+            dst_ref=dst,
+            send_sem=self.send_sem.at[index],
+            recv_sem=self.recv_sem.at[index],
+            device_id=device,
+            device_id_type=pl.DeviceIdType.MESH,
+        )
+
+    def start(self, *names):
+        for name in names:
+            self.get(name).start()
+
+    def arrived(self, *names):
+        for name in names:
+            self.get(name).wait_recv()
+
+    def sent(self, *names):
+        for name in names:
+            self.get(name).wait_send()
+
+
+GROUP = 4
+
+
+def place(n_sp):
+    dp, sp = lax.axis_index("dp"), lax.axis_index("sp")
+    g = lax.rem(dp, GROUP)
+    gy, gx = g // 2, lax.rem(g, 2)
+    z, c = sp // 2, lax.rem(sp, 2)
+    across_x = (dp - g + gy * 2 + (1 - gx), sp)
+    across_y = (dp - g + (1 - gy) * 2 + gx, sp)
+    diagonal = (dp - g + (1 - gy) * 2 + (1 - gx), sp)
+    partner = (dp, z * 2 + (1 - c))
+    return dp, sp, g, gy, gx, z, c, across_x, across_y, diagonal, partner
+
+
+class Gather:
+    def __init__(self, copies, tag, n_z, own, full, where):
+        dp, sp, g, gy, gx, z, c, across_x, across_y, _, partner = where
+        self.copies, self.tag, self.n_z = copies, tag, n_z
+        shard = own.shape[0]
+        quarter = shard // GROUP
+        half = quarter // 2
+        sub = 16 if half % 16 == 0 else 8
+
+        def rows(zz, gg, count, hh=0):
+            start = (zz * 2 + c) * shard + gg * quarter + hh * half
+            return full.at[pl.ds(pl.multiple_of(start, sub), count)]
+
+        gx_of, gy_of = gy * 2 + (1 - gx), (1 - gy) * 2 + gx
+        diag = (1 - gy) * 2 + (1 - gx)
+        add = lambda name, src, dst, device: copies.add((tag, name), src, dst, device)
+        mine = own.at[pl.ds(pl.multiple_of(g * quarter, sub), quarter)]
+        self.own_place = rows(z, 0, shard)
+        add("c0", own, self.own_place, partner)
+        for i in range(1, n_z):
+            zt = lax.rem(z + i, n_z)
+            zs = lax.rem(z + n_z - i, n_z)
+            add(f"z{i}", mine, rows(z, g, quarter), (dp, zt * 2 + c))
+            here = rows(zs, g, quarter)
+            add(f"x{i}", here, here, across_x)
+            add(f"y{i}", here, here, across_y)
+            add(f"c1{i}", here, here, partner)
+            first = rows(zs, gx_of, half)
+            add(f"d0{i}", first, first, across_y)
+            second = rows(zs, gy_of, half, 1)
+            add(f"d1{i}", second, second, across_x)
+            for name, gg in (("c2", gx_of), ("c3", gy_of), ("c4", diag)):
+                there = rows(zs, gg, quarter)
+                add(f"{name}{i}", there, there, partner)
+
+    def each(self, *names):
+        return [(self.tag, f"{name}{i}") for i in range(1, self.n_z) for name in names]
+
+    def stage(self, n):
+        copies = self.copies
+        if n == 0:
+            copies.start(*self.each("z"), (self.tag, "c0"))
+        elif n == 1:
+            for i in range(1, self.n_z):
+                copies.arrived((self.tag, f"z{i}"))
+                copies.start(*[(self.tag, f"{name}{i}") for name in ("x", "y", "c1")])
+        elif n == 2:
+            for i in range(1, self.n_z):
+                copies.arrived((self.tag, f"x{i}"), (self.tag, f"y{i}"))
+                copies.start(*[(self.tag, f"{name}{i}") for name in ("d0", "d1", "c2", "c3")])
+        elif n == 3:
+            for i in range(1, self.n_z):
+                copies.arrived((self.tag, f"d0{i}"), (self.tag, f"d1{i}"))
+                copies.start((self.tag, f"c4{i}"))
+        else:
+            copies.arrived((self.tag, "c0"), *self.each("c1", "c2", "c3", "c4"))
+            copies.sent((self.tag, "c0"), *self.each("z", "x", "y", "c1", "d0", "d1", "c2", "c3", "c4"))
+
+
+def n_copies(n_z):
+    return 1 + 9 * (n_z - 1)
+
+
+def meet(devices):
+    barrier = pltpu.get_barrier_semaphore()
+    for device in devices:
+        pl.semaphore_signal(barrier, inc=1, device_id=device, device_id_type=pl.DeviceIdType.MESH)
+    pl.semaphore_wait(barrier, len(devices))
+
+
+def placed(state, side, z_rows):
+    zero = jnp.zeros((64, PAD_F), state.dtype)
+    values = [state[0:64], zero] if side == 0 else [zero, state[0:64]]
+    return jnp.concatenate(values + [z_rows], axis=0)
+
+
+def rows_sum(values):
+    total = values[0]
+    for value in values[1:]:
+        total = total + value
+    return total
+
+
+def forward_kernel(
+    n_sp, x_ref, gains_ref, doc_col_ref, doc_row_ref, prior_ref, tail_ref, passes_ref, table_ref,
+    joint_own, out_own, gate_own, up_own, down_own,
+    att_ref, inv_ref, q_ref, k_ref, v_ref, normed_ref, state_ref, gain_ref,
+    joint_full, out_full, gate_full, up_full, down_full,
+    mask_ref, joint_vm, num_ref, den_ref, own_state, in_state, out_state, gains_in,
+    send_sem, recv_sem, local_sem,
+):
+    tok = x_ref.shape[0]
+    n_z = n_sp // 2
+    lanes = q_ref.shape[1]
+    pairs = v_ref.shape[1] // 128
+    where = place(n_sp)
+    dp, sp, g, gy, gx, z, c, across_x, across_y, diagonal, partner = where
+    copies = Copies(send_sem, recv_sem)
+    owns = (joint_own, out_own, gate_own, up_own, down_own)
+    fulls = (joint_full, out_full, gate_full, up_full, down_full)
+    gathers = [Gather(copies, k, n_z, own, full, where) for k, (own, full) in enumerate(zip(owns, fulls))]
+    others = [(dp, lax.rem(sp + i, n_sp)) for i in range(1, n_sp)]
+    for i, device in enumerate(others, 1):
+        copies.add(("gain", i), gains_ref, gains_in.at[i - 1], device)
+    following = (dp, lax.rem(sp + 1, n_sp))
+    copies.add("state", out_state, in_state, following)
+    meet(others + [across_x, across_y])
+    copies.start(*[("gain", i) for i in range(1, n_sp)])
+    for gather in gathers:
+        gather.stage(0)
+    local = [
+        pltpu.make_async_copy(own, gather.own_place, local_sem.at[k])
+        for k, (own, gather) in enumerate(zip(owns, gathers))
+    ]
+    for copy in local:
+        copy.start()
+
     table = table_ref[...]
+    row = lax.broadcasted_iota(jnp.int32, (tok, tok), 0)
+    col = lax.broadcasted_iota(jnp.int32, (tok, tok), 1)
+    mask_ref[...] = jnp.where((row >= col) & (doc_col_ref[...] == doc_row_ref[...]), 1.0, 0.0)
+    copies.arrived(*[("gain", i) for i in range(1, n_sp)])
+    gain_ref[...] = gains_ref[...] + rows_sum([gains_in[i] for i in range(n_sp - 1)])
+    x = x_ref[...].astype(F32)
+    scale = lax.rsqrt(jnp.mean(x * x, axis=1, keepdims=True) + EPSILON)
+    normed_ref[...] = (x * scale * gain_ref[0:1]).astype(BF16)
+    gathers[0].stage(1)
+    gathers[0].stage(2)
+    gathers[0].stage(3)
+    gathers[1].stage(1)
+    gathers[2].stage(1)
+    gathers[0].stage(4)
+    for copy in local:
+        copy.wait()
+    fetch = pltpu.make_async_copy(joint_full, joint_vm, local_sem.at[0])
+    fetch.start()
+    fetch.wait()
+    wide = joint_vm.shape[1]
+    for first in range(0, wide, BLK):
+        part = mm(normed_ref[...], joint_vm[:, first : first + BLK]).astype(BF16)
+        if first < lanes:
+            q_ref[:, first : first + BLK] = part
+        elif first < 2 * lanes:
+            k_ref[:, first - lanes : first - lanes + BLK] = part
+        else:
+            v_ref[:, first - 2 * lanes : first - 2 * lanes + BLK] = part
+
     tail = tail_ref[...]
 
-    def pair(p, carry):
+    def at(p, step, *todo):
+        @pl.when(p == step)
+        def _():
+            for k, n in todo:
+                gathers[k].stage(n)
+
+    def state_pair(p, carry):
+        at(p, 2, (3, 1))
+        at(p, 5, (1, 2), (2, 2))
         columns = pl.ds(pl.multiple_of(p * 128, 128), 128)
         v_t = v_ref[:, columns].astype(F32).T * tail
         ones = jnp.broadcast_to(tail, (16, tail.shape[1]))
@@ -79,64 +277,126 @@
             one, two = factors(k_ref[...], sel, table)
             phi = (one * two).astype(BF16)
             lhs = jnp.concatenate([v_t[side * 64 : side * 64 + 64], ones], axis=0)
-            out_ref[head] = mm(lhs.astype(BF16), phi).astype(BF16)
+            own_state[head] = mm(lhs.astype(BF16), phi).astype(BF16)
         return carry
 
-    lax.fori_loop(0, v_ref.shape[1] // 128, pair, 0)
-
-
-def placed(state, side, z_rows):
-    zero = jnp.zeros((64, PAD_F), state.dtype)
-    values = [state[0:64], zero] if side == 0 else [zero, state[0:64]]
-    return jnp.concatenate(values + [z_rows], axis=0)
-
-
-def forward_kernel(
-    q_ref, k_ref, v_ref, state_ref, doc_col_ref, doc_row_ref, prior_ref, table_ref,
-    att_ref, inv_ref, mask_ref,
-):
-    tok, lanes = q_ref.shape
-    table = table_ref[...]
-    row = lax.broadcasted_iota(jnp.int32, (tok, tok), 0)
-    col = lax.broadcasted_iota(jnp.int32, (tok, tok), 1)
-    mask_ref[...] = jnp.where(
-        (row >= col) & (doc_col_ref[...] == doc_row_ref[...]), 1.0, 0.0
-    )
+    lax.fori_loop(0, pairs, state_pair, 0)
+
+    turn = jnp.minimum((z * 11 + c * 2 + 2) // 3, pairs - 1)
+
+    def pass_state(p):
+        @pl.when((p == turn) & (sp > 0))
+        def _():
+            copies.arrived("state")
+
+        @pl.when((p == turn) & (sp == 0))
+        def _():
+            in_state[...] = jnp.zeros_like(in_state)
+
+        @pl.when((p == turn) & (sp < n_sp - 1))
+        def _():
+            go_on = passes_ref[0:1, :]
+            for head in range(in_state.shape[0]):
+                out_state[head] = (
+                    own_state[head].astype(F32) + go_on * in_state[head].astype(F32)
+                ).astype(BF16)
+            copies.start("state")
+
     lane = lax.broadcasted_iota(jnp.int32, (BLK, 128), 1)
 
-    def pair(p, carry):
+    def intra_pair(p, carry):
+        at(p, 0, (4, 1))
+        at(p, 2, (1, 3), (2, 3))
+        at(p, 4, (3, 2))
+        at(p, 6, (4, 2))
+        pass_state(p)
         columns = pl.ds(pl.multiple_of(p * 128, 128), 128)
         v_hat = with_ones(v_ref[:, columns])
-        results = []
+        heads = [head_lanes(q_ref[...], p * 2 + side) for side in range(2)]
+        for i in range(tok // BLK):
+            rows = slice(i * BLK, (i + 1) * BLK)
+            keys = slice(0, (i + 1) * BLK)
+            totals = []
+            for side in range(2):
+                t = mm(heads[side][rows], k_ref[keys, :], NT) + 4.0
+                w = ((t * t + 16.0) * mask_ref[rows, keys]).astype(BF16)
+                totals.append(mm(w, v_hat[keys]))
+            num_ref[rows, columns] = jnp.where(lane < 64, totals[0][:, :128], totals[1][:, :128])
+            den_ref[rows, columns] = jnp.where(lane < 64, totals[0][:, 128:], totals[1][:, 128:])
+        return carry
+
+    lax.fori_loop(0, pairs, intra_pair, 0)
+    for head in range(in_state.shape[0]):
+        state_ref[head] = (in_state[head].astype(F32) * table[4:5]).astype(BF16)
+    prior = prior_ref[...]
+    wide_lane = lax.broadcasted_iota(jnp.int32, (tok, 128), 1)
+
+    def inter_pair(p, carry):
+        at(p, 2, (3, 3))
+        at(p, 6, (4, 3))
+        columns = pl.ds(pl.multiple_of(p * 128, 128), 128)
+        totals = []
         for side in range(2):
             head = p * 2 + side
             sel = selectors(table, head, lanes)
             state = state_ref[head]
             z_rows = jnp.broadcast_to(state[64:65].astype(F32), (128, PAD_F)).astype(BF16)
-            rows_n = placed(state, side, z_rows)
             one, two = factors(q_ref[...], sel, table)
-            phi = (one * two).astype(BF16)
-            inter = mm(phi, rows_n, NT) * prior_ref[...]
-            q_head = head_lanes(q_ref[...], head)
-            parts = []
-            for i in range(tok // BLK):
-                rows = slice(i * BLK, (i + 1) * BLK)
-                keys = slice(0, (i + 1) * BLK)
-                t = mm(q_head[rows], k_ref[keys, :], NT) + 4.0
-                w = ((t * t + 16.0) * mask_ref[rows, keys]).astype(BF16)
-                total = mm(w, v_hat[keys]) + inter[rows]
-                inv = 1.0 / total[:, 128:]
-                parts.append((total[:, :128] * inv, inv))
-            results.append(parts)
-        for i in range(tok // BLK):
-            rows = slice(i * BLK, (i + 1) * BLK)
-            att_ref[rows, columns] = jnp.where(
-                lane < 64, results[0][i][0], results[1][i][0]
-            ).astype(BF16)
-            inv_ref[rows, columns] = jnp.where(lane < 64, results[0][i][1], results[1][i][1])
+            totals.append(mm((one * two).astype(BF16), placed(state, side, z_rows), NT) * prior)
+        num = num_ref[:, columns] + jnp.where(wide_lane < 64, totals[0][:, :128], totals[1][:, :128])
+        den = den_ref[:, columns] + jnp.where(wide_lane < 64, totals[0][:, 128:], totals[1][:, 128:])
+        inv = 1.0 / den
+        inv_ref[:, columns] = inv
+        att_ref[:, columns] = (num * inv).astype(BF16)
         return carry
 
-    lax.fori_loop(0, v_ref.shape[1] // 128, pair, 0)
+    lax.fori_loop(0, pairs, inter_pair, 0)
+    for gather in gathers[1:]:
+        gather.stage(4)
+    copies.sent(*[("gain", i) for i in range(1, n_sp)])
+
+    @pl.when(sp < n_sp - 1)
+    def _():
+        copies.sent("state")
+
+
+def forward(n_sp, x, gains, doc_col, doc_row, prior_col, tail_row, passes, table, shards):
+    tok, dim = x.shape
+    joint = shards[0]
+    lanes = (joint.shape[1] // (2 * FEAT + HEAD_V)) * FEAT
+    values = joint.shape[1] - 2 * lanes
+    heads = lanes // FEAT
+    vmem, anywhere = pl.BlockSpec(memory_space=pltpu.VMEM), pl.BlockSpec(memory_space=pl.ANY)
+    n_z = n_sp // 2
+    sems = 5 * n_copies(n_z) + n_sp
+    shape = jax.ShapeDtypeStruct
+    return pl.pallas_call(
+        functools.partial(forward_kernel, n_sp),
+        out_shape=(
+            shape((tok, values), BF16), shape((tok, values), F32), shape((tok, lanes), BF16),
+            shape((tok, lanes), BF16), shape((tok, values), BF16), shape((tok, dim), BF16),
+            shape((heads, ROWS_S, PAD_F), BF16), shape((8, dim), F32),
+        ) + tuple(shape((s.shape[0] * n_sp, s.shape[1]), BF16) for s in shards),
+        in_specs=[vmem] * 8 + [anywhere] * 5,
+        out_specs=(vmem,) * 8 + (anywhere,) * 5,
+        scratch_shapes=[
+            pltpu.VMEM((tok, tok), F32),
+            pltpu.VMEM((dim, joint.shape[1]), BF16),
+            pltpu.VMEM((tok, values), F32),
+            pltpu.VMEM((tok, values), F32),
+            pltpu.VMEM((heads, ROWS_S, PAD_F), BF16),
+            pltpu.VMEM((heads, ROWS_S, PAD_F), BF16),
+            pltpu.VMEM((heads, ROWS_S, PAD_F), BF16),
+            pltpu.VMEM((n_sp - 1, 8, dim), F32),
+            pltpu.SemaphoreType.DMA((sems,)),
+            pltpu.SemaphoreType.DMA((sems,)),
+            pltpu.SemaphoreType.DMA((5,)),
+        ],
+        compiler_params=pltpu.CompilerParams(
+            collective_id=0, has_side_effects=True, vmem_limit_bytes=60 << 20
+        ),
+        name="forward",
+    )(x, gains, doc_col, doc_row, prior_col, tail_row, passes, table, *shards)
 
 
 def ghat_kernel(q_ref, g_ref, att_ref, inv_ref, head_row_ref, table_ref, ghat_ref, out_ref):
@@ -372,15 +632,6 @@
     tok = tokens.shape[0]
     heads = w_query.shape[1] // FEAT
     table = feature_table()
-    gather = lambda a: lax.all_gather(a, "sp", axis=0, tiled=True)
-    gain_one = gather(gain_attn).astype(F32)
-    gain_two = gather(gain_mlp).astype(F32)
-    w_joint = gather(jnp.concatenate([w_query, w_key, w_value], axis=1))
-    out_t = gather(w_out.T)
-    wg = gather(w_gate)
-    wu = gather(w_up)
-    wd = gather(w_down.T)
-
     doc_all = doc_ids[0]
     doc = lax.dynamic_slice(doc_all, (me * tok,), (tok,))
     ends = doc_all.reshape(n_sp, tok)
@@ -389,7 +640,6 @@
     prev_last = jnp.where(me > 0, lasts[jnp.maximum(me - 1, 0)], -1)
     next_first = jnp.where(me < n_sp - 1, firsts[jnp.minimum(me + 1, n_sp - 1)], -1)
     order = jnp.arange(n_sp)
-    from_prior = ((order < me) & (lasts == prev_last)).astype(F32)
     from_later = ((order > me) & (firsts == next_first)).astype(F32)
     tail_row = (doc == my_last).astype(F32)[None, :]
     head_row = (doc == my_first).astype(F32)[None, :]
@@ -397,26 +647,27 @@
     later_col = (doc == next_first).astype(F32)[:, None]
     doc_col, doc_row = doc[:, None], doc[None, :]
 
+    width = gain_attn.shape[0]
+    dim = tokens.shape[1]
+    gains = lax.dynamic_update_slice(
+        jnp.zeros((8, dim), F32), jnp.stack([gain_attn, gain_mlp]).astype(F32), (0, me * width)
+    )
+    go_on = jnp.full((8, PAD_F), (my_last == prev_last).astype(F32))
+    shards = (
+        jnp.concatenate([w_query, w_key, w_value], axis=1), w_out.T, w_gate, w_up, w_down.T
+    )
+    (
+        att, inv, q, k, v, normed_one, prior_state, gain, w_joint, out_t, wg, wu, wd
+    ) = forward(n_sp, tokens, gains, doc_col, doc_row, prior_col, tail_row, go_on, table, shards)
+    gain_one, gain_two = gain[0], gain[1]
     resid = tokens.astype(F32)
-    normed_one = rms_scale(resid, gain_one).astype(BF16)
-    projected = mm(normed_one, w_joint).astype(BF16)
     lanes = heads * FEAT
-    q, k, v = projected[:, :lanes], projected[:, lanes : 2 * lanes], projected[:, 2 * lanes :]
     state_shape = jax.ShapeDtypeStruct((heads, ROWS_S, PAD_F), BF16)
-    own_state = call(states_kernel, state_shape, k, v, tail_row, table, name="states")
 
     def combine(state, weights):
         every = lax.all_gather(state, "sp", axis=0, tiled=False).astype(F32)
         return (jnp.einsum("n,nhrf->hrf", weights, every) * table[4]).astype(BF16)
 
-    prior_state = combine(own_state, from_prior)
-    att, inv = call(
-        forward_kernel,
-        (jax.ShapeDtypeStruct(v.shape, BF16), jax.ShapeDtypeStruct(v.shape, F32)),
-        q, k, v, prior_state, doc_col, doc_row, prior_col, table,
-        scratch=[pltpu.VMEM((tok, tok), F32)],
-        name="attend",
-    )
     output, g_hidden, grad_gain_two, dg, du, dd = ffn(
         tokens, att, out_t, gain_two[None, :], cotangent, wg, wu, wd
     )

time: 869 us -> 733 us (0.84)
  waiting for transfers between devices: 521 us -> 300 us
  Pallas kernels: 191 us -> 308 us
  blocking collectives: 48.5 us -> 25 us
  matrix products: 43 us -> 31.2 us
    all_gather x5 -> x0, waiting for transfers between devices: 201 us -> none  [body(): gather = lambda a: lax.all_gather(a, 'sp', axis=0, tiled=True)]
    pallas_call x0 -> x1, Pallas kernels: none -> 156 us  [forward(): pl.pallas_call(functools.partial(forward_kernel, n_sp), out_shape=(shape(...]
    pallas_call x4 -> x2, Pallas kernels: 120 us -> 81.1 us  [call(): pl.pallas_call(kernel, out_shape=out_shape, in_specs=[vmem] * len(args),...]
    all_gather x2 -> x0, blocking collectives: 23.6 us -> none  [body(): gather = lambda a: lax.all_gather(a, 'sp', axis=0, tiled=True)]
    all_gather x2 -> x1, waiting for transfers between devices: 81.3 us -> 62.5 us  [combine(): every = lax.all_gather(state, 'sp', axis=0, tiled=False).astype(F32)]
    dot_general x5 -> x4, matrix products: 31.1 us -> 25.3 us  [mm(): return lax.dot_general(a, b, dims, preferred_element_type=F32)]
    unnamed x56 -> x59, local copies, waits for them, and re-layouts: 16.1 us -> 18.3 us
  transfers between devices with their start and end apart: 13 -> 7, of which waited for: 11 -> 6; matrix products, arithmetic and copies ran while one was open for 7% -> 5% of each run, Pallas kernels for 11% -> 9%
where the time goes in v2:
time: 733 us; the launch traced here: 724 us
  Pallas kernels  308 us (42%)
  waiting for transfers between devices  300 us (41%)
  matrix products  31.2 us (4%)
  local copies, waits for them, and re-layouts  26.7 us (4%)
  blocking collectives  25 us (3%)
  between operations  17.2 us (2%)
  other arithmetic  15.4 us (2%)
    reduce_scatter x5, waiting for transfers between devices, reduced(): lax.psum_scatter(grad.astype(BF16), 'sp', scatter_dimension=0, tiled=True)  193 us
    pallas_call x1, Pallas kernels, forward(): pl.pallas_call(functools.partial(forward_kernel, n_sp), out_shape=(shape(...  156 us
    pallas_call x2, Pallas kernels, call(): pl.pallas_call(kernel, out_shape=out_shape, in_specs=[vmem] * len(args),...  81.1 us
    pallas_call x1, Pallas kernels, ffn(): pl.pallas_call(functools.partial(ffn_kernel, width), grid=(pl.cdiv(width,...  71.1 us
    all_gather x1, waiting for transfers between devices, combine(): every = lax.all_gather(state, 'sp', axis=0, tiled=False).astype(F32)  62.5 us
    psum x1, waiting for transfers between devices, reduced(): return lax.psum(part, 'dp').astype(F32)  42.4 us
    dot_general x4, matrix products, mm(): return lax.dot_general(a, b, dims, preferred_element_type=F32)  25.3 us
    unnamed x59, local copies, waits for them, and re-layouts  18.3 us
  transfers between devices with their start and end apart: 7, of which 6 were waited for; matrix products, arithmetic and copies ran while one was open for 5% of the time, Pallas kernels for 9%

profile of v2, /device:TPU:0, one launch (start us, length us, event | category | flops | bytes accessed | tf_op | source)
XLA Modules:
  0.0 724.1 jit_solution(9000533476633987463)
XLA Ops:
  8.6 1.9 compare_convert_fusion.2
  16.1 2.3 copy.62
  18.3 2.3 copy.64.gate_own
  26.3 156.3 %forward.1 = (bf16[1024,1024]{1,0:T(8,128)(2,1)}, f32[1024,1024]{1,0:T(8,128)}, bf16[1024,256]{1,0:T(8,128)(2,1)}, bf16[1024,256]{1,0:T(8,128)(2,1)}, bf16[1024,...) custom-call(bf16[1024,1024]{1,0:T(8,128)(2,1)} %x_ref.3, ...), custom_call_target="tpu_custom_call" | custom-call | tf_op jit(solution)/shard_map/forward/pallas_call | solution.py:373
  184.0 71.1 %ffn.1 = (bf16[1024,1024]{1,0:T(8,128)(2,1)}, f32[1024,1024]{1,0:T(8,128)}, f32[1,1024]{1,0:T(1,128)}, bf16[1024,2752]{1,0:T(8,128)(2,1)}, bf16[1024,2752]{1,0:T(8,128)(2,1)}, /*index=5*/bf16[1024,2752]{1,0:T(8,128)(2,1)}) custom-call(bf16[1024,1024]{1,0:T(8,128)(2,1)} %x_ref.3, bf16[1024,1024]{1,0:T(8,128)(2,1)} %get-tuple-element.35.att_ref, ...), custom_call_target="tpu_custom_call" | custom-call | tf_op jit(solution)/shard_map/ffn/pallas_call | solution.py:588
  255.2 5.9 convolution_convert_fusion.2.g_ref
  261.0 16.2 %ghat.1 = (bf16[8,1024,256]{2,1,0:T(8,128)(2,1)}, bf16[16,80,256]{2,1,0:T(8,128)(2,1)}) custom-call(bf16[1024,256]{1,0:T(8,128)(2,1)} %get-tuple-element.43.q_ref, bf16[1024,1024]{1,0:T(8,128)(2,1)} %convolution_convert_fusion.2.g_ref, bf16[1024,1024]{1,0:T(8,128)(2,1)} %get-tuple-element.35.att_ref, f32[1024,1024]{1,0:T(8,128)} %get-tuple-element.46.inv_ref, ...), custom_call_target="tpu_custom_call" | custom-call | tf_op jit(solution)/shard_map/ghat/pallas_call | solution.py:516
  277.3 5.9 convolution_convert_fusion.1
  285.2 62.5 %all-gather.3.cloned.1.call-done = bf16[128,80,256]{2,1,0:T(8,128)(2,1)} async-done(((bf16[16,80,256]{2,1,0:T(8,128)(2,1)}), bf16[128,80,256]{2,1,0:T(8,128)(2,1)}) %all-gather.3.cloned.1.call-update) | async-done | bytes 5242896 | tf_op jit(solution)/shard_map/all_gather | solution.py:668
  347.7 5.9 fusion
  354.6 64.9 %attend_back.1 = (bf16[1024,256]{1,0:T(8,128)(2,1)}, bf16[1024,256]{1,0:T(8,128)(2,1)}, bf16[1024,1024]{1,0:T(8,128)(2,1)}) custom-call(bf16[1024,256]{1,0:T(8,128)(2,1)} %get-tuple-element.43.q_ref, bf16[1024,256]{1,0:T(8,128)(2,1)} %get-tuple-element.44.k_ref, bf16[1024,1024]{1,0:T(8,128)(2,1)} %get-tuple-element.45.v_ref, ...), custom_call_target="tpu_custom_call" | custom-call | tf_op jit(solution)/shard_map/attend_back/pallas_call | solution.py:516
  422.2 1.6 copy-done.13
  423.9 5.1 convolution_convert_fusion
  429.2 21.1 %reduce-scatter.14.cloned.1.call-done = bf16[128,2752]{1,0:T(8,128)(2,1)} async-done(((bf16[1024,2752]{1,0:T(8,128)(2,1)}), bf16[128,2752]{1,0:T(8,128)(2,1)}) %reduce-scatter.14.cloned.1.call-update) | async-done | bytes 704528 | tf_op jit(solution)/shard_map/reduce_scatter | solution.py:702
  450.3 65.4 %reduce-scatter.10.cloned.1.call-done = bf16[128,2752]{1,0:T(8,128)(2,1)} async-done(((bf16[1024,2752]{1,0:T(8,128)(2,1)}), bf16[128,2752]{1,0:T(8,128)(2,1)}) %reduce-scatter.10.cloned.1.call-update) | async-done | bytes 704528 | tf_op jit(solution)/shard_map/reduce_scatter | solution.py:702
  515.8 65.4 %reduce-scatter.12.cloned.1.call-done = bf16[128,2752]{1,0:T(8,128)(2,1)} async-done(((bf16[1024,2752]{1,0:T(8,128)(2,1)}), bf16[128,2752]{1,0:T(8,128)(2,1)}) %reduce-scatter.12.cloned.1.call-update) | async-done | bytes 704528 | tf_op jit(solution)/shard_map/reduce_scatter | solution.py:702
  581.2 40.9 %reduce-scatter.6.cloned.1.call-done = bf16[128,1536]{1,0:T(8,128)(2,1)} async-done(((bf16[1024,1536]{1,0:T(8,128)(2,1)}), bf16[128,1536]{1,0:T(8,128)(2,1)}) %reduce-scatter.6.cloned.1.call-update) | async-done | bytes 393232 | tf_op jit(solution)/shard_map/reduce_scatter | solution.py:702
  623.9 8.5 %fusion.7 = (bf16[1024]{0:T(1024)(128)(2,1)S(1)}, f32[1024]{0:T(1024)S(1)}, f32[1024,1024]{1,0:T(8,128)}) fusion(bf16[1024,1024]{1,0:T(8,128)(2,1)S(1)} %copy-done, f32[1024]{0:T(1024)S(1)} %add_rsqrt_fusion, f32[1024]{0:T(1024)S(1)} %bitcast.40, bf16[1024,1536]{1,0:T(8,128)(2,1)} %copy-done.13, bf16[1024,1536]{1,0:T(8,128)(2,1)} %get-tuple-element.53), kind=kOutput, calls=%fused_computation.11 | convolution fusion | flops 3228563456 | bytes 12597248 | tf_op jit(solution)/shard_map/dot_general | solution.py:26
  632.4 15.0 %all-reduce.2 = (bf16[1024]{0:T(1024)(128)(2,1)S(1)}, bf16[1024]{0:T(1024)(128)(2,1)S(1)}) all-reduce(bf16[1024]{0:T(1024)(128)(2,1)S(1)} %get-tuple-element.103, bf16[1024]{0:T(1024)(128)(2,1)S(1)} %convert_reduce_fusion), channel_id=3, replica_groups=mesh['dp'=4,'sp'=8] {'sp'}, use_global_device_ids=true, to_apply=%region_3.4.clone | all-reduce | flops 2048 | bytes 8192
  647.6 9.9 %all-reduce.3 = (bf16[128]{0:T(256)(128)(2,1)S(1)}, bf16[128]{0:T(256)(128)(2,1)S(1)}) all-reduce(bf16[128]{0:T(256)(128)(2,1)S(1)} %dynamic-slice.4, bf16[128]{0:T(256)(128)(2,1)S(1)} %dynamic-slice.6), channel_id=1, replica_groups=mesh['dp'=4,'sp'=8] {'dp'}, use_global_device_ids=true, to_apply=%region_4.5 | all-reduce | flops 256 | bytes 1024 | tf_op jit(solution)/shard_map/psum | solution.py:703
  658.5 6.4 fusion.5
  665.0 42.4 %all-reduce.7.cloned.1.call-done = (bf16[128,1536]{1,0:T(8,128)(2,1)}, bf16[1024,128]{0,1:T(8,128)(2,1)}, bf16[128,2752]{1,0:T(8,128)(2,1)}, bf16[128,2752]{1,0:T(8,128)(2,1)}, bf16[2752,128]{0,1:T(8,128)(2,1)}) async-done(((bf16[128,1536]{1,0:T(8,128)(2,1)}, bf16[1024,128]{0,1:T(8,128)(2,1)}, bf16[128,2752]{1,0:T(8,128)(2,1)}, bf16[128,2752]{1,0:T(8,128)(2,1)}, bf16[2752,128]{0,1:T(8,128)(2,1)}), ...) | async-done | bytes 2768912 | tf_op jit(solution)/shard_map/psum | solution.py:703
  707.4 1.9 slice.46
  710.9 2.5 copy.71
  (93 shorter events, 25.5 us)
Async XLA Ops:
  7.2 13.4 %copy-start.7 = (bf16[128,2752]{0,1:T(8,128)(2,1)S(1)}, bf16[128,2752]{0,1:T(8,128)(2,1)}, u32[]{:S(2)}) copy-start(bf16[128,2752]{0,1:T(8,128)(2,1)} %param.22) | copy-start | bytes 2113540
  7.2 14.6 %copy-start.10 = (bf16[1024,128]{1,0:T(8,128)(2,1)S(1)}, bf16[1024,128]{1,0:T(8,128)(2,1)}, u32[]{:S(2)}) copy-start(bf16[1024,128]{1,0:T(8,128)(2,1)} %param.19) | copy-start | bytes 786436
  7.2 340.5 %all-gather.3.cloned.1.call-start = ((), (), s32[]{:S(2)}) async-start(), calls=%async_computation.10 | async-start | bytes 5898240 | tf_op jit(solution)/shard_map/all_gather | solution.py:668
  10.5 14.4 %copy-start.12 = (s32[1,1024]{1,0:T(1,128)}, s32[1,1024]{1,0:T(1,128)S(1)}, u32[]{:S(2)}) copy-start(s32[1,1024]{1,0:T(1,128)S(1)} %get-tuple-element.115.doc_row_ref) | copy-start | bytes 12292
  12.0 12.9 %copy-start.2 = (s32[1024,1]{1,0:T(8,128)}, s32[1024,1]{1,0:T(8,128)S(1)}, u32[]{:S(2)}) copy-start(s32[1024,1]{1,0:T(8,128)S(1)} %copy.63.doc_col_ref) | copy-start | bytes 12292
  16.0 8.9 %copy-start.8 = (bf16[128,1024]{1,0:T(8,128)(2,1)S(1)}, bf16[128,1024]{1,0:T(8,128)(2,1)}, u32[]{:S(2)}) copy-start(bf16[128,1024]{1,0:T(8,128)(2,1)} %param.18) | copy-start | bytes 786436
  16.0 8.8 %copy-start.14 = (bf16[128,256]{1,0:T(8,128)(2,1)S(1)}, bf16[128,256]{1,0:T(8,128)(2,1)}, u32[]{:S(2)}) copy-start(bf16[128,256]{1,0:T(8,128)(2,1)} %param.17) | copy-start | bytes 196612
  16.0 8.8 %copy-start.15 = (bf16[128,256]{1,0:T(8,128)(2,1)S(1)}, bf16[128,256]{1,0:T(8,128)(2,1)}, u32[]{:S(2)}) copy-start(bf16[128,256]{1,0:T(8,128)(2,1)} %param.16) | copy-start | bytes 196612
  18.3 7.3 %copy-start.18 = (bf16[128]{0:T(256)(128)(2,1)S(1)}, bf16[128]{0:T(256)(128)(2,1)}, u32[]{:S(2)}) copy-start(bf16[128]{0:T(256)(128)(2,1)} %param.20) | copy-start | bytes 772
  18.3 7.3 %copy-start.19 = (bf16[128]{0:T(256)(128)(2,1)S(1)}, bf16[128]{0:T(256)(128)(2,1)}, u32[]{:S(2)}) copy-start(bf16[128]{0:T(256)(128)(2,1)} %param.15) | copy-start | bytes 772
  184.0 71.1 %copy-start.4 = (bf16[1024,1024]{1,0:T(8,128)(2,1)S(1)}, bf16[1024,1024]{1,0:T(8,128)(2,1)}, u32[]{:S(2)}) copy-start(bf16[1024,1024]{1,0:T(8,128)(2,1)} %get-tuple-element.36.out_t_ref) | copy-start | bytes 6291460
  261.0 16.3 %copy-start.1 = (bf16[1024,1024]{1,0:T(8,128)(2,1)S(1)}, bf16[1024,1024]{1,0:T(8,128)(2,1)}, u32[]{:S(2)}) copy-start(bf16[1024,1024]{1,0:T(8,128)(2,1)} %get-tuple-element.35.att_ref) | copy-start | bytes 6291460
  277.3 152.0 %reduce-scatter.8.cloned.1.call-start = ((), (), s32[]{:S(2)}) async-start(), calls=%async_computation.6 | async-start | bytes 2359296 | tf_op jit(solution)/shard_map/reduce_scatter | solution.py:702
  283.2 167.1 %reduce-scatter.14.cloned.1.call-start = ((), (), s32[]{:S(2)}) async-start(), calls=%async_computation.9 | async-start | bytes 6488064 | tf_op jit(solution)/shard_map/reduce_scatter | solution.py:702
  284.0 231.8 %reduce-scatter.10.cloned.1.call-start = ((), (), s32[]{:S(2)}) async-start(), calls=%async_computation.7 | async-start | bytes 6488064 | tf_op jit(solution)/shard_map/reduce_scatter | solution.py:702
  284.5 296.6 %reduce-scatter.12.cloned.1.call-start = ((), (), s32[]{:S(2)}) async-start(), calls=%async_computation.8 | async-start | bytes 6488064 | tf_op jit(solution)/shard_map/reduce_scatter | solution.py:702
  285.1 337.0 %reduce-scatter.6.cloned.1.call-start = ((), (), s32[]{:S(2)}) async-start(), calls=%async_computation.5 | async-start | bytes 3538944 | tf_op jit(solution)/shard_map/reduce_scatter | solution.py:702
  347.7 5.9 copy-start.17
  428.9 193.2 %copy-start.21 = (u32[32]{0:T(128)S(1)}, u32[32]{0:T(128)}, u32[]{:S(2)}) copy-start(u32[32]{0:T(128)} %constant.42) | copy-start | bytes 388
  428.9 194.4 %copy-start.16 = (f32[1,1024]{1,0:T(1,128)S(1)}, f32[1,1024]{1,0:T(1,128)}, u32[]{:S(2)}) copy-start(f32[1,1024]{1,0:T(1,128)} %get-tuple-element.55) | copy-start | bytes 12292
  428.9 194.5 %copy-start = (bf16[1024,1024]{1,0:T(8,128)(2,1)S(1)}, bf16[1024,1024]{1,0:T(8,128)(2,1)}, u32[]{:S(2)}) copy-start(bf16[1024,1024]{1,0:T(8,128)(2,1)} %x_ref.3) | copy-start | bytes 6291460
  428.9 278.4 %all-reduce.7.cloned.1.call-start = ((), (), s32[]{:S(2)}) async-start(), calls=%async_computation.11 | async-start | bytes 5636096 | tf_op jit(solution)/shard_map/psum | solution.py:703
  707.4 6.0 copy-start.6
  707.4 7.4 %copy-start.5 = (bf16[2752,128]{0,1:T(8,128)(2,1)S(1)}, bf16[2752,128]{0,1:T(8,128)(2,1)}, u32[]{:S(2)}) copy-start(bf16[2752,128]{0,1:T(8,128)(2,1)} %get-tuple-element.113) | copy-start | bytes 2113540
  (5 other events, 14.4 us)
Sparse Core Ops, SparseCore 0:
  277.4 70.2 all-gather.2
  350.0 34.6 reduce-scatter.7
  386.9 63.3 reduce-scatter.13
  452.5 63.2 reduce-scatter.9
  517.9 63.2 reduce-scatter.11
  583.3 38.7 reduce-scatter.5
  625.7 81.5 all-reduce.6

commit v3 on v2

v3 whole, which is shorter than its diff:
```python
import functools
import math

import jax
import jax.numpy as jnp
import numpy as np
from jax import lax
from jax.experimental import pallas as pl
from jax.experimental.pallas import tpu as pltpu
from jax.sharding import PartitionSpec as P

FEAT = 16
HEAD_V = 64
EPSILON = 1e-05
BF16 = jnp.bfloat16
F32 = jnp.float32
BLK = 256
PAD_F = 256
ROWS_S = 80
NN = (((1,), (0,)), ((), ()))
NT = (((1,), (1,)), ((), ()))
TN = (((0,), (0,)), ((), ()))


def mm(a, b, dims=NN):
    return lax.dot_general(a, b, dims, preferred_element_type=F32)


def feature_table():
    rows = []
    for a in range(FEAT):
        for b in range(a, FEAT):
            rows.append((a, b, 0.0, 0.0, 1.0 if a == b else 2.0))
    for a in range(FEAT):
        rows.append((a, -1, 0.0, 1.0, 8.0))
    rows.append((-1, -1, 1.0, 1.0, 32.0))
    while len(rows) < PAD_F:
        rows.append((-1, -1, 0.0, 0.0, 0.0))
    table = np.zeros((8, PAD_F), np.float32)
    table[:5] = np.array(rows, np.float32).T
    return jnp.asarray(table)


def selectors(table, head, lanes):
    row = lax.broadcasted_iota(jnp.int32, (lanes, PAD_F), 0).astype(F32)
    base = (head * FEAT).astype(F32)
    first = jnp.where((row == table[0:1] + base) & (table[0:1] >= 0), 1.0, 0.0).astype(BF16)
    second = jnp.where((row == table[1:2] + base) & (table[1:2] >= 0), 1.0, 0.0).astype(BF16)
    return first, second


def head_lanes(values, head, scale=1):
    lane = lax.broadcasted_iota(jnp.int32, values.shape, 1)
    return jnp.where(lane // FEAT == head, values * scale, jnp.zeros_like(values))


def factors(values, sel, table):
    one = mm(values, sel[0]) + table[2:3]
    two = mm(values, sel[1]) + table[3:4]
    return one, two


def with_ones(v_pair):
    return jnp.concatenate([v_pair, jnp.ones_like(v_pair)], axis=1)


class Copies:
    def __init__(self, send_sem, recv_sem):
        self.send_sem, self.recv_sem, self.made = send_sem, recv_sem, {}

    def add(self, name, src, dst, device):
        self.made[name] = (src, dst, len(self.made), device)

    def get(self, name):
        src, dst, index, device = self.made[name]
        return pltpu.make_async_remote_copy(
            src_ref=src,
            dst_ref=dst,
            send_sem=self.send_sem.at[index],
            recv_sem=self.recv_sem.at[index],
            device_id=device,
            device_id_type=pl.DeviceIdType.MESH,
        )

    def start(self, *names):
        for name in names:
            self.get(name).start()

    def arrived(self, *names):
        for name in names:
            self.get(name).wait_recv()

    def sent(self, *names):
        for name in names:
            self.get(name).wait_send()


GROUP = 4


def place(n_sp):
    dp, sp = lax.axis_index("dp"), lax.axis_index("sp")
    g = lax.rem(dp, GROUP)
    gy, gx = g // 2, lax.rem(g, 2)
    z, c = sp // 2, lax.rem(sp, 2)
    across_x = (dp - g + gy * 2 + (1 - gx), sp)
    across_y = (dp - g + (1 - gy) * 2 + gx, sp)
    diagonal = (dp - g + (1 - gy) * 2 + (1 - gx), sp)
    partner = (dp, z * 2 + (1 - c))
    return dp, sp, g, gy, gx, z, c, across_x, across_y, diagonal, partner


class Gather:
    def __init__(self, copies, tag, n_z, own, full, where):
        dp, sp, g, gy, gx, z, c, across_x, across_y, _, partner = where
        self.copies, self.tag, self.n_z = copies, tag, n_z
        shard, width = own.shape
        quarter = shard // GROUP
        lower, upper = pl.ds(0, width // 2), pl.ds(width // 2, width // 2)

        def rows(zz, gg, count, lanes=None):
            start = pl.multiple_of((zz * 2 + c) * shard + gg * quarter, 16)
            return full.at[pl.ds(start, count)] if lanes is None else full.at[pl.ds(start, count), lanes]

        gx_of, gy_of = gy * 2 + (1 - gx), (1 - gy) * 2 + gx
        diag = (1 - gy) * 2 + (1 - gx)
        add = lambda name, src, dst, device: copies.add((tag, name), src, dst, device)
        mine = own.at[pl.ds(pl.multiple_of(g * quarter, 16), quarter)]
        self.own_place = rows(z, 0, shard)
        add("c0", own, self.own_place, partner)
        for i in range(1, n_z):
            zt = lax.rem(z + i, n_z)
            zs = lax.rem(z + n_z - i, n_z)
            add(f"z{i}", mine, rows(z, g, quarter), (dp, zt * 2 + c))
            here = rows(zs, g, quarter)
            add(f"x{i}", here, here, across_x)
            add(f"y{i}", here, here, across_y)
            add(f"c1{i}", here, here, partner)
            first = rows(zs, gx_of, quarter, lower)
            add(f"d0{i}", first, first, across_y)
            second = rows(zs, gy_of, quarter, upper)
            add(f"d1{i}", second, second, across_x)
            for name, gg in (("c2", gx_of), ("c3", gy_of), ("c4", diag)):
                there = rows(zs, gg, quarter)
                add(f"{name}{i}", there, there, partner)

    def each(self, *names):
        return [(self.tag, f"{name}{i}") for i in range(1, self.n_z) for name in names]

    def stage(self, n):
        copies = self.copies
        if n == 0:
            copies.start(*self.each("z"), (self.tag, "c0"))
        elif n == 1:
            for i in range(1, self.n_z):
                copies.arrived((self.tag, f"z{i}"))
                copies.start(*[(self.tag, f"{name}{i}") for name in ("x", "y", "c1")])
        elif n == 2:
            for i in range(1, self.n_z):
                copies.arrived((self.tag, f"x{i}"), (self.tag, f"y{i}"))
                copies.start(*[(self.tag, f"{name}{i}") for name in ("d0", "d1", "c2", "c3")])
        elif n == 3:
            for i in range(1, self.n_z):
                copies.arrived((self.tag, f"d0{i}"), (self.tag, f"d1{i}"))
                copies.start((self.tag, f"c4{i}"))
        else:
            copies.arrived((self.tag, "c0"), *self.each("c1", "c2", "c3", "c4"))
            copies.sent((self.tag, "c0"), *self.each("z", "x", "y", "c1", "d0", "d1", "c2", "c3", "c4"))


def n_copies(n_z):
    return 1 + 9 * (n_z - 1)


def meet(devices):
    barrier = pltpu.get_barrier_semaphore()
    for device in devices:
        pl.semaphore_signal(barrier, inc=1, device_id=device, device_id_type=pl.DeviceIdType.MESH)
    pl.semaphore_wait(barrier, len(devices))


def placed(state, side, z_rows):
    zero = jnp.zeros((64, PAD_F), state.dtype)
    values = [state[0:64], zero] if side == 0 else [zero, state[0:64]]
    return jnp.concatenate(values + [z_rows], axis=0)


class Reduce:
    def __init__(self, copies, tag, n_z, where, source, swapped, buffers, final, stage_buf=None, local_sem=None):
        dp, sp, g, gy, gx, z, c, across_x, across_y, diagonal, partner = where
        self.copies, self.tag, self.n_z = copies, tag, n_z
        self.gy, self.gx, self.z, self.c = gy, gx, z, c
        self.source, self.swapped, self.final = source, swapped, final
        self.work, self.first, self.second, self.along = buffers
        self.stage_buf, self.local_sem = stage_buf, local_sem
        work = self.work
        half = work.shape[-1] // 2
        self.halves = (pl.ds(0, half), pl.ds(half, half))
        lower, upper = self.halves
        everything = slice(None)
        add = lambda name, src, dst, device: copies.add((tag, name), src, dst, device)
        add("s", source.at[:, 1 - c], swapped, partner)
        add("a1", work.at[:, :, 1 - gx, everything, lower], self.first.at[0], across_x)
        add("b1", work.at[:, 1 - gy, :, everything, upper], self.first.at[1], across_y)
        add("a2", work.at[:, 1 - gy, gx, everything, lower], self.second.at[0], across_y)
        add("b2", work.at[:, gy, 1 - gx, everything, upper], self.second.at[1], across_x)
        for i in range(1, n_z):
            zt = lax.rem(z + i, n_z)
            add(f"z{i}", work.at[zt, gy, gx], self.along.at[i - 1], (dp, zt * 2 + c))
        for name, device in (("fx", across_x), ("fy", across_y), ("fd", diagonal)):
            add(name, final.at[gy, gx], final.at[gy, gx], device)

    def names(self, *names):
        return [(self.tag, name) for name in names]

    def load(self, zz):
        slot = zz % 2
        return (
            pltpu.make_async_copy(self.source.at[zz, self.c], self.stage_buf.at[slot, 0], self.local_sem.at[slot, 0]),
            pltpu.make_async_copy(self.swapped.at[zz], self.stage_buf.at[slot, 1], self.local_sem.at[slot, 1]),
        )

    def stage(self, n):
        copies, work, gy, gx, n_z = self.copies, self.work, self.gy, self.gx, self.n_z
        zs = ["z%d" % i for i in range(1, n_z)]
        lower, upper = self.halves
        if n == 0:
            copies.start(*self.names("s"))
        elif n == 1:
            copies.arrived(*self.names("s"))
            if self.stage_buf is None:

                def add_held(i, carry):
                    zz, yy, xx = i // 4, lax.rem(i // 2, 2), lax.rem(i, 2)
                    work[zz, yy, xx] = self.source[zz, self.c, yy, xx] + self.swapped[zz, yy, xx]
                    return carry

                lax.fori_loop(0, 4 * n_z, add_held, 0)
                copies.start(*self.names("a1", "b1"))
                return
            for copy in self.load(0):
                copy.start()
            for zz in range(n_z):
                if zz + 1 < n_z:
                    for copy in self.load(zz + 1):
                        copy.start()
                for copy in self.load(zz):
                    copy.wait()
                slot = zz % 2

                def add_quarter(i, carry):
                    yy, xx = i // 2, lax.rem(i, 2)
                    work[zz, yy, xx] = self.stage_buf[slot, 0, yy, xx] + self.stage_buf[slot, 1, yy, xx]
                    return carry

                lax.fori_loop(0, 4, add_quarter, 0)
            copies.start(*self.names("a1", "b1"))
        elif n == 2:
            copies.arrived(*self.names("a1"))

            def add_a(i, carry):
                zz, yy = i // 2, lax.rem(i, 2)
                work[zz, yy, gx, :, lower] = work[zz, yy, gx, :, lower] + self.first[0, zz, yy]
                return carry

            lax.fori_loop(0, 2 * n_z, add_a, 0)
            copies.start(*self.names("a2"))
            copies.arrived(*self.names("b1"))

            def add_b(i, carry):
                zz, xx = i // 2, lax.rem(i, 2)
                work[zz, gy, xx, :, upper] = work[zz, gy, xx, :, upper] + self.first[1, zz, xx]
                return carry

            lax.fori_loop(0, 2 * n_z, add_b, 0)
            copies.start(*self.names("b2"))
        elif n == 3:
            copies.arrived(*self.names("a2", "b2"))

            def add_c(zz, carry):
                work[zz, gy, gx, :, lower] = work[zz, gy, gx, :, lower] + self.second[0, zz]
                work[zz, gy, gx, :, upper] = work[zz, gy, gx, :, upper] + self.second[1, zz]
                return carry

            lax.fori_loop(0, n_z, add_c, 0)
            copies.start(*self.names(*zs))
        elif n == 4:
            copies.arrived(*self.names(*zs))
            total = work[self.z, gy, gx].astype(F32)
            for i in range(n_z - 1):
                total = total + self.along[i].astype(F32)
            self.final[gy, gx] = total.astype(BF16)
            copies.start(*self.names("fx", "fy", "fd"))
        else:
            copies.arrived(*self.names("fx", "fy", "fd"))
            copies.sent(*self.names("s", "a1", "b1", "a2", "b2", "fx", "fy", "fd", *zs))


def reduce_scratch(n_z, rows, width):
    return [
        pltpu.VMEM((n_z, 2, 2, rows, width), BF16),
        pltpu.VMEM((2, n_z, 2, rows, width // 2), BF16),
        pltpu.VMEM((2, n_z, rows, width // 2), BF16),
        pltpu.VMEM((n_z - 1, rows, width), BF16),
    ]


def n_reduce(n_z):
    return 8 + n_z - 1


class Chain:
    def __init__(self, copies, where, n_z, onward, own, mate, carry, out, pass_lead, pass_other):
        dp, sp, g, gy, gx, z, c, across_x, across_y, diagonal, partner = where
        lead = 1 if onward else 0
        self.copies, self.n_z = copies, n_z
        self.own, self.mate, self.carry, self.out = own, mate, carry, out
        self.pass_lead, self.pass_other = pass_lead, pass_other
        self.leads = c == lead
        self.place = z if onward else n_z - 1 - z
        to = lax.rem(z + 1, n_z) if onward else lax.rem(z + n_z - 1, n_z)
        before = lax.rem(z + n_z - 1, n_z) if onward else lax.rem(z + 1, n_z)
        self.next_device, self.last_device = (dp, to * 2 + c), (dp, before * 2 + c)
        copies.add("own", own, mate, partner)
        copies.add("raw", carry, carry, partner)
        copies.add("carry", out, carry, self.next_device)

    def begin(self):
        @pl.when(jnp.logical_not(self.leads))
        def _():
            self.copies.start("own")

        @pl.when(self.leads & (self.place == 0))
        def _():
            self.carry[...] = jnp.zeros_like(self.carry)

    def middle(self, now):
        now = now & self.leads

        @pl.when(now)
        def _():
            self.copies.arrived("own")

        @pl.when(now & (self.place > 0))
        def _():
            self.copies.arrived("carry")

        @pl.when(now)
        def _():
            self.copies.start("raw")

        @pl.when(now & (self.place < self.n_z - 1))
        def _():
            def one(head, carry):
                inner = self.mate[head].astype(F32) + self.pass_other * self.carry[head].astype(F32)
                self.out[head] = (self.own[head].astype(F32) + self.pass_lead * inner).astype(BF16)
                return carry

            lax.fori_loop(0, self.own.shape[0], one, 0)
            self.copies.start("carry")

    def finish(self, result, weights):
        @pl.when(jnp.logical_not(self.leads))
        def _():
            self.copies.arrived("raw")

            def one(head, carry):
                result[head] = (self.carry[head].astype(F32) * weights).astype(BF16)
                return carry

            lax.fori_loop(0, self.own.shape[0], one, 0)

        @pl.when(self.leads)
        def _():
            def one(head, carry):
                total = self.mate[head].astype(F32) + self.pass_other * self.carry[head].astype(F32)
                result[head] = (total * weights).astype(BF16)
                return carry

            lax.fori_loop(0, self.own.shape[0], one, 0)

    def drain(self):
        @pl.when(jnp.logical_not(self.leads))
        def _():
            self.copies.sent("own")

        @pl.when(self.leads)
        def _():
            self.copies.sent("raw")

        @pl.when(self.leads & (self.place < self.n_z - 1))
        def _():
            self.copies.sent("carry")


class Documents:
    def __init__(self, doc_ref, sp):
        self.ref, self.n_sp, self.tok = doc_ref, doc_ref.shape[0], doc_ref.shape[1]
        self.row = self.of(sp)
        self.column = jnp.broadcast_to(self.row, (128, self.tok)).T[:, 0:1]

    def of(self, sp):
        return self.ref[pl.ds(sp, 1), :].astype(F32)

    def last(self, sp):
        value = self.of(jnp.maximum(sp, 0))[:, self.tok - 1 : self.tok]
        return jnp.where(sp >= 0, value, -1.0)

    def first(self, sp):
        value = self.of(jnp.minimum(sp, self.n_sp - 1))[:, 0:1]
        return jnp.where(sp < self.n_sp, value, -2.0)

    def through(self, here, there):
        return jnp.broadcast_to(jnp.where(here == there, 1.0, 0.0), (1, PAD_F))


def rows_sum(values):
    total = values[0]
    for value in values[1:]:
        total = total + value
    return total


CHAIN_STEPS = 3
CHAIN_BACK_STEPS = 5
CHUNK = 256
UNITS = 4
EARLY = 2


def units_of(width):
    chunks = -(-width // CHUNK)
    step = -(-chunks // UNITS)
    return [(first, min(chunks, first + step)) for first in range(0, chunks, step)]


def forward_kernel(
    n_sp, x_ref, gain_parts_ref, doc_ref, table_ref, wo_ref, wg_ref, wu_ref, wd_ref, wq_ref, wk_ref, wv_ref, *rest,
):
    n_unit = len(units_of(wd_ref.shape[0]))
    (att_ref, inv_ref, q_ref, k_ref, v_ref, normed_ref, state_ref, gain_ref), rest = rest[:8], rest[8:]
    fulls, rest = rest[: 2 + EARLY], rest[2 + EARLY :]
    kept, rest = rest[: n_unit - EARLY], rest[n_unit - EARLY :]
    (joint_own, out_own), rest = rest[:2], rest[2:]
    ffn_own, rest = rest[:n_unit], rest[n_unit:]
    (
        mask_ref, joint_vm, num_ref, den_ref, own_state, mate_state, in_state, out_state, gains_ref, gains_in,
        prior_ref, send_sem, recv_sem, local_sem,
    ) = rest
    tok = x_ref.shape[0]
    n_z = n_sp // 2
    lanes = q_ref.shape[1]
    pairs = v_ref.shape[1] // 128
    where = place(n_sp)
    dp, sp, g, gy, gx, z, c, across_x, across_y, diagonal, partner = where
    copies = Copies(send_sem, recv_sem)
    joint_full = fulls[0]
    owns = (joint_own, out_own) + tuple(ffn_own[:EARLY])
    gathers = [Gather(copies, k, n_z, own, full, where) for k, (own, full) in enumerate(zip(owns, fulls))]
    others = [(dp, lax.rem(sp + i, n_sp)) for i in range(1, n_sp)]
    for i, device in enumerate(others, 1):
        copies.add(("gain", i), gains_ref, gains_in.at[i - 1], device)
    docs = Documents(doc_ref, sp)
    even = sp - c
    chain = Chain(
        copies, where, n_z, True, own_state, mate_state, in_state, out_state,
        docs.through(docs.last(even + 1), docs.last(even)), docs.through(docs.last(even), docs.last(even - 1)),
    )
    part_lane = lax.broadcasted_iota(jnp.int32, gains_ref.shape, 1)
    gains_ref[...] = jnp.where(part_lane // (gains_ref.shape[1] // n_sp) == sp, gain_parts_ref[...], 0.0)
    assembled = [
        pltpu.make_async_copy(wq_ref, joint_own.at[:, 0:lanes], local_sem.at[0]),
        pltpu.make_async_copy(wk_ref, joint_own.at[:, lanes : 2 * lanes], local_sem.at[1]),
        pltpu.make_async_copy(wv_ref, joint_own.at[:, 2 * lanes :], local_sem.at[2]),
    ]
    for copy in assembled:
        copy.start()
    meet(others + [across_x, across_y])
    copies.start(*[("gain", i) for i in range(1, n_sp)])
    for copy in assembled:
        copy.wait()
    gathers[0].stage(0)
    out_own[...] = wo_ref[...].T
    width = wd_ref.shape[0]
    for own, (first, last) in zip(ffn_own, units_of(width)):
        lo, hi = first * CHUNK, min(last * CHUNK, width)
        span = (last - first) * CHUNK
        for i, piece in enumerate((wg_ref[lo:hi, :].T, wu_ref[lo:hi, :].T, wd_ref[lo:hi, :].T)):
            if hi - lo < span:
                own[:, (i + 1) * span - CHUNK : (i + 1) * span] = jnp.zeros((own.shape[0], CHUNK), BF16)
            own[:, i * span : i * span + hi - lo] = piece

    table = table_ref[...]
    row = lax.broadcasted_iota(jnp.int32, (tok, tok), 0)
    col = lax.broadcasted_iota(jnp.int32, (tok, tok), 1)
    mask_ref[...] = jnp.where((row >= col) & (docs.column == docs.row), 1.0, 0.0)
    prior_ref[...] = jnp.broadcast_to(jnp.where(docs.column == docs.last(sp - 1), 1.0, 0.0), prior_ref.shape)
    copies.arrived(*[("gain", i) for i in range(1, n_sp)])
    gain_ref[...] = gains_ref[...] + rows_sum([gains_in[i] for i in range(n_sp - 1)])
    x = x_ref[...].astype(F32)
    scale = lax.rsqrt(jnp.mean(x * x, axis=1, keepdims=True) + EPSILON)
    normed_ref[...] = (x * scale * gain_ref[0:1]).astype(BF16)
    local = [
        pltpu.make_async_copy(own, gather.own_place, local_sem.at[k])
        for k, (own, gather) in enumerate(zip(owns, gathers))
    ] + [
        pltpu.make_async_copy(own, keep, local_sem.at[len(owns) + k])
        for k, (own, keep) in enumerate(zip(ffn_own[EARLY:], kept))
    ]
    for copy in local:
        copy.start()
    gathers[0].stage(1)
    gathers[1].stage(0)
    gathers[2].stage(0)
    gathers[0].stage(2)
    gathers[0].stage(3)
    gathers[0].stage(4)
    for copy in local:
        copy.wait()
    fetch = pltpu.make_async_copy(joint_full, joint_vm, local_sem.at[0])
    fetch.start()
    fetch.wait()
    wide = joint_vm.shape[1]
    for first in range(0, wide, BLK):
        part = mm(normed_ref[...], joint_vm[:, first : first + BLK]).astype(BF16)
        if first < lanes:
            q_ref[:, first : first + BLK] = part
        elif first < 2 * lanes:
            k_ref[:, first - lanes : first - lanes + BLK] = part
        else:
            v_ref[:, first - 2 * lanes : first - 2 * lanes + BLK] = part

    tail = jnp.where(docs.row == docs.last(sp), 1.0, 0.0)

    def at(p, step, *todo):
        @pl.when(p == step)
        def _():
            for k, n in todo:
                gathers[k].stage(n)

    def state_pair(p, carry):
        at(p, 0, (1, 1))
        at(p, 2, (2, 1), (3, 0))
        at(p, 5, (1, 2))
        columns = pl.ds(pl.multiple_of(p * 128, 128), 128)
        v_t = v_ref[:, columns].astype(F32).T * tail
        ones = jnp.broadcast_to(tail, (16, tail.shape[1]))
        for side in range(2):
            head = p * 2 + side
            sel = selectors(table, head, lanes)
            one, two = factors(k_ref[...], sel, table)
            phi = (one * two).astype(BF16)
            lhs = jnp.concatenate([v_t[side * 64 : side * 64 + 64], ones], axis=0)
            own_state[head] = mm(lhs.astype(BF16), phi).astype(BF16)
        return carry

    lax.fori_loop(0, pairs, state_pair, 0)

    chain.begin()
    turn = jnp.minimum(z * CHAIN_STEPS, pairs - 1)

    lane = lax.broadcasted_iota(jnp.int32, (BLK, 128), 1)

    def intra_pair(p, carry):
        at(p, 1, (1, 3), (2, 2))
        at(p, 3, (3, 1))
        at(p, 4, (2, 3))
        at(p, 7, (3, 2))
        chain.middle(p == turn)
        columns = pl.ds(pl.multiple_of(p * 128, 128), 128)
        v_hat = with_ones(v_ref[:, columns])
        heads = [head_lanes(q_ref[...], p * 2 + side) for side in range(2)]
        for i in range(tok // BLK):
            rows = slice(i * BLK, (i + 1) * BLK)
            keys = slice(0, (i + 1) * BLK)
            totals = []
            for side in range(2):
                t = mm(heads[side][rows], k_ref[keys, :], NT) + 4.0
                w = ((t * t + 16.0) * mask_ref[rows, keys]).astype(BF16)
                totals.append(mm(w, v_hat[keys]))
            num_ref[rows, columns] = jnp.where(lane < 64, totals[0][:, :128], totals[1][:, :128])
            den_ref[rows, columns] = jnp.where(lane < 64, totals[0][:, 128:], totals[1][:, 128:])
        return carry

    lax.fori_loop(0, pairs, intra_pair, 0)
    chain.finish(state_ref, table[4:5])
    prior = prior_ref[:, 0:1]
    wide_lane = lax.broadcasted_iota(jnp.int32, (tok, 128), 1)

    def inter_pair(p, carry):
        at(p, 4, (3, 3))
        columns = pl.ds(pl.multiple_of(p * 128, 128), 128)
        totals = []
        for side in range(2):
            head = p * 2 + side
            sel = selectors(table, head, lanes)
            state = state_ref[head]
            z_rows = jnp.broadcast_to(state[64:65].astype(F32), (128, PAD_F)).astype(BF16)
            one, two = factors(q_ref[...], sel, table)
            totals.append(mm((one * two).astype(BF16), placed(state, side, z_rows), NT) * prior)
        num = num_ref[:, columns] + jnp.where(wide_lane < 64, totals[0][:, :128], totals[1][:, :128])
        den = den_ref[:, columns] + jnp.where(wide_lane < 64, totals[0][:, 128:], totals[1][:, 128:])
        inv = 1.0 / den
        inv_ref[:, columns] = inv
        att_ref[:, columns] = (num * inv).astype(BF16)
        return carry

    lax.fori_loop(0, pairs, inter_pair, 0)
    for gather in gathers[1:]:
        gather.stage(4)
    copies.sent(*[("gain", i) for i in range(1, n_sp)])
    chain.drain()


def forward(n_sp, x, gains, docs, table, wo, wg, wu, wd, wq, wk, wv):
    tok, dim = x.shape
    lanes, values = wq.shape[1], wv.shape[1]
    heads = lanes // FEAT
    shard = wq.shape[0]
    vmem, anywhere = pl.BlockSpec(memory_space=pltpu.VMEM), pl.BlockSpec(memory_space=pl.ANY)
    n_z = n_sp // 2
    spans = [3 * CHUNK * (last - first) for first, last in units_of(wd.shape[0])]
    gathered = [2 * lanes + values, dim] + spans[:EARLY]
    sems = len(gathered) * n_copies(n_z) + n_sp + 2
    shape = jax.ShapeDtypeStruct
    result = pl.pallas_call(
        functools.partial(forward_kernel, n_sp),
        out_shape=(
            shape((tok, values), BF16), shape((tok, values), F32), shape((tok, lanes), BF16),
            shape((tok, lanes), BF16), shape((tok, values), BF16), shape((tok, dim), BF16),
            shape((heads, ROWS_S, PAD_F), BF16), shape((8, dim), F32),
        )
        + tuple(shape((shard * n_sp, w), BF16) for w in gathered)
        + tuple(shape((shard, w), BF16) for w in spans[EARLY:]),
        in_specs=[vmem] * 8 + [anywhere] * 3,
        out_specs=(vmem,) * 8 + (anywhere,) * (len(gathered) + len(spans) - EARLY),
        scratch_shapes=[pltpu.VMEM((shard, w), BF16) for w in [2 * lanes + values, dim] + spans]
        + [
            pltpu.VMEM((tok, tok), F32),
            pltpu.VMEM((dim, 2 * lanes + values), BF16),
            pltpu.VMEM((tok, values), F32),
            pltpu.VMEM((tok, values), F32),
            pltpu.VMEM((heads, ROWS_S, PAD_F), BF16),
            pltpu.VMEM((heads, ROWS_S, PAD_F), BF16),
            pltpu.VMEM((heads, ROWS_S, PAD_F), BF16),
            pltpu.VMEM((heads, ROWS_S, PAD_F), BF16),
            pltpu.VMEM((8, dim), F32),
            pltpu.VMEM((n_sp - 1, 8, dim), F32),
            pltpu.VMEM((tok, 128), F32),
            pltpu.SemaphoreType.DMA((sems,)),
            pltpu.SemaphoreType.DMA((sems,)),
            pltpu.SemaphoreType.DMA((8,)),
        ],
        compiler_params=pltpu.CompilerParams(
            collective_id=0, has_side_effects=True, vmem_limit_bytes=60 << 20
        ),
        name="forward",
    )(x, gains, docs, table, wo, wg, wu, wd, wq, wk, wv)
    n = 8 + len(gathered)
    return result[:8], result[8:10], result[10:n], result[n:]


def backward_kernel(
    n_sp, widths, q_ref, k_ref, v_ref, g_ref, att_ref, inv_ref, prior_state_ref, doc_ref, table_ref, *rest,
):
    n_red = len(widths)
    sources, rest = rest[:n_red], rest[n_red:]
    (gq_ref, gk_ref, gv_ref), rest = rest[:3], rest[3:]
    finals, rest = rest[:n_red], rest[n_red:]
    swaps, rest = rest[:n_red], rest[n_red:]
    buffers, rest = [rest[4 * i : 4 * i + 4] for i in range(n_red)], rest[4 * n_red :]
    (
        stage_buf, mask_ref, ghat_ref, gq_acc, gk_acc, own_state, mate_state, in_state, out_state, prior_ref, later_ref,
        send_sem, recv_sem, local_sem,
    ) = rest
    tok, lanes = q_ref.shape
    n_z = n_sp // 2
    pairs = v_ref.shape[1] // 128
    where = place(n_sp)
    dp, sp, g, gy, gx, z, c, across_x, across_y, diagonal, partner = where
    copies = Copies(send_sem, recv_sem)
    reduces = [
        Reduce(
            copies, k, n_z, where, sources[k], swaps[k], buffers[k], finals[k],
            stage_buf.at[:, :, :, :, :, 0 : widths[k]], local_sem,
        )
        for k in range(n_red)
    ]
    docs = Documents(doc_ref, sp)
    even = sp - c
    chain = Chain(
        copies, where, n_z, False, own_state, mate_state, in_state, out_state,
        docs.through(docs.first(even), docs.first(even + 1)), docs.through(docs.first(even + 1), docs.first(even + 2)),
    )
    along = [(dp, lax.rem(z + i, n_z) * 2 + c) for i in range(1, n_z)]
    meet([partner, across_x, across_y, diagonal] + along)
    for reduce in reduces:
        reduce.stage(0)

    def at(p, step, *todo):
        @pl.when(p == step)
        def _():
            for k, n in todo:
                reduces[k].stage(n)

    table = table_ref[...]
    row = lax.broadcasted_iota(jnp.int32, (tok, tok), 0)
    col = lax.broadcasted_iota(jnp.int32, (tok, tok), 1)
    mask_ref[...] = jnp.where((row <= col) & (docs.column == docs.row), 1.0, 0.0)
    prior_ref[...] = jnp.broadcast_to(jnp.where(docs.column == docs.last(sp - 1), 1.0, 0.0), prior_ref.shape)
    later_ref[...] = jnp.broadcast_to(jnp.where(docs.column == docs.first(sp + 1), 1.0, 0.0), later_ref.shape)
    gq_acc[...] = jnp.zeros_like(gq_acc)
    gk_acc[...] = jnp.zeros_like(gk_acc)
    r = lax.broadcasted_iota(jnp.int32, (128, 128), 0)
    c128 = lax.broadcasted_iota(jnp.int32, (128, 128), 1)
    same = jnp.where(r // 64 == c128 // 64, 1.0, 0.0).astype(BF16)
    lane64 = lax.broadcasted_iota(jnp.int32, (tok, 128), 1) % 64
    head_row = jnp.where(docs.row == docs.first(sp), 1.0, 0.0)

    def ghat_pair(p, carry):
        for when, todo in GHAT_SCHEDULE:
            at(p, when, *todo)
        columns = pl.ds(pl.multiple_of(p * 128, 128), 128)
        scaled = g_ref[:, columns].astype(F32) * inv_ref[:, columns]
        product = scaled * att_ref[:, columns].astype(F32)
        high = product.astype(BF16)
        low = (product - high.astype(F32)).astype(BF16)
        dots = -(mm(high, same) + mm(low, same))
        dots_high = dots.astype(BF16)
        dots_low = (dots - dots_high.astype(F32)).astype(BF16)
        extra = jnp.where(lane64 == 0, dots_high, jnp.where(lane64 == 1, dots_low, jnp.zeros_like(dots_low)))
        ghat = jnp.concatenate([scaled.astype(BF16), extra], axis=1)
        ghat_ref[p] = ghat
        ghat_t = ghat.astype(F32).T * head_row
        for side in range(2):
            head = p * 2 + side
            sel = selectors(table, head, lanes)
            one, two = factors(q_ref[...], sel, table)
            phi = (one * two).astype(BF16)
            lhs = jnp.concatenate(
                [ghat_t[side * 64 : side * 64 + 64], ghat_t[128 + side * 64 : 128 + side * 64 + 16]], axis=0
            )
            state = mm(lhs.astype(BF16), phi)
            z_row = jnp.sum(state[64:80], axis=0, keepdims=True)
            own_state[head] = jnp.concatenate(
                [state[0:64], jnp.broadcast_to(z_row, (16, PAD_F))], axis=0
            ).astype(BF16)
        return carry

    lax.fori_loop(0, pairs, ghat_pair, 0)

    chain.begin()
    turn = jnp.minimum((n_z - 1 - z) * CHAIN_BACK_STEPS, 2 * pairs - 1)

    lane = lax.broadcasted_iota(jnp.int32, (tok, 256), 1)
    first_row = lax.broadcasted_iota(jnp.int32, (128, PAD_F), 0)

    def main_pair(p, carry):
        columns = pl.ds(pl.multiple_of(p * 128, 128), 128)
        v_hat = with_ones(v_ref[:, columns])
        gv = [jnp.zeros((BLK, 128), F32) for _ in range(tok // BLK)]
        for side in range(2):
            step = p * 2 + side
            for when, todo in SCHEDULE:
                if when % 2 == side:
                    at(step, when, *todo)
            chain.middle(step == turn)
            head = p * 2 + side
            sel = selectors(table, head, lanes)
            ghat = jnp.where((lane % 128) // 64 == side, ghat_ref[p], jnp.zeros((tok, 256), BF16))
            q_head = head_lanes(q_ref[...], head)
            q_twice = q_head + q_head
            k_twice = head_lanes(k_ref[...], head, 2)
            prior = prior_state_ref[head]
            z_two = jnp.where(first_row // 2 == side * 32, prior[64:65], jnp.zeros((128, PAD_F), BF16))
            rows_p = placed(prior, side, z_two)
            q_one, q_two = factors(q_ref[...], sel, table)
            d_phi = mm(ghat, rows_p) * prior_ref[:, 0:1]
            gq_acc[...] += mm((d_phi * q_two).astype(BF16), sel[0], NT) + mm(
                (d_phi * q_one).astype(BF16), sel[1], NT
            )
            for j in range(tok // BLK):
                rows = slice(j * BLK, (j + 1) * BLK)
                onward = slice(j * BLK, tok)
                t = mm(k_ref[rows, :], q_head[onward], NT) + 4.0
                g_w = mm(v_hat[rows], ghat[onward], NT)
                mask = mask_ref[rows, onward]
                masked_t = t * mask
                w = (masked_t * t + 16.0 * mask).astype(BF16)
                g_s = (g_w * masked_t).astype(BF16)
                gv[j] = gv[j] + mm(w, ghat[onward, 0:128])
                gk_acc[rows, :] += mm(g_s, q_twice[onward])
                gq_acc[onward, :] += mm(g_s, k_twice[rows], TN)
        for j in range(tok // BLK):
            rows = slice(j * BLK, (j + 1) * BLK)
            gv_ref[rows, columns] = gv[j].astype(BF16)
        return carry

    lax.fori_loop(0, pairs, main_pair, 0)
    chain.drain()
    chain.finish(out_state, table[4:5])

    def later_pair(p, carry):
        for when, todo in LATE_SCHEDULE:
            at(p, when, *todo)
        columns = pl.ds(pl.multiple_of(p * 128, 128), 128)
        v_hat = with_ones(v_ref[:, columns])
        gv_inter = None
        for side in range(2):
            head = p * 2 + side
            sel = selectors(table, head, lanes)
            later = out_state[head]
            z_one = jnp.where(first_row == 0, later[64:65], jnp.zeros((128, PAD_F), BF16))
            rows_n = placed(later, side, z_one)
            k_one, k_two = factors(k_ref[...], sel, table)
            phi_k = (k_one * k_two).astype(BF16)
            gvi = mm(phi_k, rows_n[0:128], NT)
            gv_inter = gvi if gv_inter is None else gv_inter + gvi
            d_phi = mm(v_hat, rows_n) * later_ref[:, 0:1]
            gk_acc[...] += mm((d_phi * k_two).astype(BF16), sel[0], NT) + mm(
                (d_phi * k_one).astype(BF16), sel[1], NT
            )
        gv_ref[:, columns] = (gv_ref[:, columns].astype(F32) + gv_inter * later_ref[...]).astype(BF16)
        return carry

    lax.fori_loop(0, pairs, later_pair, 0)
    gq_ref[...] = gq_acc[...].astype(BF16)
    gk_ref[...] = gk_acc[...].astype(BF16)
    for k, n in LAST_SCHEDULE:
        reduces[k].stage(n)


GHAT_SCHEDULE = ((1, ((0, 1),)), (3, ((1, 1),)), (4, ((0, 2),)), (6, ((2, 1),)), (7, ((1, 2),)), )
SCHEDULE = ((1, ((0, 3),)), (2, ((3, 1),)), (4, ((2, 2),)), (6, ((1, 3),)), (7, ((0, 4),)), (9, ((3, 2),)), (10, ((2, 3),)), (12, ((1, 4),)), (14, ((0, 5),)), (15, ((3, 3),)), )
LATE_SCHEDULE = ((1, ((2, 4),)), (2, ((1, 5),)), (4, ((3, 4),)), (5, ((2, 5),)), (7, ((3, 5),)), )
LAST_SCHEDULE = ()


def shards_of(parts):
    return [part.reshape(-1, part.shape[-1]) for part in parts]


def backward(n_sp, arrays, grads):
    q, v = arrays[0], arrays[2]
    tok, lanes = q.shape
    heads = lanes // FEAT
    n_z = n_sp // 2
    rows = grads[0].shape[4]
    widths = tuple(grad.shape[5] for grad in grads)
    n_red = len(grads)
    vmem, anywhere = pl.BlockSpec(memory_space=pltpu.VMEM), pl.BlockSpec(memory_space=pl.ANY)
    shape = jax.ShapeDtypeStruct
    sems = n_red * n_reduce(n_z) + 3
    result = pl.pallas_call(
        functools.partial(backward_kernel, n_sp, widths),
        out_shape=(shape(q.shape, BF16), shape(q.shape, BF16), shape(v.shape, BF16))
        + tuple(shape((2, 2, rows, w), BF16) for w in widths)
        + tuple(shape((n_z, 2, 2, rows, w), BF16) for w in widths),
        in_specs=[vmem] * len(arrays) + [anywhere] * n_red,
        out_specs=(vmem,) * (3 + n_red) + (anywhere,) * n_red,
        scratch_shapes=sum([reduce_scratch(n_z, rows, w) for w in widths], [])
        + [
            pltpu.VMEM((2, 2, 2, 2, rows, max(widths)), BF16),
            pltpu.VMEM((tok, tok), F32),
            pltpu.VMEM((heads // 2, tok, 256), BF16),
            pltpu.VMEM(q.shape, F32),
            pltpu.VMEM(q.shape, F32),
            pltpu.VMEM((heads, ROWS_S, PAD_F), BF16),
            pltpu.VMEM((heads, ROWS_S, PAD_F), BF16),
            pltpu.VMEM((heads, ROWS_S, PAD_F), BF16),
            pltpu.VMEM((heads, ROWS_S, PAD_F), BF16),
            pltpu.VMEM((tok, 128), F32),
            pltpu.VMEM((tok, 128), F32),
            pltpu.SemaphoreType.DMA((sems,)),
            pltpu.SemaphoreType.DMA((sems,)),
            pltpu.SemaphoreType.DMA((2, 2)),
        ],
        compiler_params=pltpu.CompilerParams(
            collective_id=1, has_side_effects=True, vmem_limit_bytes=63 << 20
        ),
        name="backward",
    )(*arrays, *grads)
    return result[:3], shards_of(result[3 : 3 + n_red])


def reduce_units(chunks):
    edges = [0, 2, 4, 6, 8, chunks]
    return list(zip(edges[:-1], edges[1:]))


IN_FFN = 2
FFN_SCHEDULE = {
    1: (("g", 0, 1), ("g", 1, 0)),
    3: (("g", 0, 2), ("r", 0, 0)),
    4: (("g", 1, 1), ("g", 0, 3), ("r", 0, 1)),
    5: (("g", 0, 4), ("r", 1, 0)),
    6: (("g", 1, 2), ("r", 0, 2), ("r", 1, 1)),
    7: (("g", 1, 3),),
    8: (("g", 1, 4), ("r", 0, 3), ("r", 1, 2)),
    9: (("r", 1, 3),),
    10: (("r", 0, 4),),
}
FFN_LATE = (("r", 1, 4),)
FFN_LAST = (("r", 0, 5), ("r", 1, 5))


def ffn_kernel(n_sp, gather_units, chunks, x_ref, att_ref, out_w_ref, gain_ref, cot_ref, *rest):
    n_unit = len(gather_units)
    sums = reduce_units(chunks)
    n_sum = len(sums)
    early, rest = rest[:EARLY], rest[EARLY:]
    kept, rest = rest[: n_unit - EARLY], rest[n_unit - EARLY :]
    ggain_ref, rest = rest[0], rest[1:]
    finals, rest = rest[:IN_FFN], rest[IN_FFN:]
    (output_ref, gh_ref, gatt_ref, gout_ref), rest = rest[:4], rest[4:]
    grads, rest = rest[:n_sum], rest[n_sum:]
    swaps, rest = rest[:IN_FFN], rest[IN_FFN:]
    late, rest = rest[: n_unit - EARLY], rest[n_unit - EARLY :]
    buffers, rest = [rest[4 * i : 4 * i + 4] for i in range(IN_FFN)], rest[4 * IN_FFN :]
    (
        stage_buf, hid, n2, n2_t, cot_t, acc_o, acc_n, gout, w_buf, g_buf, send_sem, recv_sem, local_sem, w_sem, g_sem,
        o_sem,
    ) = rest
    tok, dim = x_ref.shape
    n_z = n_sp // 2
    where = place(n_sp)
    dp, sp, g, gy, gx, z, c, across_x, across_y, diagonal, partner = where
    copies = Copies(send_sem, recv_sem)
    gathers = [Gather(copies, ("g", k), n_z, own, full, where) for k, (own, full) in enumerate(zip(kept, late))]
    reduces = [
        Reduce(
            copies, ("r", k), n_z, where, grads[k], swaps[k], buffers[k], finals[k],
            stage_buf.at[:, :, :, :, :, 0 : grads[k].shape[-1]], local_sem,
        )
        for k in range(IN_FFN)
    ]
    along = [(dp, lax.rem(z + i, n_z) * 2 + c) for i in range(1, n_z)]
    meet([partner, across_x, across_y, diagonal] + along)
    gathers[0].stage(0)
    own_copies = [
        pltpu.make_async_copy(own, gather.own_place, o_sem.at[k])
        for k, (own, gather) in enumerate(zip(kept, gathers))
    ]
    for copy in own_copies:
        copy.start()

    def run(todo):
        for kind, k, n in todo:
            (gathers if kind == "g" else reduces)[k].stage(n)

    fulls = list(early) + list(late)

    def load(chunk, slot, do_wait=False):
        if do_wait:
            for i in range(3):
                pltpu.make_async_copy(fulls[0].at[:, 0:CHUNK], w_buf.at[slot, i], w_sem.at[slot, i]).wait()
            return
        for full, (first, last) in zip(fulls, gather_units):
            @pl.when((chunk >= first) & (chunk < last))
            def _():
                for i in range(3):
                    lane = pl.multiple_of((chunk - first + i * (last - first)) * CHUNK, CHUNK)
                    pltpu.make_async_copy(full.at[:, pl.ds(lane, CHUNK)], w_buf.at[slot, i], w_sem.at[slot, i]).start()

    def save(chunk, slot, do_wait=False):
        if do_wait:
            for i in range(3):
                pltpu.make_async_copy(
                    g_buf.at[slot, i], grads[0].at[:, :, :, :, :, 0:CHUNK], g_sem.at[slot, i]
                ).wait()
            return
        for grad, (first, last) in zip(grads, sums):
            @pl.when((chunk >= first) & (chunk < last))
            def _():
                for i in range(3):
                    lane = pl.multiple_of((chunk - first + i * (last - first)) * CHUNK, CHUNK)
                    pltpu.make_async_copy(
                        g_buf.at[slot, i], grad.at[:, :, :, :, :, pl.ds(lane, CHUNK)], g_sem.at[slot, i]
                    ).start()

    load(0, 0)
    gain = gain_ref[1:2]
    for i in range(tok // BLK):
        rows = slice(i * BLK, (i + 1) * BLK)
        hidden = x_ref[rows, :].astype(F32) + mm(att_ref[rows, :], out_w_ref[...], NT)
        hid[rows, :] = hidden
        scale = lax.rsqrt(jnp.mean(hidden * hidden, axis=1, keepdims=True) + EPSILON)
        normed = (hidden * scale * gain).astype(BF16)
        n2[rows, :] = normed
        n2_t[:, rows] = normed.T
        cot_t[:, rows] = cot_ref[rows, :].T
    acc_o[...] = jnp.zeros_like(acc_o)
    acc_n[...] = jnp.zeros_like(acc_n)
    for copy in own_copies:
        copy.wait()
    grad_shape = g_buf.shape[2:]

    def step(chunk, carry):
        slot = lax.rem(chunk, 2)
        load(chunk, slot, True)

        @pl.when(chunk >= 2)
        def _():
            save(chunk, slot, True)

        for when, todo in FFN_SCHEDULE.items():
            @pl.when(chunk == when)
            def _():
                run(todo)

        @pl.when(chunk + 1 < chunks)
        def _():
            load(chunk + 1, 1 - slot)

        wg, wu, wd = w_buf[slot, 0], w_buf[slot, 1], w_buf[slot, 2]
        gate = mm(n2[...], wg)
        up = mm(n2[...], wu)
        g_mixed = mm(cot_ref[...], wd)
        sig = 1.0 / (1.0 + jnp.exp(-gate))
        act = gate * sig
        mixed = (act * up).astype(BF16)
        g_gate = (g_mixed * up * sig * (1.0 + gate * (1.0 - sig))).astype(BF16)
        g_up = (g_mixed * act).astype(BF16)
        g_buf[slot, 0] = mm(n2_t[...], g_gate).astype(BF16).reshape(grad_shape)
        g_buf[slot, 1] = mm(n2_t[...], g_up).astype(BF16).reshape(grad_shape)
        g_buf[slot, 2] = mm(cot_t[...], mixed).astype(BF16).reshape(grad_shape)
        save(chunk, slot)
        acc_o[...] += mm(mixed, wd, NT)
        acc_n[...] += mm(g_gate, wg, NT) + mm(g_up, wu, NT)
        return carry

    lax.fori_loop(0, chunks, step, 0)
    run(FFN_LATE)
    total = jnp.zeros((1, dim), F32)
    for i in range(tok // BLK):
        rows = slice(i * BLK, (i + 1) * BLK)
        hidden = hid[rows, :]
        n2[rows, :] = (hidden + acc_o[rows, :]).astype(BF16)
        scale = lax.rsqrt(jnp.mean(hidden * hidden, axis=1, keepdims=True) + EPSILON)
        e = acc_n[rows, :]
        total = total + jnp.sum(e * hidden * scale, axis=0, keepdims=True)
        eg = e * gain
        inner = jnp.mean(eg * hidden, axis=1, keepdims=True)
        gh = cot_ref[rows, :].astype(F32) + scale * eg - hidden * (scale * scale * scale * inner)
        acc_o[rows, :] = gh
        n2_t[rows, :] = gh.astype(BF16)
        cot_t[rows, :] = mm(n2_t[rows, :], out_w_ref[...]).astype(BF16)
    ggain_ref[...] = jnp.broadcast_to(total, ggain_ref.shape)
    outs = [
        pltpu.make_async_copy(n2, output_ref, o_sem.at[0]),
        pltpu.make_async_copy(acc_o, gh_ref, o_sem.at[1]),
        pltpu.make_async_copy(cot_t, gatt_ref, o_sem.at[2]),
    ]
    for copy in outs:
        copy.start()
    for first in range(0, att_ref.shape[1], CHUNK):
        columns = slice(first, first + CHUNK)
        gout[:, :, :, :, :, columns] = (
            mm(n2_t[...], att_ref[:, columns], TN).astype(BF16).reshape(grad_shape)
        )
    outs.append(pltpu.make_async_copy(gout, gout_ref, o_sem.at[3]))
    outs[3].start()
    save(chunks - 2, (chunks - 2) % 2, True)
    save(chunks - 1, (chunks - 1) % 2, True)
    run(FFN_LAST)
    for copy in outs:
        copy.wait()


def ffn(n_sp, x, att, out_w, gain, cot, width, early, kept):
    tok, dim = x.shape
    values = att.shape[1]
    n_z = n_sp // 2
    chunks = -(-width // CHUNK)
    gather_units = units_of(width)
    sums = reduce_units(chunks)
    rows = dim // n_sp // GROUP
    spans = [3 * CHUNK * (last - first) for first, last in sums]
    vmem, anywhere = pl.BlockSpec(memory_space=pltpu.VMEM), pl.BlockSpec(memory_space=pl.ANY)
    shape = jax.ShapeDtypeStruct
    split = lambda w: shape((n_z, 2, 2, 2, rows, w), BF16)
    sems = len(kept) * n_copies(n_z) + IN_FFN * n_reduce(n_z)
    full_shapes = tuple(shape((k.shape[0] * n_sp, k.shape[1]), BF16) for k in kept)
    result = pl.pallas_call(
        functools.partial(ffn_kernel, n_sp, gather_units, chunks),
        out_shape=(shape((8, dim), F32),)
        + tuple(shape((2, 2, rows, w), BF16) for w in spans[:IN_FFN])
        + (shape((tok, dim), BF16), shape((tok, dim), F32), shape((tok, values), BF16), split(values))
        + tuple(split(w) for w in spans)
        + tuple(shape((n_z, 2, 2, rows, w), BF16) for w in spans[:IN_FFN])
        + full_shapes,
        in_specs=[vmem] * 5 + [anywhere] * len(early) + [vmem] * len(kept),
        out_specs=(vmem,) * (1 + IN_FFN) + (anywhere,) * (4 + len(spans) + IN_FFN + len(kept)),
        scratch_shapes=sum([reduce_scratch(n_z, rows, w) for w in spans[:IN_FFN]], [])
        + [
            pltpu.VMEM((2, 2, 2, 2, rows, max(spans[:IN_FFN])), BF16),
            pltpu.VMEM((tok, dim), F32),
            pltpu.VMEM((tok, dim), BF16),
            pltpu.VMEM((dim, tok), BF16),
            pltpu.VMEM((dim, tok), BF16),
            pltpu.VMEM((tok, dim), F32),
            pltpu.VMEM((tok, dim), F32),
            pltpu.VMEM((n_z, 2, 2, 2, rows, values), BF16),
            pltpu.VMEM((2, 3, dim, CHUNK), BF16),
            pltpu.VMEM((2, 3, n_z, 2, 2, 2, rows, CHUNK), BF16),
            pltpu.SemaphoreType.DMA((sems,)),
            pltpu.SemaphoreType.DMA((sems,)),
            pltpu.SemaphoreType.DMA((2, 2)),
            pltpu.SemaphoreType.DMA((2, 3)),
            pltpu.SemaphoreType.DMA((2, 3)),
            pltpu.SemaphoreType.DMA((4,)),
        ],
        compiler_params=pltpu.CompilerParams(
            collective_id=2, has_side_effects=True, vmem_limit_bytes=63 << 20
        ),
        name="ffn",
    )(x, att, out_w, gain, cot, *early, *kept)
    n = 1 + IN_FFN
    shards = shards_of(result[1:n])
    output, g_hidden, g_att, g_out = result[n : n + 4]
    grads = result[n + 4 + IN_FFN : n + 4 + len(spans)]
    return output, g_hidden, g_att, result[0], g_out, shards, grads


def tail_kernel(
    n_sp, normed_ref, gq_ref, gk_ref, gv_ref, w_ref, x_ref, gh_ref, gain_ref, ggain_ref,
    gin_ref, gains_ref, final_v, final_qk,
    src_v, src_qk, swap_v, swap_qk, *rest,
):
    buffers, rest = (rest[:4], rest[4:8]), rest[8:]
    own_gains, sum_gains, in_sp, in_dp, send_sem, recv_sem = rest
    tok, dim = x_ref.shape
    n_z = n_sp // 2
    lanes = gq_ref.shape[1]
    where = place(n_sp)
    dp, sp, g, gy, gx, z, c, across_x, across_y, diagonal, partner = where
    copies = Copies(send_sem, recv_sem)
    first = Reduce(copies, "v", n_z, where, src_v, swap_v, buffers[0], final_v)
    second = Reduce(copies, "qk", n_z, where, src_qk, swap_qk, buffers[1], final_qk)
    others = [(dp, lax.rem(sp + i, n_sp)) for i in range(1, n_sp)]
    groups = [across_x, across_y, diagonal]
    for i, device in enumerate(others):
        copies.add(("sp", i), own_gains, in_sp.at[i], device)
    for i, device in enumerate(groups):
        copies.add(("dp", i), sum_gains, in_dp.at[i], device)
    meet(others + groups)
    block = src_v.shape[:-1] + (BLK,)
    for i in range(0, gv_ref.shape[1], BLK):
        columns = slice(i, i + BLK)
        src_v[:, :, :, :, :, columns] = mm(normed_ref[...], gv_ref[:, columns], TN).astype(BF16).reshape(block)
    for i, ref in enumerate((gq_ref, gk_ref)):
        for j in range(0, lanes, BLK):
            src_qk[:, :, :, :, :, i * lanes + j : i * lanes + j + BLK] = (
                mm(normed_ref[...], ref[:, j : j + BLK], TN).astype(BF16).reshape(block)
            )
        if i == 0:
            first.stage(0)
    todo = [[(second, 0), (first, 1)], [(second, 1)], [(first, 2)], [(second, 2)]]
    total = jnp.zeros((1, dim), F32)
    gain = gain_ref[0:1]
    for i in range(tok // BLK):
        rows = slice(i * BLK, (i + 1) * BLK)
        e = (
            mm(gq_ref[rows, :], w_ref[:, 0:lanes], NT)
            + mm(gk_ref[rows, :], w_ref[:, lanes : 2 * lanes], NT)
            + mm(gv_ref[rows, :], w_ref[:, 2 * lanes :], NT)
        )
        u = x_ref[rows, :].astype(F32)
        scale = lax.rsqrt(jnp.mean(u * u, axis=1, keepdims=True) + EPSILON)
        total = total + jnp.sum(e * u * scale, axis=0, keepdims=True)
        eg = e * gain
        inner = jnp.mean(eg * u, axis=1, keepdims=True)
        gin_ref[rows, :] = gh_ref[rows, :] + scale * eg - u * (scale * scale * scale * inner)
        for reduce, n in todo[i] if i < len(todo) else ():
            reduce.stage(n)
    for i in range(tok // BLK, len(todo)):
        for reduce, n in todo[i]:
            reduce.stage(n)
    row = lax.broadcasted_iota(jnp.int32, own_gains.shape, 0)
    own_gains[...] = jnp.where(row == 0, jnp.broadcast_to(total, own_gains.shape), ggain_ref[...])
    first.stage(3)
    copies.start(*[("sp", i) for i in range(n_sp - 1)])
    second.stage(3)
    copies.arrived(*[("sp", i) for i in range(n_sp - 1)])
    sum_gains[...] = own_gains[...] + rows_sum([in_sp[i] for i in range(n_sp - 1)])
    first.stage(4)
    copies.start(*[("dp", i) for i in range(3)])
    second.stage(4)
    copies.arrived(*[("dp", i) for i in range(3)])
    gains_ref[...] = sum_gains[...] + rows_sum([in_dp[i] for i in range(3)])
    first.stage(5)
    second.stage(5)
    copies.sent(*[("sp", i) for i in range(n_sp - 1)], *[("dp", i) for i in range(3)])


def tail(n_sp, normed, gq, gk, gv, w_joint, x, g_hidden, gain, ggain):
    tok, dim = x.shape
    lanes, values = gq.shape[1], gv.shape[1]
    n_z = n_sp // 2
    rows = dim // n_sp // GROUP
    vmem = pl.BlockSpec(memory_space=pltpu.VMEM)
    shape = jax.ShapeDtypeStruct
    widths = (values, 2 * lanes)
    sems = 2 * n_reduce(n_z) + n_sp + 2
    return pl.pallas_call(
        functools.partial(tail_kernel, n_sp),
        out_shape=(shape((tok, dim), F32), shape((8, dim), F32))
        + tuple(shape((2, 2, rows, w), BF16) for w in widths),
        in_specs=[vmem] * 9,
        out_specs=(vmem,) * 4,
        scratch_shapes=[pltpu.VMEM((n_z, 2, 2, 2, rows, w), BF16) for w in widths]
        + [pltpu.VMEM((n_z, 2, 2, rows, w), BF16) for w in widths]
        + sum([reduce_scratch(n_z, rows, w) for w in widths], [])
        + [
            pltpu.VMEM((8, dim), F32),
            pltpu.VMEM((8, dim), F32),
            pltpu.VMEM((n_sp - 1, 8, dim), F32),
            pltpu.VMEM((3, 8, dim), F32),
            pltpu.SemaphoreType.DMA((sems,)),
            pltpu.SemaphoreType.DMA((sems,)),
        ],
        compiler_params=pltpu.CompilerParams(
            collective_id=3, has_side_effects=True, vmem_limit_bytes=60 << 20
        ),
        name="tail",
    )(normed, gq, gk, gv, w_joint, x, g_hidden, gain, ggain)


def finish_kernel(sums, *refs):
    n = len(sums) + 3
    sources, refs = refs[:n], refs[n:]
    (q_out, k_out, v_out, out_out, gate_out, up_out, down_out), refs = refs[:7], refs[7:]
    held, sem = refs[:n], refs[n]
    copies = [pltpu.make_async_copy(src, dst, sem.at[i]) for i, (src, dst) in enumerate(zip(sources, held))]
    for copy in copies:
        copy.start()
    for copy in copies:
        copy.wait()
    qk_ref, v_ref, out_ref, units = held[0], held[1], held[2], held[3:]
    lanes = q_out.shape[1]
    width = gate_out.shape[0]
    q_out[...] = qk_ref[:, :lanes].astype(F32)
    k_out[...] = qk_ref[:, lanes:].astype(F32)
    v_out[...] = v_ref[...].astype(F32)
    out_out[...] = out_ref[...].astype(F32).T
    for unit, (first, last) in zip(units, sums):
        lo, hi = first * CHUNK, min(last * CHUNK, width)
        span = (last - first) * CHUNK
        for i, out in enumerate((gate_out, up_out, down_out)):
            out[lo:hi, :] = unit[:, i * span : i * span + hi - lo].astype(F32).T


def finish(width, lanes, qk, v, out, units):
    shard = v.shape[0]
    vmem, anywhere = pl.BlockSpec(memory_space=pltpu.VMEM), pl.BlockSpec(memory_space=pl.ANY)
    shape = jax.ShapeDtypeStruct
    arrays = (qk, v, out, *units)
    return pl.pallas_call(
        functools.partial(finish_kernel, reduce_units(-(-width // CHUNK))),
        out_shape=(
            shape((shard, lanes), F32), shape((shard, lanes), F32), shape(v.shape, F32),
            shape(out.shape[::-1], F32), shape((width, shard), F32), shape((width, shard), F32),
            shape((width, shard), F32),
        ),
        in_specs=[anywhere] * len(arrays),
        out_specs=(vmem,) * 7,
        scratch_shapes=[pltpu.VMEM(a.shape, BF16) for a in arrays] + [pltpu.SemaphoreType.DMA((len(arrays),))],
        compiler_params=pltpu.CompilerParams(vmem_limit_bytes=63 << 20),
        name="finish",
    )(*arrays)


def body(
    tokens, doc_ids, gain_attn, w_query, w_key, w_value, w_out, gain_mlp, w_gate, w_up, w_down, cotangent
):
    n_sp = lax.axis_size("sp")
    me = lax.axis_index("sp")
    tok = tokens.shape[0]
    heads = w_query.shape[1] // FEAT
    table = feature_table()
    docs = doc_ids.reshape(n_sp, tok)
    width = gain_attn.shape[0]
    lanes = heads * FEAT
    hidden_units = w_gate.shape[1]
    gain_parts = jnp.tile(jnp.stack([gain_attn, gain_mlp] + [gain_mlp] * 6).astype(F32), (1, n_sp))
    (
        (att, inv, q, k, v, normed_one, prior_state, gain), (w_joint, out_t), early, kept
    ) = forward(
        n_sp, tokens, gain_parts, docs, table, w_out, w_gate.T, w_up.T, w_down, w_query, w_key, w_value
    )
    output, g_hidden, g_att, grad_gain_two, g_out, shards, grads = ffn(
        n_sp, tokens, att, out_t, gain, cotangent, hidden_units, early, kept
    )
    (gq, gk, gv), (s_out, *more) = backward(
        n_sp, (q, k, v, g_att, att, inv, prior_state, docs, table), (g_out, *grads)
    )
    grad_input, grad_gains, *joint = tail(
        n_sp, normed_one, gq, gk, gv, w_joint, tokens, g_hidden, gain, grad_gain_two
    )
    n_dp = lax.axis_size("dp")

    def over_groups(shard):
        if n_dp > GROUP:
            shard = lax.psum(shard, "dp") * jnp.asarray(GROUP / n_dp, shard.dtype)
        return shard

    s_value, s_query_key = shards_of(joint)
    g_query, g_key, g_value, g_w_out, g_gate, g_up, g_down = finish(
        hidden_units, lanes, over_groups(s_query_key), over_groups(s_value), over_groups(s_out),
        [over_groups(shard) for shard in (*shards, *more)],
    )
    s_gains = over_groups(lax.dynamic_slice(grad_gains, (0, me * width), (2, width)))
    return (
        output, grad_input, s_gains[0], g_query, g_key, g_value, g_w_out, s_gains[1], g_gate.T, g_up.T, g_down
    )


def solution(mesh):
    placed_in = (
        P(("dp", "sp"), None), P("dp", None), P("sp"), P("sp", None), P("sp", None), P("sp", None),
        P(None, "sp"), P("sp"), P("sp", None), P("sp", None), P(None, "sp"), P(("dp", "sp"), None),
    )
    return jax.shard_map(
        body,
        mesh=mesh,
        in_specs=placed_in,
        out_specs=(
            P(("dp", "sp"), None), P(("dp", "sp"), None), P("sp"), P("sp", None), P("sp", None),
            P("sp", None), P(None, "sp"), P("sp"), P("sp", None), P("sp", None), P(None, "sp"),
        ),
        check_vma=False,
    )
```

time: 733 us -> 386 us (0.53)
  waiting for transfers between devices: 300 us -> 0 us
  Pallas kernels: 308 us -> 368 us
  matrix products: 31.2 us -> 0 us
  blocking collectives: 25 us -> 0 us
  local copies, waits for them, and re-layouts: 26.7 us -> 9.15 us
  between operations: 17.2 us -> 0.88 us
  other arithmetic: 15.4 us -> 1.48 us
    reduce_scatter x5 -> x0, waiting for transfers between devices: 193 us -> none  [reduced(): lax.psum_scatter(grad.astype(BF16), 'sp', scatter_dimension=0, tiled=True)]
    pallas_call x3 -> x4, Pallas kernels: 152 us -> 274 us  [the longest x1 110 us: backward(): pl.pallas_call(functools.partial(backward_kernel, n_sp, widths), out_shap...]
    pallas_call x1, Pallas kernels: 156 us -> 93.3 us  [forward(): pl.pallas_call(functools.partial(forward_kernel, n_sp), out_shape=(shape(...]
    all_gather x1 -> x0, waiting for transfers between devices: 62.5 us -> none  [combine(): every = lax.all_gather(state, 'sp', axis=0, tiled=False).astype(F32)]
    psum x1 -> x0, waiting for transfers between devices: 42.4 us -> none  [reduced(): return lax.psum(part, 'dp').astype(F32)]
    dot_general x5 -> x0, matrix products: 31.2 us -> none  [the longest x4 25.3 us: mm(): return lax.dot_general(a, b, dims, preferred_element_type=F32)]
    unnamed x1 -> x0, blocking collectives: 15 us -> none
    unnamed x59 -> x5, local copies, waits for them, and re-layouts: 18.3 us -> 5.77 us
  transfers between devices with their start and end apart: 7 -> 0, of which waited for: 6 -> 0; matrix products, arithmetic and copies ran while one was open for 5% -> 0% of each run, Pallas kernels for 9% -> 0%
where the time goes in v3:
time: 386 us; the launch traced here: 379 us
  Pallas kernels  368 us (95%)
  local copies, waits for them, and re-layouts  9.15 us (2%)
    pallas_call x1, Pallas kernels, backward(): pl.pallas_call(functools.partial(backward_kernel, n_sp, widths), out_shap...  110 us
    pallas_call x1, Pallas kernels, ffn(): pl.pallas_call(functools.partial(ffn_kernel, n_sp, gather_units, chunks),...  107 us
    pallas_call x1, Pallas kernels, forward(): pl.pallas_call(functools.partial(forward_kernel, n_sp), out_shape=(shape(...  93.3 us
    pallas_call x1, Pallas kernels, tail(): pl.pallas_call(functools.partial(tail_kernel, n_sp), out_shape=(shape((to...  53 us

profile of v3, /device:TPU:0, one launch (start us, length us, event | category | flops | bytes accessed | tf_op | source)
XLA Modules:
  0.0 379.1 jit_solution(4713235761386661819)
XLA Ops:
  0.6 0.5 broadcast.5
  1.2 1.5 reduce.3
  2.6 0.6 reshape.117.doc_ref
  3.3 0.9 stack.8
  4.2 0.6 broadcast_bitcast_fusion.gain_parts_ref
  4.8 93.3 %forward.1 = (bf16[1024,1024]{1,0:T(8,128)(2,1)}, f32[1024,1024]{1,0:T(8,128)}, bf16[1024,256]{1,0:T(8,128)(2,1)}, bf16[1024,256]{1,0:T(8,128)(2,1)}, bf16[1024,...) custom-call(bf16[1024,1024]{1,0:T(8,128)(2,1)} %x_ref.5, ...), custom_call_target="tpu_custom_call" | custom-call | tf_op jit(solution)/shard_map/forward/pallas_call | solution.py:626
  98.2 107.0 %ffn.1 = (f32[8,1024]{1,0:T(8,128)}, bf16[2,2,32,1536]{3,2,1,0:T(8,128)(2,1)}, bf16[2,2,32,1536]{3,2,1,0:T(8,128)(2,1)}, bf16[1024,1024]{1,0:T(8,128)(2,1)}, f32...) custom-call(bf16[1024,1024]{1,0:T(8,128)(2,1)} %x_ref.5, ...), custom_call_target="tpu_custom_call" | custom-call | tf_op jit(solution)/shard_map/ffn/pallas_call | solution.py:1084
  205.1 109.5 %backward.1 = (bf16[1024,256]{1,0:T(8,128)(2,1)}, bf16[1024,256]{1,0:T(8,128)(2,1)}, bf16[1024,1024]{1,0:T(8,128)(2,1)}, bf16[2,2,32,1024]{3,2,1,0:T(8,128)(2,1)...) custom-call(bf16[1024,256]{1,0:T(8,128)(2,1)} %get-tuple-element.62., ...), custom_call_target="tpu_custom_call" | custom-call | tf_op jit(solution)/shard_map/backward/pallas_call | solution.py:854
  314.7 53.0 %tail.1 = (f32[1024,1024]{1,0:T(8,128)}, f32[8,1024]{1,0:T(8,128)}, bf16[2,2,32,1024]{3,2,1,0:T(8,128)(2,1)}, bf16[2,2,32,512]{3,2,1,0:T(8,128)(2,1)}) custom-call(bf16[1024,1024]{1,0:T(8,128)(2,1)} %get-tuple-element.61.normed_ref, bf16[1024,256]{1,0:T(8,128)(2,1)} %get-tuple-element.72.gq_ref, bf16[1024,256]{1,0:T(8,128)(2,1)} %get-tuple-element.73.gk_ref, ...), custom_call_target="tpu_custom_call" | custom-call | tf_op jit(solution)/shard_map/tail/pallas_call | solution.py:1205
  367.7 4.7 %finish.1 = (f32[128,256]{1,0:T(8,128)}, f32[128,256]{1,0:T(8,128)}, f32[128,1024]{1,0:T(8,128)}, f32[1024,128]{1,0:T(8,128)}, f32[2752,128]{1,0:T(8,128)}, /*index=5*/f32[2752,128]{1,0:T(8,128)}, f32[2752,128]{1,0:T(8,128)}) custom-call(bf16[128,512]{1,0:T(8,128)(2,1)} %bitcast.29, bf16[128,1024]{1,0:T(8,128)(2,1)} %bitcast.28, bf16[128,1024]{1,0:T(8,128)(2,1)} %bitcast.27, ...), custom_call_target="tpu_custom_call" | custom-call | tf_op jit(solution)/shard_map/finish/pallas_call | solution.py:1258
  372.4 0.7 constant_dynamic-slice_fusion
  373.1 0.5 slice_bitcast_fusion
  373.6 0.0 copy-start
  373.6 3.2 copy.26
  376.9 0.0 copy-done
  376.9 2.0 copy.27
  (1 shorter events, 0.0 us)
Async XLA Ops:
  373.6 3.2 copy-start

commit v4 on v3

--- a/solution.py
+++ b/solution.py
@@ -309,6 +309,28 @@
     return 8 + n_z - 1
 
 
+TAIL_LANES = 32
+PER_TILE = 128 // TAIL_LANES
+
+
+def packed_shape(heads):
+    return (heads + heads // PER_TILE, ROWS_S, 128)
+
+
+def pack(ref, heads, p, side, state):
+    head = p * 2 + side
+    block = heads + head // PER_TILE
+    ref[head] = state[:, :128].astype(BF16)
+    rest = state[:, 128:]
+    first, second = [pltpu.roll(rest, TAIL_LANES * (side + 2 * half), 1) if side + 2 * half else rest for half in range(2)]
+    moved = jnp.where(lax.rem(p, 2) == 0, first, second).astype(BF16)
+    if side == 0:
+        held = jnp.where(lax.rem(p, 2) == 0, jnp.zeros_like(moved), ref[block])
+        ref[block] = held + moved
+    else:
+        ref[block] = ref[block] + moved
+
+
 class Chain:
     def __init__(self, copies, where, n_z, onward, own, mate, carry, out, pass_lead, pass_other):
         dp, sp, g, gy, gx, z, c, across_x, across_y, diagonal, partner = where
@@ -360,24 +382,29 @@
             self.copies.start("carry")
 
     def finish(self, result, weights):
+        heads = result.shape[0]
+
+        def unpack(value):
+            def group(q, carry):
+                rest = value(heads + q)
+                for j in range(PER_TILE):
+                    head = q * PER_TILE + j
+                    tail = pltpu.roll(rest, 128 - TAIL_LANES * j, 1) if j else rest
+                    result[head] = jnp.concatenate(
+                        [value(head) * weights[:, :128], tail * weights[:, 128:]], axis=1
+                    ).astype(BF16)
+                return carry
+
+            lax.fori_loop(0, heads // PER_TILE, group, 0)
+
         @pl.when(jnp.logical_not(self.leads))
         def _():
             self.copies.arrived("raw")
-
-            def one(head, carry):
-                result[head] = (self.carry[head].astype(F32) * weights).astype(BF16)
-                return carry
-
-            lax.fori_loop(0, self.own.shape[0], one, 0)
+            unpack(lambda i: self.carry[i].astype(F32))
 
         @pl.when(self.leads)
         def _():
-            def one(head, carry):
-                total = self.mate[head].astype(F32) + self.pass_other * self.carry[head].astype(F32)
-                result[head] = (total * weights).astype(BF16)
-                return carry
-
-            lax.fori_loop(0, self.own.shape[0], one, 0)
+            unpack(lambda i: self.mate[i].astype(F32) + self.pass_other * self.carry[i].astype(F32))
 
     def drain(self):
         @pl.when(jnp.logical_not(self.leads))
@@ -394,13 +421,13 @@
 
 
 class Documents:
-    def __init__(self, doc_ref, sp):
-        self.ref, self.n_sp, self.tok = doc_ref, doc_ref.shape[0], doc_ref.shape[1]
+    def __init__(self, doc_ref, sp, n_sp):
+        self.ref, self.n_sp, self.tok = doc_ref, n_sp, doc_ref.shape[1] // n_sp
         self.row = self.of(sp)
         self.column = jnp.broadcast_to(self.row, (128, self.tok)).T[:, 0:1]
 
     def of(self, sp):
-        return self.ref[pl.ds(sp, 1), :].astype(F32)
+        return self.ref[:, pl.ds(pl.multiple_of(sp * self.tok, 128), self.tok)].astype(F32)
 
     def last(self, sp):
         value = self.of(jnp.maximum(sp, 0))[:, self.tok - 1 : self.tok]
@@ -411,7 +438,7 @@
         return jnp.where(sp < self.n_sp, value, -2.0)
 
     def through(self, here, there):
-        return jnp.broadcast_to(jnp.where(here == there, 1.0, 0.0), (1, PAD_F))
+        return jnp.broadcast_to(jnp.where(here == there, 1.0, 0.0), (1, 128))
 
 
 def rows_sum(values):
@@ -435,17 +462,17 @@
 
 
 def forward_kernel(
-    n_sp, x_ref, gain_parts_ref, doc_ref, table_ref, wo_ref, wg_ref, wu_ref, wd_ref, wq_ref, wk_ref, wv_ref, *rest,
+    n_sp, x_ref, gain_a_ref, gain_m_ref, doc_ref, table_ref, wo_ref, wg_ref, wu_ref, wd_ref, wq_ref, wk_ref, wv_ref, *rest,
 ):
     n_unit = len(units_of(wd_ref.shape[0]))
-    (att_ref, inv_ref, q_ref, k_ref, v_ref, normed_ref, state_ref, gain_ref), rest = rest[:8], rest[8:]
-    fulls, rest = rest[: 2 + EARLY], rest[2 + EARLY :]
+    (att_ref, inv_ref, state_ref, gain_ref, q_ref, k_ref, v_ref, normed_ref, w_joint_ref), rest = rest[:9], rest[9:]
+    fulls, rest = rest[: 3 + EARLY], rest[3 + EARLY :]
     kept, rest = rest[: n_unit - EARLY], rest[n_unit - EARLY :]
-    (joint_own, out_own), rest = rest[:2], rest[2:]
+    (joint_own, more_own, out_own), rest = rest[:3], rest[3:]
     ffn_own, rest = rest[:n_unit], rest[n_unit:]
     (
         mask_ref, joint_vm, num_ref, den_ref, own_state, mate_state, in_state, out_state, gains_ref, gains_in,
-        prior_ref, send_sem, recv_sem, local_sem,
+        prior_ref, q_scr, k_scr, v_scr, normed_scr, send_sem, recv_sem, local_sem,
     ) = rest
     tok = x_ref.shape[0]
     n_z = n_sp // 2
@@ -454,24 +481,31 @@
     where = place(n_sp)
     dp, sp, g, gy, gx, z, c, across_x, across_y, diagonal, partner = where
     copies = Copies(send_sem, recv_sem)
-    joint_full = fulls[0]
-    owns = (joint_own, out_own) + tuple(ffn_own[:EARLY])
+    joint_full, more_full = fulls[:2]
+    owns = (joint_own, more_own, out_own) + tuple(ffn_own[:EARLY])
     gathers = [Gather(copies, k, n_z, own, full, where) for k, (own, full) in enumerate(zip(owns, fulls))]
     others = [(dp, lax.rem(sp + i, n_sp)) for i in range(1, n_sp)]
     for i, device in enumerate(others, 1):
         copies.add(("gain", i), gains_ref, gains_in.at[i - 1], device)
-    docs = Documents(doc_ref, sp)
+    docs = Documents(doc_ref, sp, n_sp)
     even = sp - c
     chain = Chain(
         copies, where, n_z, True, own_state, mate_state, in_state, out_state,
         docs.through(docs.last(even + 1), docs.last(even)), docs.through(docs.last(even), docs.last(even - 1)),
     )
     part_lane = lax.broadcasted_iota(jnp.int32, gains_ref.shape, 1)
-    gains_ref[...] = jnp.where(part_lane // (gains_ref.shape[1] // n_sp) == sp, gain_parts_ref[...], 0.0)
+    part = jnp.concatenate([jnp.broadcast_to(gain_a_ref[...], (4, gain_a_ref.shape[1])),
+                            jnp.broadcast_to(gain_m_ref[...], (4, gain_m_ref.shape[1]))], axis=0).astype(F32)
+    if part.shape[1] < gains_ref.shape[1]:
+        part = jnp.concatenate([part] * n_sp, axis=1)
+    gains_ref[...] = jnp.where(part_lane // (gains_ref.shape[1] // n_sp) == sp, part, 0.0)
     assembled = [
         pltpu.make_async_copy(wq_ref, joint_own.at[:, 0:lanes], local_sem.at[0]),
         pltpu.make_async_copy(wk_ref, joint_own.at[:, lanes : 2 * lanes], local_sem.at[1]),
-        pltpu.make_async_copy(wv_ref, joint_own.at[:, 2 * lanes :], local_sem.at[2]),
+        pltpu.make_async_copy(
+            wv_ref.at[:, 0 : joint_own.shape[1] - 2 * lanes], joint_own.at[:, 2 * lanes :], local_sem.at[2]
+        ),
+        pltpu.make_async_copy(wv_ref.at[:, joint_own.shape[1] - 2 * lanes :], more_own, local_sem.at[3]),
     ]
     for copy in assembled:
         copy.start()
@@ -480,6 +514,7 @@
     for copy in assembled:
         copy.wait()
     gathers[0].stage(0)
+    gathers[1].stage(0)
     out_own[...] = wo_ref[...].T
     width = wd_ref.shape[0]
     for own, (first, last) in zip(ffn_own, units_of(width)):
@@ -499,7 +534,7 @@
     gain_ref[...] = gains_ref[...] + rows_sum([gains_in[i] for i in range(n_sp - 1)])
     x = x_ref[...].astype(F32)
     scale = lax.rsqrt(jnp.mean(x * x, axis=1, keepdims=True) + EPSILON)
-    normed_ref[...] = (x * scale * gain_ref[0:1]).astype(BF16)
+    normed_scr[...] = (x * scale * gain_ref[0:1]).astype(BF16)
     local = [
         pltpu.make_async_copy(own, gather.own_place, local_sem.at[k])
         for k, (own, gather) in enumerate(zip(owns, gathers))
@@ -510,25 +545,44 @@
     for copy in local:
         copy.start()
     gathers[0].stage(1)
-    gathers[1].stage(0)
+    gathers[1].stage(1)
+    gathers[0].stage(2)
     gathers[2].stage(0)
-    gathers[0].stage(2)
+    gathers[3].stage(0)
+    gathers[1].stage(2)
     gathers[0].stage(3)
+    gathers[1].stage(3)
     gathers[0].stage(4)
     for copy in local:
         copy.wait()
-    fetch = pltpu.make_async_copy(joint_full, joint_vm, local_sem.at[0])
-    fetch.start()
-    fetch.wait()
+    split = joint_full.shape[1]
+    fetches = [
+        pltpu.make_async_copy(joint_full, joint_vm.at[:, 0:split], local_sem.at[0]),
+        pltpu.make_async_copy(more_full, joint_vm.at[:, split:], local_sem.at[1]),
+    ]
+    fetches[0].start()
+    fetches[0].wait()
     wide = joint_vm.shape[1]
     for first in range(0, wide, BLK):
-        part = mm(normed_ref[...], joint_vm[:, first : first + BLK]).astype(BF16)
+        if first == split:
+            gathers[1].stage(4)
+            fetches[1].start()
+            fetches[1].wait()
+        part = mm(normed_scr[...], joint_vm[:, first : first + BLK]).astype(BF16)
         if first < lanes:
-            q_ref[:, first : first + BLK] = part
+            q_scr[:, first : first + BLK] = part
         elif first < 2 * lanes:
-            k_ref[:, first - lanes : first - lanes + BLK] = part
+            k_scr[:, first - lanes : first - lanes + BLK] = part
         else:
-            v_ref[:, first - 2 * lanes : first - 2 * lanes + BLK] = part
+            v_scr[:, first - 2 * lanes : first - 2 * lanes + BLK] = part
+    saves = [
+        pltpu.make_async_copy(src, dst, local_sem.at[i])
+        for i, (src, dst) in enumerate(
+            ((q_scr, q_ref), (k_scr, k_ref), (v_scr, v_ref), (normed_scr, normed_ref), (joint_vm, w_joint_ref))
+        )
+    ]
+    for copy in saves:
+        copy.start()
 
     tail = jnp.where(docs.row == docs.last(sp), 1.0, 0.0)
 
@@ -539,19 +593,19 @@
                 gathers[k].stage(n)
 
     def state_pair(p, carry):
-        at(p, 0, (1, 1))
-        at(p, 2, (2, 1), (3, 0))
-        at(p, 5, (1, 2))
+        at(p, 0, (2, 1))
+        at(p, 2, (3, 1), (4, 0))
+        at(p, 5, (2, 2))
         columns = pl.ds(pl.multiple_of(p * 128, 128), 128)
-        v_t = v_ref[:, columns].astype(F32).T * tail
+        v_t = v_scr[:, columns].astype(F32).T * tail
         ones = jnp.broadcast_to(tail, (16, tail.shape[1]))
         for side in range(2):
             head = p * 2 + side
             sel = selectors(table, head, lanes)
-            one, two = factors(k_ref[...], sel, table)
+            one, two = factors(k_scr[...], sel, table)
             phi = (one * two).astype(BF16)
             lhs = jnp.concatenate([v_t[side * 64 : side * 64 + 64], ones], axis=0)
-            own_state[head] = mm(lhs.astype(BF16), phi).astype(BF16)
+            pack(own_state, 2 * pairs, p, side, mm(lhs.astype(BF16), phi))
         return carry
 
     lax.fori_loop(0, pairs, state_pair, 0)
@@ -562,20 +616,20 @@
     lane = lax.broadcasted_iota(jnp.int32, (BLK, 128), 1)
 
     def intra_pair(p, carry):
-        at(p, 1, (1, 3), (2, 2))
-        at(p, 3, (3, 1))
-        at(p, 4, (2, 3))
-        at(p, 7, (3, 2))
+        at(p, 1, (2, 3), (3, 2))
+        at(p, 3, (4, 1))
+        at(p, 4, (3, 3))
+        at(p, 7, (4, 2))
         chain.middle(p == turn)
         columns = pl.ds(pl.multiple_of(p * 128, 128), 128)
-        v_hat = with_ones(v_ref[:, columns])
-        heads = [head_lanes(q_ref[...], p * 2 + side) for side in range(2)]
+        v_hat = with_ones(v_scr[:, columns])
+        heads = [head_lanes(q_scr[...], p * 2 + side) for side in range(2)]
         for i in range(tok // BLK):
             rows = slice(i * BLK, (i + 1) * BLK)
             keys = slice(0, (i + 1) * BLK)
             totals = []
             for side in range(2):
-                t = mm(heads[side][rows], k_ref[keys, :], NT) + 4.0
+                t = mm(heads[side][rows], k_scr[keys, :], NT) + 4.0
                 w = ((t * t + 16.0) * mask_ref[rows, keys]).astype(BF16)
                 totals.append(mm(w, v_hat[keys]))
             num_ref[rows, columns] = jnp.where(lane < 64, totals[0][:, :128], totals[1][:, :128])
@@ -588,7 +642,7 @@
     wide_lane = lax.broadcasted_iota(jnp.int32, (tok, 128), 1)
 
     def inter_pair(p, carry):
-        at(p, 4, (3, 3))
+        at(p, 4, (4, 3))
         columns = pl.ds(pl.multiple_of(p * 128, 128), 128)
         totals = []
         for side in range(2):
@@ -596,23 +650,25 @@
             sel = selectors(table, head, lanes)
             state = state_ref[head]
             z_rows = jnp.broadcast_to(state[64:65].astype(F32), (128, PAD_F)).astype(BF16)
-            one, two = factors(q_ref[...], sel, table)
+            one, two = factors(q_scr[...], sel, table)
             totals.append(mm((one * two).astype(BF16), placed(state, side, z_rows), NT) * prior)
         num = num_ref[:, columns] + jnp.where(wide_lane < 64, totals[0][:, :128], totals[1][:, :128])
         den = den_ref[:, columns] + jnp.where(wide_lane < 64, totals[0][:, 128:], totals[1][:, 128:])
         inv = 1.0 / den
-        inv_ref[:, columns] = inv
+        inv_ref[:, columns] = inv.astype(BF16)
         att_ref[:, columns] = (num * inv).astype(BF16)
         return carry
 
     lax.fori_loop(0, pairs, inter_pair, 0)
-    for gather in gathers[1:]:
+    for gather in gathers[2:]:
         gather.stage(4)
+    for copy in saves:
+        copy.wait()
     copies.sent(*[("gain", i) for i in range(1, n_sp)])
     chain.drain()
 
 
-def forward(n_sp, x, gains, docs, table, wo, wg, wu, wd, wq, wk, wv):
+def forward(n_sp, x, gain_a, gain_m, docs, table, wo, wg, wu, wd, wq, wk, wv):
     tok, dim = x.shape
     lanes, values = wq.shape[1], wv.shape[1]
     heads = lanes // FEAT
@@ -620,44 +676,49 @@
     vmem, anywhere = pl.BlockSpec(memory_space=pltpu.VMEM), pl.BlockSpec(memory_space=pl.ANY)
     n_z = n_sp // 2
     spans = [3 * CHUNK * (last - first) for first, last in units_of(wd.shape[0])]
-    gathered = [2 * lanes + values, dim] + spans[:EARLY]
+    joint = 2 * lanes + values
+    gathered = [joint // 2, joint // 2, dim] + spans[:EARLY]
     sems = len(gathered) * n_copies(n_z) + n_sp + 2
     shape = jax.ShapeDtypeStruct
     result = pl.pallas_call(
         functools.partial(forward_kernel, n_sp),
         out_shape=(
-            shape((tok, values), BF16), shape((tok, values), F32), shape((tok, lanes), BF16),
-            shape((tok, lanes), BF16), shape((tok, values), BF16), shape((tok, dim), BF16),
-            shape((heads, ROWS_S, PAD_F), BF16), shape((8, dim), F32),
+            shape((tok, values), BF16), shape((tok, values), BF16), shape((heads, ROWS_S, PAD_F), BF16),
+            shape((8, dim), F32), shape((tok, lanes), BF16), shape((tok, lanes), BF16),
+            shape((tok, values), BF16), shape((tok, dim), BF16), shape((dim, joint), BF16),
         )
         + tuple(shape((shard * n_sp, w), BF16) for w in gathered)
         + tuple(shape((shard, w), BF16) for w in spans[EARLY:]),
-        in_specs=[vmem] * 8 + [anywhere] * 3,
-        out_specs=(vmem,) * 8 + (anywhere,) * (len(gathered) + len(spans) - EARLY),
-        scratch_shapes=[pltpu.VMEM((shard, w), BF16) for w in [2 * lanes + values, dim] + spans]
+        in_specs=[vmem] * 9 + [anywhere] * 3,
+        out_specs=(vmem,) * 4 + (anywhere,) * (5 + len(gathered) + len(spans) - EARLY),
+        scratch_shapes=[pltpu.VMEM((shard, w), BF16) for w in [joint // 2, joint // 2, dim] + spans]
         + [
             pltpu.VMEM((tok, tok), F32),
-            pltpu.VMEM((dim, 2 * lanes + values), BF16),
+            pltpu.VMEM((dim, joint), BF16),
             pltpu.VMEM((tok, values), F32),
             pltpu.VMEM((tok, values), F32),
-            pltpu.VMEM((heads, ROWS_S, PAD_F), BF16),
-            pltpu.VMEM((heads, ROWS_S, PAD_F), BF16),
-            pltpu.VMEM((heads, ROWS_S, PAD_F), BF16),
-            pltpu.VMEM((heads, ROWS_S, PAD_F), BF16),
+            pltpu.VMEM(packed_shape(heads), BF16),
+            pltpu.VMEM(packed_shape(heads), BF16),
+            pltpu.VMEM(packed_shape(heads), BF16),
+            pltpu.VMEM(packed_shape(heads), BF16),
             pltpu.VMEM((8, dim), F32),
             pltpu.VMEM((n_sp - 1, 8, dim), F32),
             pltpu.VMEM((tok, 128), F32),
+            pltpu.VMEM((tok, lanes), BF16),
+            pltpu.VMEM((tok, lanes), BF16),
+            pltpu.VMEM((tok, values), BF16),
+            pltpu.VMEM((tok, dim), BF16),
             pltpu.SemaphoreType.DMA((sems,)),
             pltpu.SemaphoreType.DMA((sems,)),
-            pltpu.SemaphoreType.DMA((8,)),
+            pltpu.SemaphoreType.DMA((10,)),
         ],
         compiler_params=pltpu.CompilerParams(
             collective_id=0, has_side_effects=True, vmem_limit_bytes=60 << 20
         ),
         name="forward",
-    )(x, gains, docs, table, wo, wg, wu, wd, wq, wk, wv)
-    n = 8 + len(gathered)
-    return result[:8], result[8:10], result[10:n], result[n:]
+    )(x, gain_a, gain_m, docs, table, wo, wg, wu, wd, wq, wk, wv)
+    n = 9 + len(gathered)
+    return result[:9], result[11], result[12:n], result[n:]
 
 
 def backward_kernel(
@@ -670,7 +731,8 @@
     swaps, rest = rest[:n_red], rest[n_red:]
     buffers, rest = [rest[4 * i : 4 * i + 4] for i in range(n_red)], rest[4 * n_red :]
     (
-        stage_buf, mask_ref, ghat_ref, gq_acc, gk_acc, own_state, mate_state, in_state, out_state, prior_ref, later_ref,
+        stage_buf, mask_ref, ghat_ref, gq_acc, gk_acc, own_state, mate_state, in_state, out_state, later_state,
+        prior_ref, later_ref,
         send_sem, recv_sem, local_sem,
     ) = rest
     tok, lanes = q_ref.shape
@@ -686,7 +748,7 @@
         )
         for k in range(n_red)
     ]
-    docs = Documents(doc_ref, sp)
+    docs = Documents(doc_ref, sp, n_sp)
     even = sp - c
     chain = Chain(
         copies, where, n_z, False, own_state, mate_state, in_state, out_state,
@@ -721,7 +783,7 @@
         for when, todo in GHAT_SCHEDULE:
             at(p, when, *todo)
         columns = pl.ds(pl.multiple_of(p * 128, 128), 128)
-        scaled = g_ref[:, columns].astype(F32) * inv_ref[:, columns]
+        scaled = g_ref[:, columns].astype(F32) * inv_ref[:, columns].astype(F32)
         product = scaled * att_ref[:, columns].astype(F32)
         high = product.astype(BF16)
         low = (product - high.astype(F32)).astype(BF16)
@@ -742,9 +804,10 @@
             )
             state = mm(lhs.astype(BF16), phi)
             z_row = jnp.sum(state[64:80], axis=0, keepdims=True)
-            own_state[head] = jnp.concatenate(
-                [state[0:64], jnp.broadcast_to(z_row, (16, PAD_F))], axis=0
-            ).astype(BF16)
+            pack(
+                own_state, 2 * pairs, p, side,
+                jnp.concatenate([state[0:64], jnp.broadcast_to(z_row, (16, PAD_F))], axis=0),
+            )
         return carry
 
     lax.fori_loop(0, pairs, ghat_pair, 0)
@@ -798,7 +861,7 @@
 
     lax.fori_loop(0, pairs, main_pair, 0)
     chain.drain()
-    chain.finish(out_state, table[4:5])
+    chain.finish(later_state, table[4:5])
 
     def later_pair(p, carry):
         for when, todo in LATE_SCHEDULE:
@@ -809,7 +872,7 @@
         for side in range(2):
             head = p * 2 + side
             sel = selectors(table, head, lanes)
-            later = out_state[head]
+            later = later_state[head]
             z_one = jnp.where(first_row == 0, later[64:65], jnp.zeros((128, PAD_F), BF16))
             rows_n = placed(later, side, z_one)
             k_one, k_two = factors(k_ref[...], sel, table)
@@ -865,9 +928,10 @@
             pltpu.VMEM((heads // 2, tok, 256), BF16),
             pltpu.VMEM(q.shape, F32),
             pltpu.VMEM(q.shape, F32),
-            pltpu.VMEM((heads, ROWS_S, PAD_F), BF16),
-            pltpu.VMEM((heads, ROWS_S, PAD_F), BF16),
-            pltpu.VMEM((heads, ROWS_S, PAD_F), BF16),
+            pltpu.VMEM(packed_shape(heads), BF16),
+            pltpu.VMEM(packed_shape(heads), BF16),
+            pltpu.VMEM(packed_shape(heads), BF16),
+            pltpu.VMEM(packed_shape(heads), BF16),
             pltpu.VMEM((heads, ROWS_S, PAD_F), BF16),
             pltpu.VMEM((tok, 128), F32),
             pltpu.VMEM((tok, 128), F32),
@@ -913,13 +977,13 @@
     ggain_ref, rest = rest[0], rest[1:]
     finals, rest = rest[:IN_FFN], rest[IN_FFN:]
     (output_ref, gh_ref, gatt_ref, gout_ref), rest = rest[:4], rest[4:]
-    grads, rest = rest[:n_sum], rest[n_sum:]
+    grads, rest = rest[: n_sum - IN_FFN], rest[n_sum - IN_FFN :]
+    late, rest = rest[: n_unit - EARLY], rest[n_unit - EARLY :]
+    grads, rest = rest[:IN_FFN] + grads, rest[IN_FFN:]
     swaps, rest = rest[:IN_FFN], rest[IN_FFN:]
-    late, rest = rest[: n_unit - EARLY], rest[n_unit - EARLY :]
     buffers, rest = [rest[4 * i : 4 * i + 4] for i in range(IN_FFN)], rest[4 * IN_FFN :]
     (
-        stage_buf, hid, n2, n2_t, cot_t, acc_o, acc_n, gout, w_buf, g_buf, send_sem, recv_sem, local_sem, w_sem, g_sem,
-        o_sem,
+        hid, n2, n2_t, cot_t, acc_o, acc_n, w_buf, g_buf, send_sem, recv_sem, w_sem, g_sem, o_sem,
     ) = rest
     tok, dim = x_ref.shape
     n_z = n_sp // 2
@@ -928,10 +992,7 @@
     copies = Copies(send_sem, recv_sem)
     gathers = [Gather(copies, ("g", k), n_z, own, full, where) for k, (own, full) in enumerate(zip(kept, late))]
     reduces = [
-        Reduce(
-            copies, ("r", k), n_z, where, grads[k], swaps[k], buffers[k], finals[k],
-            stage_buf.at[:, :, :, :, :, 0 : grads[k].shape[-1]], local_sem,
-        )
+        Reduce(copies, ("r", k), n_z, where, grads[k], swaps[k], buffers[k], finals[k])
         for k in range(IN_FFN)
     ]
     along = [(dp, lax.rem(z + i, n_z) * 2 + c) for i in range(1, n_z)]
@@ -979,7 +1040,7 @@
                     ).start()
 
     load(0, 0)
-    gain = gain_ref[1:2]
+    gain = gain_ref[4:5]
     for i in range(tok // BLK):
         rows = slice(i * BLK, (i + 1) * BLK)
         hidden = x_ref[rows, :].astype(F32) + mm(att_ref[rows, :], out_w_ref[...], NT)
@@ -1053,15 +1114,18 @@
     ]
     for copy in outs:
         copy.start()
-    for first in range(0, att_ref.shape[1], CHUNK):
-        columns = slice(first, first + CHUNK)
-        gout[:, :, :, :, :, columns] = (
-            mm(n2_t[...], att_ref[:, columns], TN).astype(BF16).reshape(grad_shape)
-        )
-    outs.append(pltpu.make_async_copy(gout, gout_ref, o_sem.at[3]))
-    outs[3].start()
     save(chunks - 2, (chunks - 2) % 2, True)
     save(chunks - 1, (chunks - 1) % 2, True)
+    for i, first in enumerate(range(0, att_ref.shape[1], CHUNK)):
+        columns = slice(first, first + CHUNK)
+        piece = g_buf.at[i // 3, i % 3]
+        piece[...] = mm(n2_t[...], att_ref[:, columns], TN).astype(BF16).reshape(grad_shape)
+        outs.append(
+            pltpu.make_async_copy(
+                piece, gout_ref.at[:, :, :, :, :, pl.ds(first, CHUNK)], g_sem.at[i // 3, i % 3]
+            )
+        )
+        outs[-1].start()
     run(FFN_LAST)
     for copy in outs:
         copy.wait()
@@ -1086,26 +1150,24 @@
         out_shape=(shape((8, dim), F32),)
         + tuple(shape((2, 2, rows, w), BF16) for w in spans[:IN_FFN])
         + (shape((tok, dim), BF16), shape((tok, dim), F32), shape((tok, values), BF16), split(values))
-        + tuple(split(w) for w in spans)
-        + tuple(shape((n_z, 2, 2, rows, w), BF16) for w in spans[:IN_FFN])
+        + tuple(split(w) for w in spans[IN_FFN:])
         + full_shapes,
         in_specs=[vmem] * 5 + [anywhere] * len(early) + [vmem] * len(kept),
-        out_specs=(vmem,) * (1 + IN_FFN) + (anywhere,) * (4 + len(spans) + IN_FFN + len(kept)),
-        scratch_shapes=sum([reduce_scratch(n_z, rows, w) for w in spans[:IN_FFN]], [])
+        out_specs=(vmem,) * (1 + IN_FFN) + (anywhere,) * (4 + len(spans) - IN_FFN + len(kept)),
+        scratch_shapes=[pltpu.VMEM((n_z, 2, 2, 2, rows, w), BF16) for w in spans[:IN_FFN]]
+        + [pltpu.VMEM((n_z, 2, 2, rows, w), BF16) for w in spans[:IN_FFN]]
+        + sum([reduce_scratch(n_z, rows, w) for w in spans[:IN_FFN]], [])
         + [
-            pltpu.VMEM((2, 2, 2, 2, rows, max(spans[:IN_FFN])), BF16),
             pltpu.VMEM((tok, dim), F32),
             pltpu.VMEM((tok, dim), BF16),
             pltpu.VMEM((dim, tok), BF16),
             pltpu.VMEM((dim, tok), BF16),
             pltpu.VMEM((tok, dim), F32),
             pltpu.VMEM((tok, dim), F32),
-            pltpu.VMEM((n_z, 2, 2, 2, rows, values), BF16),
             pltpu.VMEM((2, 3, dim, CHUNK), BF16),
             pltpu.VMEM((2, 3, n_z, 2, 2, 2, rows, CHUNK), BF16),
             pltpu.SemaphoreType.DMA((sems,)),
             pltpu.SemaphoreType.DMA((sems,)),
-            pltpu.SemaphoreType.DMA((2, 2)),
             pltpu.SemaphoreType.DMA((2, 3)),
             pltpu.SemaphoreType.DMA((2, 3)),
             pltpu.SemaphoreType.DMA((4,)),
@@ -1118,25 +1180,32 @@
     n = 1 + IN_FFN
     shards = shards_of(result[1:n])
     output, g_hidden, g_att, g_out = result[n : n + 4]
-    grads = result[n + 4 + IN_FFN : n + 4 + len(spans)]
+    grads = result[n + 4 : n + 4 + len(spans) - IN_FFN]
     return output, g_hidden, g_att, result[0], g_out, shards, grads
 
 
 def tail_kernel(
-    n_sp, normed_ref, gq_ref, gk_ref, gv_ref, w_ref, x_ref, gh_ref, gain_ref, ggain_ref,
-    gin_ref, gains_ref, final_v, final_qk,
-    src_v, src_qk, swap_v, swap_qk, *rest,
+    n_sp, normed_ref, gq_ref, gk_ref, gv_ref, gain_ref, ggain_ref, w_hbm, x_hbm, gh_hbm, gains_ref, *rest,
 ):
-    buffers, rest = (rest[:4], rest[4:8]), rest[8:]
-    own_gains, sum_gains, in_sp, in_dp, send_sem, recv_sem = rest
+    finals, rest = rest[:3], rest[3:]
+    gin_ref, rest = rest[0], rest[1:]
+    sources, rest = rest[:3], rest[3:]
+    swaps, rest = rest[:3], rest[3:]
+    buffers, rest = [rest[4 * i : 4 * i + 4] for i in range(3)], rest[12:]
+    w_ref, x_ref, gh_ref, own_gains, sum_gains, in_sp, in_dp, send_sem, recv_sem, local_sem = rest
     tok, dim = x_ref.shape
     n_z = n_sp // 2
     lanes = gq_ref.shape[1]
     where = place(n_sp)
     dp, sp, g, gy, gx, z, c, across_x, across_y, diagonal, partner = where
+    loads = [
+        pltpu.make_async_copy(src, dst, local_sem.at[i])
+        for i, (src, dst) in enumerate(((w_hbm, w_ref), (x_hbm, x_ref), (gh_hbm, gh_ref)))
+    ]
+    for copy in loads:
+        copy.start()
     copies = Copies(send_sem, recv_sem)
-    first = Reduce(copies, "v", n_z, where, src_v, swap_v, buffers[0], final_v)
-    second = Reduce(copies, "qk", n_z, where, src_qk, swap_qk, buffers[1], final_qk)
+    reduces = [Reduce(copies, k, n_z, where, sources[k], swaps[k], buffers[k], finals[k]) for k in range(3)]
     others = [(dp, lax.rem(sp + i, n_sp)) for i in range(1, n_sp)]
     groups = [across_x, across_y, diagonal]
     for i, device in enumerate(others):
@@ -1144,20 +1213,26 @@
     for i, device in enumerate(groups):
         copies.add(("dp", i), sum_gains, in_dp.at[i], device)
     meet(others + groups)
-    block = src_v.shape[:-1] + (BLK,)
-    for i in range(0, gv_ref.shape[1], BLK):
-        columns = slice(i, i + BLK)
-        src_v[:, :, :, :, :, columns] = mm(normed_ref[...], gv_ref[:, columns], TN).astype(BF16).reshape(block)
-    for i, ref in enumerate((gq_ref, gk_ref)):
-        for j in range(0, lanes, BLK):
-            src_qk[:, :, :, :, :, i * lanes + j : i * lanes + j + BLK] = (
-                mm(normed_ref[...], ref[:, j : j + BLK], TN).astype(BF16).reshape(block)
+    block = sources[0].shape[:-1] + (BLK,)
+    half = gv_ref.shape[1] // 2
+    pieces = [
+        [(gv_ref, i) for i in range(0, half, BLK)],
+        [(gv_ref, i) for i in range(half, 2 * half, BLK)],
+        [(ref, i) for ref in (gq_ref, gk_ref) for i in range(0, lanes, BLK)],
+    ]
+    for k, piece in enumerate(pieces):
+        for j, (ref, i) in enumerate(piece):
+            sources[k][:, :, :, :, :, j * BLK : (j + 1) * BLK] = (
+                mm(normed_ref[...], ref[:, i : i + BLK], TN).astype(BF16).reshape(block)
             )
-        if i == 0:
-            first.stage(0)
-    todo = [[(second, 0), (first, 1)], [(second, 1)], [(first, 2)], [(second, 2)]]
+            if j == 0 and k > 0:
+                reduces[k - 1].stage(0)
+    for copy in loads:
+        copy.wait()
+    todo = [[(2, 0), (0, 1)], [(1, 1)], [(0, 2), (2, 1)], [(1, 2)]]
     total = jnp.zeros((1, dim), F32)
     gain = gain_ref[0:1]
+    saves = []
     for i in range(tok // BLK):
         rows = slice(i * BLK, (i + 1) * BLK)
         e = (
@@ -1170,27 +1245,33 @@
         total = total + jnp.sum(e * u * scale, axis=0, keepdims=True)
         eg = e * gain
         inner = jnp.mean(eg * u, axis=1, keepdims=True)
-        gin_ref[rows, :] = gh_ref[rows, :] + scale * eg - u * (scale * scale * scale * inner)
-        for reduce, n in todo[i] if i < len(todo) else ():
-            reduce.stage(n)
+        gh_ref[rows, :] = gh_ref[rows, :] + scale * eg - u * (scale * scale * scale * inner)
+        for k, n in todo[i] if i < len(todo) else ():
+            reduces[k].stage(n)
     for i in range(tok // BLK, len(todo)):
-        for reduce, n in todo[i]:
-            reduce.stage(n)
+        for k, n in todo[i]:
+            reduces[k].stage(n)
+    save = pltpu.make_async_copy(gh_ref, gin_ref, local_sem.at[0])
+    save.start()
     row = lax.broadcasted_iota(jnp.int32, own_gains.shape, 0)
     own_gains[...] = jnp.where(row == 0, jnp.broadcast_to(total, own_gains.shape), ggain_ref[...])
-    first.stage(3)
+    reduces[0].stage(3)
+    reduces[2].stage(2)
     copies.start(*[("sp", i) for i in range(n_sp - 1)])
-    second.stage(3)
+    reduces[1].stage(3)
+    reduces[0].stage(4)
+    reduces[2].stage(3)
     copies.arrived(*[("sp", i) for i in range(n_sp - 1)])
     sum_gains[...] = own_gains[...] + rows_sum([in_sp[i] for i in range(n_sp - 1)])
-    first.stage(4)
+    reduces[1].stage(4)
     copies.start(*[("dp", i) for i in range(3)])
-    second.stage(4)
+    reduces[2].stage(4)
     copies.arrived(*[("dp", i) for i in range(3)])
     gains_ref[...] = sum_gains[...] + rows_sum([in_dp[i] for i in range(3)])
-    first.stage(5)
-    second.stage(5)
+    for reduce in reduces:
+        reduce.stage(5)
     copies.sent(*[("sp", i) for i in range(n_sp - 1)], *[("dp", i) for i in range(3)])
+    save.wait()
 
 
 def tail(n_sp, normed, gq, gk, gv, w_joint, x, g_hidden, gain, ggain):
@@ -1198,36 +1279,41 @@
     lanes, values = gq.shape[1], gv.shape[1]
     n_z = n_sp // 2
     rows = dim // n_sp // GROUP
-    vmem = pl.BlockSpec(memory_space=pltpu.VMEM)
+    vmem, anywhere = pl.BlockSpec(memory_space=pltpu.VMEM), pl.BlockSpec(memory_space=pl.ANY)
     shape = jax.ShapeDtypeStruct
-    widths = (values, 2 * lanes)
-    sems = 2 * n_reduce(n_z) + n_sp + 2
+    widths = (values // 2, values // 2, 2 * lanes)
+    sems = 3 * n_reduce(n_z) + n_sp + 2
     return pl.pallas_call(
         functools.partial(tail_kernel, n_sp),
-        out_shape=(shape((tok, dim), F32), shape((8, dim), F32))
-        + tuple(shape((2, 2, rows, w), BF16) for w in widths),
-        in_specs=[vmem] * 9,
-        out_specs=(vmem,) * 4,
+        out_shape=(shape((8, dim), F32),)
+        + tuple(shape((2, 2, rows, w), BF16) for w in widths)
+        + (shape((tok, dim), F32),),
+        in_specs=[vmem] * 6 + [anywhere] * 3,
+        out_specs=(vmem,) * 4 + (anywhere,),
         scratch_shapes=[pltpu.VMEM((n_z, 2, 2, 2, rows, w), BF16) for w in widths]
         + [pltpu.VMEM((n_z, 2, 2, rows, w), BF16) for w in widths]
         + sum([reduce_scratch(n_z, rows, w) for w in widths], [])
         + [
+            pltpu.VMEM(w_joint.shape, BF16),
+            pltpu.VMEM(x.shape, BF16),
+            pltpu.VMEM((tok, dim), F32),
             pltpu.VMEM((8, dim), F32),
             pltpu.VMEM((8, dim), F32),
             pltpu.VMEM((n_sp - 1, 8, dim), F32),
             pltpu.VMEM((3, 8, dim), F32),
             pltpu.SemaphoreType.DMA((sems,)),
             pltpu.SemaphoreType.DMA((sems,)),
+            pltpu.SemaphoreType.DMA((3,)),
         ],
         compiler_params=pltpu.CompilerParams(
-            collective_id=3, has_side_effects=True, vmem_limit_bytes=60 << 20
+            collective_id=3, has_side_effects=True, vmem_limit_bytes=63 << 20
         ),
         name="tail",
-    )(normed, gq, gk, gv, w_joint, x, g_hidden, gain, ggain)
+    )(normed, gq, gk, gv, gain, ggain, w_joint, x, g_hidden)
 
 
 def finish_kernel(sums, *refs):
-    n = len(sums) + 3
+    n = len(sums) + 4
     sources, refs = refs[:n], refs[n:]
     (q_out, k_out, v_out, out_out, gate_out, up_out, down_out), refs = refs[:7], refs[7:]
     held, sem = refs[:n], refs[n]
@@ -1236,12 +1322,13 @@
         copy.start()
     for copy in copies:
         copy.wait()
-    qk_ref, v_ref, out_ref, units = held[0], held[1], held[2], held[3:]
+    qk_ref, va_ref, vb_ref, out_ref, units = held[0], held[1], held[2], held[3], held[4:]
     lanes = q_out.shape[1]
     width = gate_out.shape[0]
     q_out[...] = qk_ref[:, :lanes].astype(F32)
     k_out[...] = qk_ref[:, lanes:].astype(F32)
-    v_out[...] = v_ref[...].astype(F32)
+    v_out[:, : va_ref.shape[1]] = va_ref[...].astype(F32)
+    v_out[:, va_ref.shape[1] :] = vb_ref[...].astype(F32)
     out_out[...] = out_ref[...].astype(F32).T
     for unit, (first, last) in zip(units, sums):
         lo, hi = first * CHUNK, min(last * CHUNK, width)
@@ -1250,15 +1337,15 @@
             out[lo:hi, :] = unit[:, i * span : i * span + hi - lo].astype(F32).T
 
 
-def finish(width, lanes, qk, v, out, units):
-    shard = v.shape[0]
+def finish(width, lanes, qk, va, vb, out, units):
+    shard = va.shape[0]
     vmem, anywhere = pl.BlockSpec(memory_space=pltpu.VMEM), pl.BlockSpec(memory_space=pl.ANY)
     shape = jax.ShapeDtypeStruct
-    arrays = (qk, v, out, *units)
+    arrays = (qk, va, vb, out, *units)
     return pl.pallas_call(
         functools.partial(finish_kernel, reduce_units(-(-width // CHUNK))),
         out_shape=(
-            shape((shard, lanes), F32), shape((shard, lanes), F32), shape(v.shape, F32),
+            shape((shard, lanes), F32), shape((shard, lanes), F32), shape((shard, 2 * va.shape[1]), F32),
             shape(out.shape[::-1], F32), shape((width, shard), F32), shape((width, shard), F32),
             shape((width, shard), F32),
         ),
@@ -1278,15 +1365,17 @@
     tok = tokens.shape[0]
     heads = w_query.shape[1] // FEAT
     table = feature_table()
-    docs = doc_ids.reshape(n_sp, tok)
+    docs = doc_ids
     width = gain_attn.shape[0]
     lanes = heads * FEAT
     hidden_units = w_gate.shape[1]
-    gain_parts = jnp.tile(jnp.stack([gain_attn, gain_mlp] + [gain_mlp] * 6).astype(F32), (1, n_sp))
+    parts = [part[None, :] for part in (gain_attn, gain_mlp)]
+    if width % 128:
+        parts = [jnp.tile(part, (1, n_sp)) for part in parts]
     (
-        (att, inv, q, k, v, normed_one, prior_state, gain), (w_joint, out_t), early, kept
+        (att, inv, prior_state, gain, q, k, v, normed_one, w_joint), out_t, early, kept
     ) = forward(
-        n_sp, tokens, gain_parts, docs, table, w_out, w_gate.T, w_up.T, w_down, w_query, w_key, w_value
+        n_sp, tokens, *parts, docs, table, w_out, w_gate.T, w_up.T, w_down, w_query, w_key, w_value
     )
     output, g_hidden, g_att, grad_gain_two, g_out, shards, grads = ffn(
         n_sp, tokens, att, out_t, gain, cotangent, hidden_units, early, kept
@@ -1294,7 +1383,7 @@
     (gq, gk, gv), (s_out, *more) = backward(
         n_sp, (q, k, v, g_att, att, inv, prior_state, docs, table), (g_out, *grads)
     )
-    grad_input, grad_gains, *joint = tail(
+    grad_gains, *joint, grad_input = tail(
         n_sp, normed_one, gq, gk, gv, w_joint, tokens, g_hidden, gain, grad_gain_two
     )
     n_dp = lax.axis_size("dp")
@@ -1304,9 +1393,9 @@
             shard = lax.psum(shard, "dp") * jnp.asarray(GROUP / n_dp, shard.dtype)
         return shard
 
-    s_value, s_query_key = shards_of(joint)
+    s_va, s_vb, s_query_key = shards_of(joint)
     g_query, g_key, g_value, g_w_out, g_gate, g_up, g_down = finish(
-        hidden_units, lanes, over_groups(s_query_key), over_groups(s_value), over_groups(s_out),
+        hidden_units, lanes, over_groups(s_query_key), over_groups(s_va), over_groups(s_vb), over_groups(s_out),
         [over_groups(shard) for shard in (*shards, *more)],
     )
     s_gains = over_groups(lax.dynamic_slice(grad_gains, (0, me * width), (2, width)))

time: 386 us -> 374 us (0.969)
  Pallas kernels: 368 us -> 360 us
    pallas_call x1, Pallas kernels: 53 us -> 41.8 us  [tail(): pl.pallas_call(functools.partial(tail_kernel, n_sp), out_shape=(shape((8,...]
    pallas_call x1, Pallas kernels: 107 us -> 113 us  [ffn(): pl.pallas_call(functools.partial(ffn_kernel, n_sp, gather_units, chunks),...]
where the time goes in v4:
time: 374 us; the launch traced here: 367 us
  Pallas kernels  360 us (96%)
  local copies, waits for them, and re-layouts  6.45 us (2%)
    pallas_call x1, Pallas kernels, ffn(): pl.pallas_call(functools.partial(ffn_kernel, n_sp, gather_units, chunks),...  113 us
    pallas_call x1, Pallas kernels, backward(): pl.pallas_call(functools.partial(backward_kernel, n_sp, widths), out_shap...  110 us
    pallas_call x1, Pallas kernels, forward(): pl.pallas_call(functools.partial(forward_kernel, n_sp), out_shape=(shape(...  90.4 us
    pallas_call x1, Pallas kernels, tail(): pl.pallas_call(functools.partial(tail_kernel, n_sp), out_shape=(shape((8,...  41.8 us

profile of v4, /device:TPU:0, one launch (start us, length us, event | category | flops | bytes accessed | tf_op | source)
XLA Modules:
  0.0 367.2 jit_solution(10682574120192394617)
XLA Ops:
  0.6 90.4 %forward.1 = (bf16[1024,1024]{1,0:T(8,128)(2,1)}, bf16[1024,1024]{1,0:T(8,128)(2,1)}, bf16[16,80,256]{2,1,0:T(8,128)(2,1)}, f32[8,1024]{1,0:T(8,128)}, bf16[1024...) custom-call(bf16[1024,1024]{1,0:T(8,128)(2,1)} %x_hbm.1, ...), custom_call_target="tpu_custom_call" | custom-call | tf_op jit(solution)/shard_map/forward/pallas_call | solution.py:683
  91.0 113.0 %ffn.1 = (f32[8,1024]{1,0:T(8,128)}, bf16[2,2,32,1536]{3,2,1,0:T(8,128)(2,1)}, bf16[2,2,32,1536]{3,2,1,0:T(8,128)(2,1)}, bf16[1024,1024]{1,0:T(8,128)(2,1)}, f32...) custom-call(bf16[1024,1024]{1,0:T(8,128)(2,1)} %x_hbm.1, ...), custom_call_target="tpu_custom_call" | custom-call | tf_op jit(solution)/shard_map/ffn/pallas_call | solution.py:1148
  204.1 109.7 %backward.1 = (bf16[1024,256]{1,0:T(8,128)(2,1)}, bf16[1024,256]{1,0:T(8,128)(2,1)}, bf16[1024,1024]{1,0:T(8,128)(2,1)}, bf16[2,2,32,1024]{3,2,1,0:T(8,128)(2,1)...) custom-call(bf16[1024,256]{1,0:T(8,128)(2,1)} %get-tuple-element.63., ...), custom_call_target="tpu_custom_call" | custom-call | tf_op jit(solution)/shard_map/backward/pallas_call | solution.py:917
  313.8 41.8 %tail.1 = (f32[8,1024]{1,0:T(8,128)}, bf16[2,2,32,512]{3,2,1,0:T(8,128)(2,1)}, bf16[2,2,32,512]{3,2,1,0:T(8,128)(2,1)}, bf16[2,2,32,512]{3,2,1,0:T(8,128)(2,1)}, f32[1024,1024]{1,0:T(8,128)}) custom-call(bf16[1024,1024]{1,0:T(8,128)(2,1)} %get-tuple-element.62.normed_ref, bf16[1024,256]{1,0:T(8,128)(2,1)} %get-tuple-element.73.gq_ref, ...), custom_call_target="tpu_custom_call" | custom-call | tf_op jit(solution)/shard_map/tail/pallas_call | solution.py:1286
  355.6 4.8 %finish.1 = (f32[128,256]{1,0:T(8,128)}, f32[128,256]{1,0:T(8,128)}, f32[128,1024]{1,0:T(8,128)}, f32[1024,128]{1,0:T(8,128)}, f32[2752,128]{1,0:T(8,128)}, /*index=5*/f32[2752,128]{1,0:T(8,128)}, f32[2752,128]{1,0:T(8,128)}) custom-call(bf16[128,512]{1,0:T(8,128)(2,1)} %bitcast.29, bf16[128,512]{1,0:T(8,128)(2,1)} %bitcast.27, bf16[128,512]{1,0:T(8,128)(2,1)} %bitcast.28, ...), custom_call_target="tpu_custom_call" | custom-call | tf_op jit(solution)/shard_map/finish/pallas_call | solution.py:1345
  360.4 0.7 constant_dynamic-slice_fusion
  361.1 0.5 slice_bitcast_fusion
  361.6 0.0 copy-start
  361.6 3.2 copy.26
  364.8 0.0 copy-done
  364.8 2.0 copy.27
Async XLA Ops:
  361.6 3.2 copy-start

commit v5 on v4

--- a/solution.py
+++ b/solution.py
@@ -448,6 +448,7 @@
     return total
 
 
+STRIP = 512
 CHAIN_STEPS = 3
 CHAIN_BACK_STEPS = 5
 CHUNK = 256
@@ -472,7 +473,7 @@
     ffn_own, rest = rest[:n_unit], rest[n_unit:]
     (
         mask_ref, joint_vm, num_ref, den_ref, own_state, mate_state, in_state, out_state, gains_ref, gains_in,
-        prior_ref, q_scr, k_scr, v_scr, normed_scr, send_sem, recv_sem, local_sem,
+        prior_ref, q_scr, k_scr, v_scr, normed_scr, normed_t, send_sem, recv_sem, local_sem,
     ) = rest
     tok = x_ref.shape[0]
     n_z = n_sp // 2
@@ -535,6 +536,7 @@
     x = x_ref[...].astype(F32)
     scale = lax.rsqrt(jnp.mean(x * x, axis=1, keepdims=True) + EPSILON)
     normed_scr[...] = (x * scale * gain_ref[0:1]).astype(BF16)
+    normed_t[...] = normed_scr[...].T
     local = [
         pltpu.make_async_copy(own, gather.own_place, local_sem.at[k])
         for k, (own, gather) in enumerate(zip(owns, gathers))
@@ -562,23 +564,27 @@
     ]
     fetches[0].start()
     fetches[0].wait()
-    wide = joint_vm.shape[1]
-    for first in range(0, wide, BLK):
-        if first == split:
+    project = lambda first: mm(normed_scr[...], joint_vm[:, pl.ds(first, BLK)]).astype(BF16)
+    for first in range(0, lanes, BLK):
+        q_scr[:, first : first + BLK] = project(first)
+        k_scr[:, first : first + BLK] = project(lanes + first)
+
+    def values_block(i, carry):
+        @pl.when(i == (split - 2 * lanes) // BLK)
+        def _():
             gathers[1].stage(4)
             fetches[1].start()
             fetches[1].wait()
-        part = mm(normed_scr[...], joint_vm[:, first : first + BLK]).astype(BF16)
-        if first < lanes:
-            q_scr[:, first : first + BLK] = part
-        elif first < 2 * lanes:
-            k_scr[:, first - lanes : first - lanes + BLK] = part
-        else:
-            v_scr[:, first - 2 * lanes : first - 2 * lanes + BLK] = part
+
+        first = pl.multiple_of(i * BLK, BLK)
+        v_scr[:, pl.ds(first, BLK)] = project(2 * lanes + first)
+        return carry
+
+    lax.fori_loop(0, v_scr.shape[1] // BLK, values_block, 0)
     saves = [
         pltpu.make_async_copy(src, dst, local_sem.at[i])
         for i, (src, dst) in enumerate(
-            ((q_scr, q_ref), (k_scr, k_ref), (v_scr, v_ref), (normed_scr, normed_ref), (joint_vm, w_joint_ref))
+            ((q_scr, q_ref), (k_scr, k_ref), (v_scr, v_ref), (normed_t, normed_ref), (joint_vm, w_joint_ref))
         )
     ]
     for copy in saves:
@@ -685,7 +691,7 @@
         out_shape=(
             shape((tok, values), BF16), shape((tok, values), BF16), shape((heads, ROWS_S, PAD_F), BF16),
             shape((8, dim), F32), shape((tok, lanes), BF16), shape((tok, lanes), BF16),
-            shape((tok, values), BF16), shape((tok, dim), BF16), shape((dim, joint), BF16),
+            shape((tok, values), BF16), shape((dim, tok), BF16), shape((dim, joint), BF16),
         )
         + tuple(shape((shard * n_sp, w), BF16) for w in gathered)
         + tuple(shape((shard, w), BF16) for w in spans[EARLY:]),
@@ -708,6 +714,7 @@
             pltpu.VMEM((tok, lanes), BF16),
             pltpu.VMEM((tok, values), BF16),
             pltpu.VMEM((tok, dim), BF16),
+            pltpu.VMEM((dim, tok), BF16),
             pltpu.SemaphoreType.DMA((sems,)),
             pltpu.SemaphoreType.DMA((sems,)),
             pltpu.SemaphoreType.DMA((10,)),
@@ -983,7 +990,7 @@
     swaps, rest = rest[:IN_FFN], rest[IN_FFN:]
     buffers, rest = [rest[4 * i : 4 * i + 4] for i in range(IN_FFN)], rest[4 * IN_FFN :]
     (
-        hid, n2, n2_t, cot_t, acc_o, acc_n, w_buf, g_buf, send_sem, recv_sem, w_sem, g_sem, o_sem,
+        hid, n2, n2_t, cot_t, acc_o, acc_n, parts, w_buf, g_buf, send_sem, recv_sem, w_sem, g_sem, o_sem,
     ) = rest
     tok, dim = x_ref.shape
     n_z = n_sp // 2
@@ -1041,8 +1048,8 @@
 
     load(0, 0)
     gain = gain_ref[4:5]
-    for i in range(tok // BLK):
-        rows = slice(i * BLK, (i + 1) * BLK)
+    def prepare(i, carry):
+        rows = pl.ds(pl.multiple_of(i * BLK, BLK), BLK)
         hidden = x_ref[rows, :].astype(F32) + mm(att_ref[rows, :], out_w_ref[...], NT)
         hid[rows, :] = hidden
         scale = lax.rsqrt(jnp.mean(hidden * hidden, axis=1, keepdims=True) + EPSILON)
@@ -1050,6 +1057,9 @@
         n2[rows, :] = normed
         n2_t[:, rows] = normed.T
         cot_t[:, rows] = cot_ref[rows, :].T
+        return carry
+
+    lax.fori_loop(0, tok // BLK, prepare, 0)
     acc_o[...] = jnp.zeros_like(acc_o)
     acc_n[...] = jnp.zeros_like(acc_n)
     for copy in own_copies:
@@ -1073,39 +1083,49 @@
         def _():
             load(chunk + 1, 1 - slot)
 
-        wg, wu, wd = w_buf[slot, 0], w_buf[slot, 1], w_buf[slot, 2]
-        gate = mm(n2[...], wg)
-        up = mm(n2[...], wu)
-        g_mixed = mm(cot_ref[...], wd)
-        sig = 1.0 / (1.0 + jnp.exp(-gate))
-        act = gate * sig
-        mixed = (act * up).astype(BF16)
-        g_gate = (g_mixed * up * sig * (1.0 + gate * (1.0 - sig))).astype(BF16)
-        g_up = (g_mixed * act).astype(BF16)
-        g_buf[slot, 0] = mm(n2_t[...], g_gate).astype(BF16).reshape(grad_shape)
-        g_buf[slot, 1] = mm(n2_t[...], g_up).astype(BF16).reshape(grad_shape)
-        g_buf[slot, 2] = mm(cot_t[...], mixed).astype(BF16).reshape(grad_shape)
+        def rows_part(i, carry):
+            rows = pl.ds(pl.multiple_of(i * STRIP, STRIP), STRIP)
+            wg, wu, wd = w_buf[slot, 0], w_buf[slot, 1], w_buf[slot, 2]
+            gate = mm(n2[rows, :], wg)
+            up = mm(n2[rows, :], wu)
+            g_mixed = mm(cot_ref[rows, :], wd)
+            sig = 1.0 / (1.0 + jnp.exp(-gate))
+            act = gate * sig
+            mixed = (act * up).astype(BF16)
+            g_gate = (g_mixed * up * sig * (1.0 + gate * (1.0 - sig))).astype(BF16)
+            g_up = (g_mixed * act).astype(BF16)
+            parts[0, rows, :] = g_gate
+            parts[1, rows, :] = g_up
+            parts[2, rows, :] = mixed
+            acc_o[rows, :] += mm(mixed, wd, NT)
+            acc_n[rows, :] += mm(g_gate, wg, NT) + mm(g_up, wu, NT)
+            return carry
+
+        lax.fori_loop(0, tok // STRIP, rows_part, 0)
+        g_buf[slot, 0] = mm(n2_t[...], parts[0]).astype(BF16).reshape(grad_shape)
+        g_buf[slot, 1] = mm(n2_t[...], parts[1]).astype(BF16).reshape(grad_shape)
+        g_buf[slot, 2] = mm(cot_t[...], parts[2]).astype(BF16).reshape(grad_shape)
         save(chunk, slot)
-        acc_o[...] += mm(mixed, wd, NT)
-        acc_n[...] += mm(g_gate, wg, NT) + mm(g_up, wu, NT)
         return carry
 
     lax.fori_loop(0, chunks, step, 0)
     run(FFN_LATE)
-    total = jnp.zeros((1, dim), F32)
-    for i in range(tok // BLK):
-        rows = slice(i * BLK, (i + 1) * BLK)
+    def conclude(i, total):
+        rows = pl.ds(pl.multiple_of(i * BLK, BLK), BLK)
         hidden = hid[rows, :]
         n2[rows, :] = (hidden + acc_o[rows, :]).astype(BF16)
         scale = lax.rsqrt(jnp.mean(hidden * hidden, axis=1, keepdims=True) + EPSILON)
         e = acc_n[rows, :]
-        total = total + jnp.sum(e * hidden * scale, axis=0, keepdims=True)
         eg = e * gain
         inner = jnp.mean(eg * hidden, axis=1, keepdims=True)
         gh = cot_ref[rows, :].astype(F32) + scale * eg - hidden * (scale * scale * scale * inner)
         acc_o[rows, :] = gh
-        n2_t[rows, :] = gh.astype(BF16)
-        cot_t[rows, :] = mm(n2_t[rows, :], out_w_ref[...]).astype(BF16)
+        branch = gh.astype(BF16)
+        n2_t[rows, :] = branch
+        cot_t[rows, :] = mm(branch, out_w_ref[...]).astype(BF16)
+        return total + jnp.sum(e * hidden * scale, axis=0, keepdims=True)
+
+    total = lax.fori_loop(0, tok // BLK, conclude, jnp.zeros((1, dim), F32))
     ggain_ref[...] = jnp.broadcast_to(total, ggain_ref.shape)
     outs = [
         pltpu.make_async_copy(n2, output_ref, o_sem.at[0]),
@@ -1116,16 +1136,22 @@
         copy.start()
     save(chunks - 2, (chunks - 2) % 2, True)
     save(chunks - 1, (chunks - 1) % 2, True)
-    for i, first in enumerate(range(0, att_ref.shape[1], CHUNK)):
-        columns = slice(first, first + CHUNK)
-        piece = g_buf.at[i // 3, i % 3]
-        piece[...] = mm(n2_t[...], att_ref[:, columns], TN).astype(BF16).reshape(grad_shape)
-        outs.append(
-            pltpu.make_async_copy(
-                piece, gout_ref.at[:, :, :, :, :, pl.ds(first, CHUNK)], g_sem.at[i // 3, i % 3]
-            )
+    def out_copy(i):
+        lanes = pl.ds(pl.multiple_of(i * CHUNK, CHUNK), CHUNK)
+        slot, part = i // 3, lax.rem(i, 3)
+        return pltpu.make_async_copy(
+            g_buf.at[slot, part], gout_ref.at[:, :, :, :, :, lanes], g_sem.at[slot, part]
         )
-        outs[-1].start()
+
+    def out_piece(i, carry):
+        lanes = pl.ds(pl.multiple_of(i * CHUNK, CHUNK), CHUNK)
+        g_buf[i // 3, lax.rem(i, 3)] = mm(n2_t[...], att_ref[:, lanes], TN).astype(BF16).reshape(grad_shape)
+        out_copy(i).start()
+        return carry
+
+    n_out = att_ref.shape[1] // CHUNK
+    lax.fori_loop(0, n_out, out_piece, 0)
+    outs = outs + [out_copy(i) for i in range(n_out)]
     run(FFN_LAST)
     for copy in outs:
         copy.wait()
@@ -1164,6 +1190,7 @@
             pltpu.VMEM((dim, tok), BF16),
             pltpu.VMEM((tok, dim), F32),
             pltpu.VMEM((tok, dim), F32),
+            pltpu.VMEM((3, tok, CHUNK), BF16),
             pltpu.VMEM((2, 3, dim, CHUNK), BF16),
             pltpu.VMEM((2, 3, n_z, 2, 2, 2, rows, CHUNK), BF16),
             pltpu.SemaphoreType.DMA((sems,)),
@@ -1215,26 +1242,38 @@
     meet(others + groups)
     block = sources[0].shape[:-1] + (BLK,)
     half = gv_ref.shape[1] // 2
-    pieces = [
-        [(gv_ref, i) for i in range(0, half, BLK)],
-        [(gv_ref, i) for i in range(half, 2 * half, BLK)],
-        [(ref, i) for ref in (gq_ref, gk_ref) for i in range(0, lanes, BLK)],
-    ]
-    for k, piece in enumerate(pieces):
-        for j, (ref, i) in enumerate(piece):
-            sources[k][:, :, :, :, :, j * BLK : (j + 1) * BLK] = (
-                mm(normed_ref[...], ref[:, i : i + BLK], TN).astype(BF16).reshape(block)
-            )
-            if j == 0 and k > 0:
-                reduces[k - 1].stage(0)
+
+    def product(k, j, ref, i):
+        sources[k][:, :, :, :, :, pl.ds(j, BLK)] = (
+            mm(normed_ref[...], ref[:, pl.ds(i, BLK)]).astype(BF16).reshape(block)
+        )
+
+    def values_piece(n, carry):
+        first = pl.multiple_of(n * BLK, BLK)
+        product(0, first, gv_ref, first)
+        return carry
+
+    def more_values_piece(n, carry):
+        first = pl.multiple_of(n * BLK, BLK)
+        product(1, first, gv_ref, pl.multiple_of(half + first, BLK))
+        return carry
+
+    lax.fori_loop(0, half // BLK, values_piece, 0)
+    lax.fori_loop(0, half // BLK, more_values_piece, 0)
+    reduces[0].stage(0)
+    for j in range(0, lanes, BLK):
+        product(2, j, gq_ref, j)
+        if j == 0:
+            reduces[1].stage(0)
+        product(2, lanes + j, gk_ref, j)
     for copy in loads:
         copy.wait()
     todo = [[(2, 0), (0, 1)], [(1, 1)], [(0, 2), (2, 1)], [(1, 2)]]
-    total = jnp.zeros((1, dim), F32)
     gain = gain_ref[0:1]
-    saves = []
-    for i in range(tok // BLK):
-        rows = slice(i * BLK, (i + 1) * BLK)
+    n_block = tok // BLK
+
+    def norm_back(i, total):
+        rows = pl.ds(pl.multiple_of(i * BLK, BLK), BLK)
         e = (
             mm(gq_ref[rows, :], w_ref[:, 0:lanes], NT)
             + mm(gk_ref[rows, :], w_ref[:, lanes : 2 * lanes], NT)
@@ -1242,15 +1281,18 @@
         )
         u = x_ref[rows, :].astype(F32)
         scale = lax.rsqrt(jnp.mean(u * u, axis=1, keepdims=True) + EPSILON)
-        total = total + jnp.sum(e * u * scale, axis=0, keepdims=True)
         eg = e * gain
         inner = jnp.mean(eg * u, axis=1, keepdims=True)
         gh_ref[rows, :] = gh_ref[rows, :] + scale * eg - u * (scale * scale * scale * inner)
-        for k, n in todo[i] if i < len(todo) else ():
-            reduces[k].stage(n)
-    for i in range(tok // BLK, len(todo)):
-        for k, n in todo[i]:
-            reduces[k].stage(n)
+        for step, stages in enumerate(todo):
+            @pl.when(i == min(step, n_block - 1))
+            def _():
+                for k, n in stages:
+                    reduces[k].stage(n)
+
+        return total + jnp.sum(e * u * scale, axis=0, keepdims=True)
+
+    total = lax.fori_loop(0, n_block, norm_back, jnp.zeros((1, dim), F32))
     save = pltpu.make_async_copy(gh_ref, gin_ref, local_sem.at[0])
     save.start()
     row = lax.broadcasted_iota(jnp.int32, own_gains.shape, 0)

time: 374 us -> 353 us (0.944); the launches traced: 367 us -> 353 us
  Pallas kernels: 360 us -> 346 us
    pallas_call x1, Pallas kernels: 113 us -> 99.2 us  [ffn(): pl.pallas_call(functools.partial(ffn_kernel, n_sp, gather_units, chunks),...]
where the time goes in v5:
time: 353 us
  Pallas kernels  346 us (98%)
  local copies, waits for them, and re-layouts  6.45 us (2%)
    pallas_call x1, Pallas kernels, backward(): pl.pallas_call(functools.partial(backward_kernel, n_sp, widths), out_shap...  109 us
    pallas_call x1, Pallas kernels, ffn(): pl.pallas_call(functools.partial(ffn_kernel, n_sp, gather_units, chunks),...  99.2 us
    pallas_call x1, Pallas kernels, forward(): pl.pallas_call(functools.partial(forward_kernel, n_sp), out_shape=(shape(...  90 us
    pallas_call x1, Pallas kernels, tail(): pl.pallas_call(functools.partial(tail_kernel, n_sp), out_shape=(shape((8,...  42.6 us

profile of v5, /device:TPU:0, one launch (start us, length us, event | category | flops | bytes accessed | tf_op | source)
XLA Modules:
  0.0 353.0 jit_solution(8233728998698709569)
XLA Ops:
  0.6 90.0 %forward.1 = (bf16[1024,1024]{1,0:T(8,128)(2,1)}, bf16[1024,1024]{1,0:T(8,128)(2,1)}, bf16[16,80,256]{2,1,0:T(8,128)(2,1)}, f32[8,1024]{1,0:T(8,128)}, bf16[1024...) custom-call(bf16[1024,1024]{1,0:T(8,128)(2,1)} %x_hbm.1, ...), custom_call_target="tpu_custom_call" | custom-call | tf_op jit(solution)/shard_map/forward/pallas_call | solution.py:689
  90.7 99.2 %ffn.1 = (f32[8,1024]{1,0:T(8,128)}, bf16[2,2,32,1536]{3,2,1,0:T(8,128)(2,1)}, bf16[2,2,32,1536]{3,2,1,0:T(8,128)(2,1)}, bf16[1024,1024]{1,0:T(8,128)(2,1)}, f32...) custom-call(bf16[1024,1024]{1,0:T(8,128)(2,1)} %x_hbm.1, ...), custom_call_target="tpu_custom_call" | custom-call | tf_op jit(solution)/shard_map/ffn/pallas_call | solution.py:1174
  189.9 109.2 %backward.1 = (bf16[1024,256]{1,0:T(8,128)(2,1)}, bf16[1024,256]{1,0:T(8,128)(2,1)}, bf16[1024,1024]{1,0:T(8,128)(2,1)}, bf16[2,2,32,1024]{3,2,1,0:T(8,128)(2,1)...) custom-call(bf16[1024,256]{1,0:T(8,128)(2,1)} %get-tuple-element.63., ...), custom_call_target="tpu_custom_call" | custom-call | tf_op jit(solution)/shard_map/backward/pallas_call | solution.py:924
  299.1 42.6 %tail.1 = (f32[8,1024]{1,0:T(8,128)}, bf16[2,2,32,512]{3,2,1,0:T(8,128)(2,1)}, bf16[2,2,32,512]{3,2,1,0:T(8,128)(2,1)}, bf16[2,2,32,512]{3,2,1,0:T(8,128)(2,1)}, f32[1024,1024]{1,0:T(8,128)}) custom-call(bf16[1024,1024]{1,0:T(8,128)(2,1)} %get-tuple-element.62.normed_ref, bf16[1024,256]{1,0:T(8,128)(2,1)} %get-tuple-element.73.gq_ref, ...), custom_call_target="tpu_custom_call" | custom-call | tf_op jit(solution)/shard_map/tail/pallas_call | solution.py:1328
  341.8 4.8 %finish.1 = (f32[128,256]{1,0:T(8,128)}, f32[128,256]{1,0:T(8,128)}, f32[128,1024]{1,0:T(8,128)}, f32[1024,128]{1,0:T(8,128)}, f32[2752,128]{1,0:T(8,128)}, /*index=5*/f32[2752,128]{1,0:T(8,128)}, f32[2752,128]{1,0:T(8,128)}) custom-call(bf16[128,512]{1,0:T(8,128)(2,1)} %bitcast.29, bf16[128,512]{1,0:T(8,128)(2,1)} %bitcast.27, bf16[128,512]{1,0:T(8,128)(2,1)} %bitcast.28, ...), custom_call_target="tpu_custom_call" | custom-call | tf_op jit(solution)/shard_map/finish/pallas_call | solution.py:1387
  346.6 0.7 constant_dynamic-slice_fusion
  347.3 0.5 slice_bitcast_fusion
  347.8 0.0 copy-start
  347.8 3.2 copy.26
  351.0 0.0 copy-done
  351.0 2.0 copy.27
Async XLA Ops:
  347.8 3.2 copy-start

commit v6 on v5

--- a/solution.py
+++ b/solution.py
@@ -1354,16 +1354,30 @@
     )(normed, gq, gk, gv, gain, ggain, w_joint, x, g_hidden)
 
 
+PASS_PARTS = 4
+
+
 def finish_kernel(sums, *refs):
     n = len(sums) + 4
-    sources, refs = refs[:n], refs[n:]
+    sources, whole, refs = refs[:n], refs[n : n + 2], refs[n + 2 :]
     (q_out, k_out, v_out, out_out, gate_out, up_out, down_out), refs = refs[:7], refs[7:]
-    held, sem = refs[:n], refs[n]
+    whole_out, refs = refs[:2], refs[2:]
+    held, passing, (sem, in_sem, out_sem) = refs[:n], refs[n : n + 2], refs[n + 2 :]
+    reads, writes = [], []
+    for a, (src, mid, dst) in enumerate(zip(whole, passing, whole_out)):
+        count = src.shape[0] // PASS_PARTS
+        for i in range(PASS_PARTS):
+            rows = pl.ds(i * count, count)
+            reads.append(pltpu.make_async_copy(src.at[rows], mid.at[rows], in_sem.at[a, i]))
+            writes.append(pltpu.make_async_copy(mid.at[rows], dst.at[rows], out_sem.at[a, i]))
     copies = [pltpu.make_async_copy(src, dst, sem.at[i]) for i, (src, dst) in enumerate(zip(sources, held))]
-    for copy in copies:
+    for copy in copies + reads:
         copy.start()
     for copy in copies:
         copy.wait()
+    for read, write in zip(reads, writes):
+        read.wait()
+        write.start()
     qk_ref, va_ref, vb_ref, out_ref, units = held[0], held[1], held[2], held[3], held[4:]
     lanes = q_out.shape[1]
     width = gate_out.shape[0]
@@ -1377,9 +1391,11 @@
         span = (last - first) * CHUNK
         for i, out in enumerate((gate_out, up_out, down_out)):
             out[lo:hi, :] = unit[:, i * span : i * span + hi - lo].astype(F32).T
-
-
-def finish(width, lanes, qk, va, vb, out, units):
+    for write in writes:
+        write.wait()
+
+
+def finish(width, lanes, qk, va, vb, out, units, whole):
     shard = va.shape[0]
     vmem, anywhere = pl.BlockSpec(memory_space=pltpu.VMEM), pl.BlockSpec(memory_space=pl.ANY)
     shape = jax.ShapeDtypeStruct
@@ -1389,14 +1405,19 @@
         out_shape=(
             shape((shard, lanes), F32), shape((shard, lanes), F32), shape((shard, 2 * va.shape[1]), F32),
             shape(out.shape[::-1], F32), shape((width, shard), F32), shape((width, shard), F32),
-            shape((width, shard), F32),
+            shape((width, shard), F32), *[shape(w.shape, w.dtype) for w in whole],
         ),
-        in_specs=[anywhere] * len(arrays),
-        out_specs=(vmem,) * 7,
-        scratch_shapes=[pltpu.VMEM(a.shape, BF16) for a in arrays] + [pltpu.SemaphoreType.DMA((len(arrays),))],
+        in_specs=[anywhere] * (len(arrays) + len(whole)),
+        out_specs=(vmem,) * 7 + (anywhere,) * len(whole),
+        scratch_shapes=[pltpu.VMEM(a.shape, a.dtype) for a in (*arrays, *whole)]
+        + [
+            pltpu.SemaphoreType.DMA((len(arrays),)),
+            pltpu.SemaphoreType.DMA((len(whole), PASS_PARTS)),
+            pltpu.SemaphoreType.DMA((len(whole), PASS_PARTS)),
+        ],
         compiler_params=pltpu.CompilerParams(vmem_limit_bytes=63 << 20),
         name="finish",
-    )(*arrays)
+    )(*arrays, *whole)
 
 
 def body(
@@ -1436,9 +1457,10 @@
         return shard
 
     s_va, s_vb, s_query_key = shards_of(joint)
-    g_query, g_key, g_value, g_w_out, g_gate, g_up, g_down = finish(
+    g_query, g_key, g_value, g_w_out, g_gate, g_up, g_down, grad_input, output = finish(
         hidden_units, lanes, over_groups(s_query_key), over_groups(s_va), over_groups(s_vb), over_groups(s_out),
         [over_groups(shard) for shard in (*shards, *more)],
+        (grad_input, output),
     )
     s_gains = over_groups(lax.dynamic_slice(grad_gains, (0, me * width), (2, width)))
     return (

time: 353 us -> 352 us (level)
  local copies, waits for them, and re-layouts: 6.45 us -> 1.2 us
  Pallas kernels: 346 us -> 350 us
    unnamed x4 -> x0, local copies, waits for them, and re-layouts: 5.25 us -> none
    pallas_call x1, Pallas kernels: 4.78 us -> 8.75 us  [finish(): pl.pallas_call(functools.partial(finish_kernel, reduce_units(-(-width //...]
where the time goes in v6:
time: 352 us
  Pallas kernels  350 us (99%)
    pallas_call x1, Pallas kernels, backward(): pl.pallas_call(functools.partial(backward_kernel, n_sp, widths), out_shap...  109 us
    pallas_call x1, Pallas kernels, ffn(): pl.pallas_call(functools.partial(ffn_kernel, n_sp, gather_units, chunks),...  99.2 us
    pallas_call x1, Pallas kernels, forward(): pl.pallas_call(functools.partial(forward_kernel, n_sp), out_shape=(shape(...  90 us
    pallas_call x1, Pallas kernels, tail(): pl.pallas_call(functools.partial(tail_kernel, n_sp), out_shape=(shape((8,...  42.6 us
    pallas_call x1, Pallas kernels, finish(): pl.pallas_call(functools.partial(finish_kernel, reduce_units(-(-width //...  8.75 us

profile of v6, /device:TPU:0, one launch (start us, length us, event | category | flops | bytes accessed | tf_op | source)
XLA Modules:
  0.0 351.7 jit_solution(10118475669247246094)
XLA Ops:
  0.6 90.0 %forward.1 = (bf16[1024,1024]{1,0:T(8,128)(2,1)}, bf16[1024,1024]{1,0:T(8,128)(2,1)}, bf16[16,80,256]{2,1,0:T(8,128)(2,1)}, f32[8,1024]{1,0:T(8,128)}, bf16[1024...) custom-call(bf16[1024,1024]{1,0:T(8,128)(2,1)} %x_hbm.1, ...), custom_call_target="tpu_custom_call" | custom-call | tf_op jit(solution)/shard_map/forward/pallas_call | solution.py:689
  90.7 99.2 %ffn.1 = (f32[8,1024]{1,0:T(8,128)}, bf16[2,2,32,1536]{3,2,1,0:T(8,128)(2,1)}, bf16[2,2,32,1536]{3,2,1,0:T(8,128)(2,1)}, bf16[1024,1024]{1,0:T(8,128)(2,1)}, f32...) custom-call(bf16[1024,1024]{1,0:T(8,128)(2,1)} %x_hbm.1, ...), custom_call_target="tpu_custom_call" | custom-call | tf_op jit(solution)/shard_map/ffn/pallas_call | solution.py:1174
  189.9 109.2 %backward.1 = (bf16[1024,256]{1,0:T(8,128)(2,1)}, bf16[1024,256]{1,0:T(8,128)(2,1)}, bf16[1024,1024]{1,0:T(8,128)(2,1)}, bf16[2,2,32,1024]{3,2,1,0:T(8,128)(2,1)...) custom-call(bf16[1024,256]{1,0:T(8,128)(2,1)} %get-tuple-element.57., ...), custom_call_target="tpu_custom_call" | custom-call | tf_op jit(solution)/shard_map/backward/pallas_call | solution.py:924
  299.1 42.6 %tail.1 = (f32[8,1024]{1,0:T(8,128)}, bf16[2,2,32,512]{3,2,1,0:T(8,128)(2,1)}, bf16[2,2,32,512]{3,2,1,0:T(8,128)(2,1)}, bf16[2,2,32,512]{3,2,1,0:T(8,128)(2,1)}, f32[1024,1024]{1,0:T(8,128)}) custom-call(bf16[1024,1024]{1,0:T(8,128)(2,1)} %get-tuple-element.56.normed_ref, bf16[1024,256]{1,0:T(8,128)(2,1)} %get-tuple-element.74.gq_ref, ...), custom_call_target="tpu_custom_call" | custom-call | tf_op jit(solution)/shard_map/tail/pallas_call | solution.py:1328
  341.8 8.7 %finish.1 = (f32[128,256]{1,0:T(8,128)}, f32[128,256]{1,0:T(8,128)}, f32[128,1024]{1,0:T(8,128)}, f32[1024,128]{1,0:T(8,128)}, f32[2752,128]{1,0:T(8,128)}, /*in...) custom-call(bf16[128,512]{1,0:T(8,128)(2,1)} %bitcast.29, ...), custom_call_target="tpu_custom_call" | custom-call | tf_op jit(solution)/shard_map/finish/pallas_call | solution.py:1403
  350.5 0.7 constant_dynamic-slice_fusion
  351.2 0.5 slice_bitcast_fusion
